TPU v7x, 32 devices: a whole 2x2x4 slice. The times are simulated.
32 devices in a mesh: sweep: 4 (over y, core), sector: 8 (over z, x).
Axes of the slice: x: 2, y: 2, z: 4, core: 2. Of those that a mesh axis runs over, the one named last changes fastest.
Arguments:
- range_image: bfloat16 [4, 64, 2048, 128], P('sweep', None, 'sector'), may hold values from -6 to 6
- send_pixel: int32 [4, 8, 8, 256], P('sweep', 'sector'), may hold values from 0 to 16383, as said below
- send_cell: int32 [4, 8, 8, 256], P('sweep', 'sector'), may hold values from 0 to 255
- send_tile: int32 [4, 8, 8, 2], P('sweep', 'sector'), may hold values from 0 to 31
- send_count: int32 [4, 8, 8], P('sweep', 'sector'), may hold values from 64 to 256, as said below
- w_range: bfloat16 [3, 3, 128, 128], replicated, may hold values from -0.1875 to 0.1875
- w_proj: bfloat16 [128, 64], replicated, may hold values from -0.5 to 0.5
- w_head: bfloat16 [3, 3, 64, 64], replicated, may hold values from -0.25 to 0.25
- cotangent: bfloat16 [64, 128, 512], P(None, 'sector', 'sweep'), may hold values from -0.046875 to 0.046875
Outputs:
- head_out: bfloat16 [64, 128, 512], P(None, 'sector', 'sweep')
- grad_w_range: float32 [3, 3, 128, 128], replicated
- grad_w_proj: float32 [128, 64], replicated
- grad_w_head: float32 [3, 3, 64, 64], replicated
Inputs may be any that keep to these rules, and one draw needn't show every extreme that they name: `send_pixel`: A pixel number beam * 256 + col of the sending device; the slots of one device's lists name distinct pixels. Slots q < send_count are live, the rest are padding with arbitrary pixel, cell and tile numbers; in every sweep some row band receives 256 live slots from every sector. `send_cell`: cell of a tile, numbered r * 16 + c. `send_tile`: tile of the destination's row band, numbered along the grid's columns.
All inputs are finite; a program needn't handle non-finite values.
Results may differ from a plain program's by a relative error of at most 0.0057.
Values may be sent and summed in bfloat16 or wider, within the bound.
No kernel may reach another device: no remote copies, remote signals or barrier semaphores. Data moves between devices by JAX's collectives and lax.ppermute only.
A program may use at most 192 MiB of HBM per device.

v0:
```python
import jax
import jax.numpy as jnp
from jax import lax
from jax.sharding import PartitionSpec as P

TILE = 16
TILES_DEV = 8


def extended(cells, sides, width, closed):
    for axis, dim in sides:
        count = lax.axis_size(axis)
        ends = count if closed else count - 1
        head = lax.slice_in_dim(cells, 0, width, axis=dim)
        tail = lax.slice_in_dim(cells, cells.shape[dim] - width, cells.shape[dim], axis=dim)
        cells = jnp.concatenate(
            [
                lax.ppermute(tail, axis, [(i, (i + 1) % count) for i in range(ends)]),
                cells,
                lax.ppermute(head, axis, [((i + 1) % count, i) for i in range(ends)]),
            ],
            axis=dim,
        )
    return cells


def silu_slope(preact):
    sigmoid = jax.nn.sigmoid(preact)
    return sigmoid * (1.0 + preact * (1.0 - sigmoid))


def shards(
    range_image, send_pixel, send_cell, send_tile, send_count, w_range, w_proj, w_head, cotangent
):
    beam_count = range_image.shape[1]
    columns = range_image.shape[2]
    channels = range_image.shape[3]
    wrapped_image = extended(range_image, (("sector", 2),), 1, True)[0]
    padded = jnp.pad(wrapped_image, ((1, 1), (0, 0), (0, 0)))

    def shifted(row_off, col_off):
        return padded[row_off : row_off + beam_count, col_off : col_off + columns].reshape(
            -1, channels
        )

    preact = jnp.zeros((beam_count * columns, channels), jnp.float32)
    for row_off in range(3):
        for col_off in range(3):
            preact = preact + jnp.dot(
                shifted(row_off, col_off),
                w_range[row_off, col_off],
                preferred_element_type=jnp.float32,
            )
    hidden = (
        range_image[0].reshape(-1, channels).astype(jnp.float32) + jax.nn.silu(preact)
    ).astype(jnp.bfloat16)
    pixels = send_pixel[0, 0]
    slot_count = pixels.shape[1]
    live_slot = jnp.arange(slot_count, dtype=jnp.int32)[None, :] < send_count[0, 0][:, None]
    outgoing = jnp.where(live_slot[:, :, None], hidden[pixels], jnp.zeros((), jnp.bfloat16))
    rows_in, cells_in, tiles_in = (
        lax.all_to_all(outgoing, "sector", split_axis=0, concat_axis=0, tiled=True),
        lax.all_to_all(send_cell[0, 0], "sector", split_axis=0, concat_axis=0, tiled=True),
        lax.all_to_all(send_tile[0, 0], "sector", split_axis=0, concat_axis=0, tiled=True),
    )
    sectors = rows_in.shape[0]
    block_count = tiles_in.shape[1]
    slot_len = slot_count // block_count
    blocks = sectors * block_count
    cell_count = TILE * TILE
    band_count = TILES_DEV * lax.axis_size("sweep")
    block_rows = rows_in.reshape(blocks, slot_len, channels)
    block_cells = cells_in.reshape(blocks, slot_len)
    block_tiles = tiles_in.reshape(blocks)
    placing = (
        block_cells[:, :, None] == jnp.arange(cell_count, dtype=jnp.int32)[None, None, :]
    ).astype(jnp.bfloat16)
    contrib = jnp.einsum("nqk,nqc->nkc", placing, block_rows, preferred_element_type=jnp.float32)
    band_sums = (
        jnp.zeros((band_count, cell_count, channels), jnp.float32).at[block_tiles].add(contrib)
    )
    weights32 = w_proj.astype(jnp.float32)
    local_proj = jnp.einsum("tkc,cb->tbk", band_sums, weights32, precision=lax.Precision.HIGHEST)
    projected = lax.psum_scatter(local_proj, "sweep", scatter_dimension=0, tiled=True)
    owned_tiles = projected.shape[0]
    head_ch = projected.shape[1]
    grid_rows = TILE
    grid_cols = owned_tiles * TILE
    ground = (
        projected.astype(jnp.bfloat16)
        .reshape(owned_tiles, head_ch, TILE, TILE)
        .transpose(1, 2, 0, 3)
        .reshape(head_ch, grid_rows, grid_cols)
    )
    ground_pad, grad_padded = (
        extended(ground, (("sweep", 2), ("sector", 1)), 1, False),
        extended(cotangent, (("sweep", 2), ("sector", 1)), 1, False),
    )
    flat_cot = cotangent.reshape(head_ch, -1)
    head_sum = jnp.zeros((head_ch, grid_rows * grid_cols), jnp.float32)
    ground_grad = jnp.zeros((head_ch, grid_rows * grid_cols), jnp.float32)
    head_grads = []
    for row_off in range(3):
        for col_off in range(3):
            window = ground_pad[
                :, row_off : row_off + grid_rows, col_off : col_off + grid_cols
            ].reshape(head_ch, -1)
            head_sum = head_sum + jnp.dot(
                w_head[row_off, col_off].T, window, preferred_element_type=jnp.float32
            )
            head_grads.append(
                lax.dot_general(
                    window, flat_cot, (((1,), (1,)), ((), ())), preferred_element_type=jnp.float32
                )
            )
            behind = grad_padded[
                :, 2 - row_off : 2 - row_off + grid_rows, 2 - col_off : 2 - col_off + grid_cols
            ].reshape(head_ch, -1)
            ground_grad = ground_grad + jnp.dot(
                w_head[row_off, col_off], behind, preferred_element_type=jnp.float32
            )
    head_out = head_sum.astype(jnp.bfloat16).reshape(head_ch, grid_rows, grid_cols)
    head_local = jnp.stack(head_grads).reshape(3, 3, head_ch, head_ch)
    tile_grad = (
        ground_grad.astype(jnp.bfloat16)
        .reshape(head_ch, TILE, owned_tiles, TILE)
        .transpose(2, 0, 1, 3)
        .reshape(owned_tiles, head_ch, cell_count)
    )
    band_grads = lax.all_gather(tile_grad, "sweep", axis=0, tiled=True)
    target_grads = band_grads[block_tiles]
    slot_grads = jnp.einsum(
        "nbk,nqk->nbq", target_grads, placing, preferred_element_type=jnp.float32
    ).astype(jnp.bfloat16)
    proj_local = jnp.einsum(
        "nqc,nbq->cb", block_rows, slot_grads, preferred_element_type=jnp.float32
    )
    row_grads = jnp.einsum(
        "nbq,cb->nqc", slot_grads, w_proj, preferred_element_type=jnp.float32
    ).reshape(sectors, slot_count, channels)
    pixel_grads = lax.all_to_all(row_grads, "sector", split_axis=0, concat_axis=0, tiled=True)
    pixel_total = hidden.shape[0]
    target = jnp.where(live_slot, pixels, pixel_total)
    masked = jnp.where(live_slot[:, :, None], pixel_grads, 0.0)
    hidden_grad = (
        jnp.zeros((pixel_total + 1, channels), jnp.float32)
        .at[target.reshape(-1)]
        .add(masked.reshape(-1, channels))[:pixel_total]
    )
    preact_grad = (hidden_grad * silu_slope(preact)).astype(jnp.bfloat16)
    range_terms = []
    for row_off in range(3):
        for col_off in range(3):
            range_terms.append(
                lax.dot_general(
                    shifted(row_off, col_off),
                    preact_grad,
                    (((0,), (0,)), ((), ())),
                    preferred_element_type=jnp.float32,
                )
            )
    range_local = jnp.stack(range_terms).reshape(3, 3, channels, channels)
    grad_range, grad_proj, grad_head = lax.psum(
        (range_local, proj_local, head_local), ("sweep", "sector")
    )
    return (head_out, grad_range, grad_proj, grad_head)


def solution(mesh):
    return jax.shard_map(
        shards,
        mesh=mesh,
        in_specs=(
            P("sweep", None, "sector", None),
            P("sweep", "sector", None, None),
            P("sweep", "sector", None, None),
            P("sweep", "sector", None, None),
            P("sweep", "sector", None),
            P(),
            P(),
            P(),
            P(None, "sector", "sweep"),
        ),
        out_specs=(P(None, "sector", "sweep"), P(), P(), P()),
        check_vma=False,
    )
```

profile of v0, /device:TPU:0, one launch (start us, length us, event | category | flops | bytes accessed | tf_op | source)
XLA Modules:
  0.0 434.0 jit_solution(12573225347712565895)
XLA Ops:
  13.4 6.6 %all-to-all-start = ((s32[8,1,2]{2,1,0:T(1,128)}), s32[8,1,2]{2,1,0:T(1,128)S(1)}, u32[]{:S(2)}, u32[]{:S(2)}) async-start(s32[8,1,2]{2,1,0:T(1,128)} %copy.51), calls=%async_computation | async-start | bytes 8192 | tf_op jit(solution)/shard_map/all_to_all | solution.py:64
  36.8 4.5 %collective-permute-start.9 = (bf16[64,1,130]{2,1,0:T(2,128)(2,1)S(1)}, bf16[64,1,130]{2,1,0:T(2,128)(2,1)S(1)}, u32[]{:S(2)}, u32[]{:S(2)}) collective-permute-start(bf16[64,1,130]{2,1,0:T(2,128)(2,1)S(1)} %get-tuple-element.25), channel_id=1, source_target_pairs={{0,1},{1,2},{2,3},{3,4},{4,5},{5,6},{6,7},{8,9},{9,10},{10,11},{11... | collective-permute-start | bytes 49928 | tf_op jit(solution)/shard_map/ppermute | solution.py:18
  47.4 13.3 %pad_slice_fusion = (bf16[64,256,128]{2,1,0:T(8,128)(2,1)}, bf16[64,256,128]{2,1,0:T(8,128)(2,1)S(1)}, bf16[64,256,128]{2,1,0:T(8,128)(2,1)}, bf16[64,256,128]{2...) fusion(bf16[64,258,128]{2,1,0:T(8,128)(2,1)S(1)} %maximum_bitca, ...), kind=kLoop, calls=%fused_computation.43 | loop fusion | bytes 54657024 | tf_op jit(solution)/shard_map/slice | solution.py:42
  64.0 4.6 %convolution_add_fusion.7 = f32[16384,128]{1,0:T(8,128)} fusion(f32[16384,128]{1,0:T(8,128)S(1)} %fusion.97, bf16[16384,128]{1,0:T(8,128)(2,1)S(1)} %bitcast.354, bf16[3,3,128,128]{3,2,1,0:T(8,128)(2,1)S(1)} %copy-done.20), kind=kOutput, calls=%fused_computation.11 | convolution fusion | flops 538968064 | bytes 21004288 | tf_op jit(solution)/shard_map/dot_general | solution.py:49
  73.1 6.0 %convolution_add_fusion.6 = f32[16384,128]{1,0:T(8,128)S(1)} fusion(f32[16384,128]{1,0:T(8,128)} %convolution_add_fusion.7, bf16[16384,128]{1,0:T(8,128)(2,1)} %bitcast.352, bf16[3,3,128,128]{3,2,1,0:T(8,128)(2,1)S(1)} %copy-done.20), kind=kOutput, calls=%fused_computation.10 | convolution fusion | flops 538968064 | bytes 21004288 | tf_op jit(solution)/shard_map/dot_general | solution.py:49
  81.3 4.5 %convolution_add_fusion.4 = f32[16384,128]{1,0:T(8,128)} fusion(f32[16384,128]{1,0:T(8,128)S(1)} %convolution_add_fusion.5, bf16[16384,128]{1,0:T(8,128)(2,1)S(1)} %bitcast.348, bf16[3,3,128,128]{3,2,1,0:T(8,128)(2,1)S(1)} %copy-done.20), kind=kOutput, calls=%fused_computation.8 | convolution fusion | flops 538968064 | bytes 21004288 | tf_op jit(solution)/shard_map/dot_general | solution.py:49
  85.8 7.9 %all-gather.2.cloned.1.call-done = bf16[32,64,256]{2,1,0:T(8,128)(2,1)} async-done(((bf16[8,64,256]{2,1,0:T(8,128)(2,1)}), bf16[32,64,256]{2,1,0:T(8,128)(2,1)}) %all-gather.2.cloned.1.call-update) | async-done | bytes 1048592 | tf_op jit(solution)/shard_map/all_gather | solution.py:130
  97.5 5.9 %all-to-all-start.3 = ((f32[8,256,128]{2,1,0:T(8,128)}), f32[8,256,128]{2,1,0:T(8,128)S(1)}, u32[]{:S(2)}, u32[]{:S(2)}) async-start(f32[8,256,128]{2,1,0:T(8,128)} %bitcast.53), calls=%async_computation.4 | async-start | bytes 2097152 | tf_op jit(solution)/shard_map/all_to_all | solution.py:141
  103.5 6.0 %convolution_add_fusion.3 = f32[16384,128]{1,0:T(8,128)S(1)} fusion(f32[16384,128]{1,0:T(8,128)} %convolution_add_fusion.4, bf16[16384,128]{1,0:T(8,128)(2,1)} %bitcast.346, bf16[3,3,128,128]{3,2,1,0:T(8,128)(2,1)S(1)} %copy-done.20), kind=kOutput, calls=%fused_computation.7 | convolution fusion | flops 538968064 | bytes 21004288 | tf_op jit(solution)/shard_map/dot_general | solution.py:49
  111.7 4.5 %convolution_add_fusion.1 = f32[16384,128]{1,0:T(8,128)} fusion(f32[16384,128]{1,0:T(8,128)S(1)} %convolution_add_fusion.2, bf16[16384,128]{1,0:T(8,128)(2,1)S(1)} %bitcast.342, bf16[3,3,128,128]{3,2,1,0:T(8,128)(2,1)S(1)} %copy-done.20), kind=kOutput, calls=%fused_computation.5 | convolution fusion | flops 538968064 | bytes 21004288 | tf_op jit(solution)/shard_map/dot_general | solution.py:49
  116.2 13.4 %all-to-all-done.3 = f32[8,256,128]{2,1,0:T(8,128)S(1)} async-done(((f32[8,256,128]{2,1,0:T(8,128)}), f32[8,256,128]{2,1,0:T(8,128)S(1)}, u32[]{:S(2)}, u32[]{:S(2)}) %all-to-all-start.3) | async-done | bytes 1048608 | tf_op jit(solution)/shard_map/all_to_all | solution.py:141
  129.9 15.8 %scatter_custom_fusion.1 = f32[16385,128]{1,0:T(8,128)} fusion(s32[2048]{0:T(1024)S(1)} %bitcast.388, f32[2048,128]{1,0:T(8,128)S(1)} %bitcast.376, f32[]{:T(128)} %constant.7.clone.1), kind=kCustom, calls=%fused_computation.18 | custom fusion | flops 262144 | bytes 8389124 | tf_op jit(solution)/shard_map/scatter-add | solution.py:148
  145.6 12.9 %fusion = (bf16[16384,128]{1,0:T(8,128)(2,1)}, bf16[16384,128]{1,0:T(8,128)(2,1)}) fusion(f32[16385,128]{1,0:T(8,128)} %scatter_custom_fusion.1, bf16[1,64,256,128]{3,2,1,0:T(8,128)(2,1)} %param.9, f32[16384,128]{1,0:T(8,128)} %convolution_add_fusion.1, bf16[16384,128]{1,0:T(8,128)(2,1)} %bitcast.358, bf16[3,3,128,128]{3,2,1,0:T(8,128)(2,1)S(1)} %copy-done.20), kind=kOutput, calls=%fused_computation.13 | convolution fusion | flops 566231040 | bytes 33587200 | tf_op jit(solution)/shard_map/dot_general | solution.py:49
  158.5 8.3 %gather_fusion = bf16[2048,128]{1,0:T(8,128)(2,1)S(1)} fusion(bf16[16384,128]{1,0:T(8,128)(2,1)} %get-tuple-element.7, s32[2048]{0:T(1024)S(1)} %broadcast_clamp_fusion), kind=kCustom, calls=%fused_computation | custom fusion | bytes 1056768 | tf_op jit(solution)/shard_map/gather | solution.py:60
  172.0 5.4 %fusion.23 = f32[9,128,128]{2,1,0:T(8,128)} fusion(bf16[16384,128]{1,0:T(8,128)(2,1)} %bitcast.357, bf16[16384,128]{1,0:T(8,128)(2,1)} %get-tuple-element.6), kind=kOutput, calls=%fused_computation.72 | convolution fusion | flops 536870912 | bytes 8454144 | tf_op jit(solution)/shard_map/dot_general | solution.py:155
  177.4 9.3 %all-to-all-done.2 = bf16[8,256,128]{2,1,0:T(8,128)(2,1)S(1)} async-done(((bf16[8,256,128]{2,1,0:T(8,128)(2,1)}), bf16[8,256,128]{2,1,0:T(8,128)(2,1)S(1)}, u32[]{:S(2)}, u32[]{:S(2)}) %all-to-all-start.2) | async-done | bytes 524320 | tf_op jit(solution)/shard_map/all_to_all | solution.py:62
  190.7 4.5 %scatter_fusion = f32[32,256,128]{2,1,0:T(8,128)} fusion(f32[32,256,128]{2,1,0:T(8,128)} %broadcast_in_dim.38, s32[16]{0:T(128)S(1)} %fusion.148, f32[16,256,128]{2,1,0:T(8,128)S(1)} %fusion.12), kind=kCustom, calls=%fused_computation.2 | custom fusion | flops 524288 | bytes 6291520 | tf_op jit(solution)/shard_map/scatter-add | solution.py:80
  195.2 6.2 %convolution_bitcast_fusion.4 = f32[32,64,256]{2,1,0:T(8,128)} fusion(f32[32,256,128]{2,1,0:T(8,128)} %scatter_fusion, bf16[128,64]{0,1:T(8,128)(2,1)S(1)} %copy-done), kind=kOutput, calls=%fused_computation.52 | convolution fusion | flops 805306368 | bytes 6307840 | tf_op jit(solution)/shard_map/tkc,cb->tbk/dot_general | solution.py:83
  201.4 4.9 %fusion.22 = f32[9,128,128]{2,1,0:T(8,128)S(1)} fusion(f32[9,128,128]{2,1,0:T(8,128)S(1)} %copy-done.16, bf16[16384,128]{1,0:T(8,128)(2,1)} %bitcast.355, bf16[16384,128]{1,0:T(8,128)(2,1)} %get-tuple-element.6), kind=kOutput, calls=%fused_computation.70 | convolution fusion | flops 536870912 | bytes 8454144 | tf_op jit(solution)/shard_map/dot_general | solution.py:155
  223.8 7.1 %reduce-scatter.2.cloned.1.call-done = f32[8,64,256]{2,1,0:T(8,128)} async-done(((f32[32,64,256]{2,1,0:T(8,128)}), f32[8,64,256]{2,1,0:T(8,128)}) %reduce-scatter.2.cloned.1.call-update) | async-done | bytes 524304 | tf_op jit(solution)/shard_map/reduce_scatter | solution.py:84
  235.6 42.8 %psum.22 = f32[128,64]{0,1:T(8,128)} all-reduce(f32[128,64]{0,1:T(8,128)S(1)} %convolution_bitcast_fusion.14), channel_id=1, replica_groups=mesh['sweep'=4,'sector'=8] {'sweep','sector'}, use_global_device_ids=true, to_apply=%region_4.5 | all-reduce | flops 8192 | bytes 65536 | tf_op jit(solution)/shard_map/psum | solution.py:163
  278.5 4.2 collective-permute-start.4
  284.4 4.2 collective-permute-done.5
  295.4 128.2 %all-reduce.4.cloned.1.call-done = (f32[3,3,128,128]{3,2,1,0:T(8,128)}, f32[3,3,64,64]{3,2,1,0:T(8,128)}) async-done(((f32[3,3,128,128]{3,2,1,0:T(8,128)}, f32[3,3,64,64]{3,2,1,0:T(8,128)}), (f32[3,3,128,128]{3,2,1,0:T(8,128)}, f32[3,3,64,64]{3,2,1,0:T(8,128)})) %all-reduce.4.cloned.1.call-update) | async-done | bytes 737296 | tf_op jit(solution)/shard_map/psum | solution.py:163
  (151 shorter events, 88.3 us)
Async XLA Ops:
  7.2 89.0 %copy-start = (bf16[128,64]{0,1:T(8,128)(2,1)S(1)}, bf16[128,64]{0,1:T(8,128)(2,1)}, u32[]{:S(2)}) copy-start(bf16[128,64]{0,1:T(8,128)(2,1)} %param.15) | copy-start | bytes 49156
  8.4 25.7 %collective-permute-start.6 = (bf16[64,16,1]{2,1,0:T(8,128)(2,1)S(1)}, bf16[64,16,1]{2,1,0:T(8,128)(2,1)S(1)}, u32[]{:S(2)}, u32[]{:S(2)}) collective-permute-start(bf16[64,16,1]{2,1,0:T(8,128)(2,1)S(1)} %get-tuple-element.41), channel_id=1, source_target_pairs={{0,8},{8,16},{16,24},{1,9},{9,17},{17,25},{2,10},{10,18},{18,26},{... | collective-permute-start | bytes 6152 | tf_op jit(solution)/shard_map/ppermute | solution.py:18
  10.8 23.3 %collective-permute-start.7 = (bf16[64,16,1]{2,1,0:T(8,128)(2,1)S(1)}, bf16[64,16,1]{2,1,0:T(8,128)(2,1)S(1)}, u32[]{:S(2)}, u32[]{:S(2)}) collective-permute-start(bf16[64,16,1]{2,1,0:T(8,128)(2,1)S(1)} %get-tuple-element.42), channel_id=1, source_target_pairs={{8,0},{16,8},{24,16},{9,1},{17,9},{25,17},{10,2},{18,10},{26,18},{... | collective-permute-start | bytes 6152 | tf_op jit(solution)/shard_map/ppermute | solution.py:20
  13.4 16.0 %all-to-all-start = ((s32[8,1,2]{2,1,0:T(1,128)}), s32[8,1,2]{2,1,0:T(1,128)S(1)}, u32[]{:S(2)}, u32[]{:S(2)}) async-start(s32[8,1,2]{2,1,0:T(1,128)} %copy.51), calls=%async_computation | async-start | bytes 8192 | tf_op jit(solution)/shard_map/all_to_all | solution.py:64
  21.1 22.6 %collective-permute-start = (bf16[1,64,1,128]{3,2,1,0:T(2,128)(2,1)S(1)}, bf16[1,64,1,128]{3,2,1,0:T(2,128)(2,1)S(1)}, u32[]{:S(2)}, u32[]{:S(2)}) collective-permute-start(bf16[1,64,1,128]{3,2,1,0:T(2,128)(2,1)S(1)} %get-tuple-element.17), channel_id=1, source_target_pairs={{0,1},{1,2},{2,3},{3,4},{4,5},{5,6},{6,7},{7,0},{8,9},{9,10},{10,1... | collective-permute-start | bytes 49160 | tf_op jit(solution)/shard_map/ppermute | solution.py:18
  23.1 20.5 %collective-permute-start.1 = (bf16[1,64,1,128]{3,2,1,0:T(2,128)(2,1)S(1)}, bf16[1,64,1,128]{3,2,1,0:T(2,128)(2,1)S(1)}, u32[]{:S(2)}, u32[]{:S(2)}) collective-permute-start(bf16[1,64,1,128]{3,2,1,0:T(2,128)(2,1)S(1)} %get-tuple-element.18), channel_id=1, source_target_pairs={{1,0},{2,1},{3,2},{4,3},{5,4},{6,5},{7,6},{0,7},{9,8},{10,9},{11,1... | collective-permute-start | bytes 49160 | tf_op jit(solution)/shard_map/ppermute | solution.py:20
  29.4 66.1 %all-to-all-start.1 = ((s32[8,1,256]{2,1,0:T(1,128)}), s32[8,1,256]{2,1,0:T(1,128)S(1)}, u32[]{:S(2)}, u32[]{:S(2)}) async-start(s32[8,1,256]{2,1,0:T(1,128)} %all_to_all.20), calls=%async_computation.1 | async-start | bytes 16384 | tf_op jit(solution)/shard_map/all_to_all | solution.py:63
  32.8 61.0 %all-gather.2.cloned.1.call-start = ((), (), s32[]{:S(2)}) async-start(), calls=%async_computation.6 | async-start | bytes 1310720 | tf_op jit(solution)/shard_map/all_gather | solution.py:130
  35.5 33.1 %collective-permute-start.8 = (bf16[64,1,130]{2,1,0:T(2,128)(2,1)S(1)}, bf16[64,1,130]{2,1,0:T(2,128)(2,1)S(1)}, u32[]{:S(2)}, u32[]{:S(2)}) collective-permute-start(bf16[64,1,130]{2,1,0:T(2,128)(2,1)S(1)} %get-tuple-element.24), channel_id=1, source_target_pairs={{1,0},{2,1},{3,2},{4,3},{5,4},{6,5},{7,6},{9,8},{10,9},{11,10},{12... | collective-permute-start | bytes 49928 | tf_op jit(solution)/shard_map/ppermute | solution.py:20
  36.8 31.8 %collective-permute-start.9 = (bf16[64,1,130]{2,1,0:T(2,128)(2,1)S(1)}, bf16[64,1,130]{2,1,0:T(2,128)(2,1)S(1)}, u32[]{:S(2)}, u32[]{:S(2)}) collective-permute-start(bf16[64,1,130]{2,1,0:T(2,128)(2,1)S(1)} %get-tuple-element.25), channel_id=1, source_target_pairs={{0,1},{1,2},{2,3},{3,4},{4,5},{5,6},{6,7},{8,9},{9,10},{10,11},{11... | collective-permute-start | bytes 49928 | tf_op jit(solution)/shard_map/ppermute | solution.py:18
  47.4 13.3 %copy-start.20 = (bf16[3,3,128,128]{3,2,1,0:T(8,128)(2,1)S(1)}, bf16[3,3,128,128]{3,2,1,0:T(8,128)(2,1)}, u32[]{:S(2)}) copy-start(bf16[3,3,128,128]{3,2,1,0:T(8,128)(2,1)} %param.14) | copy-start | bytes 884740
  73.1 6.0 %copy-start.9 = (bf16[64,256,128]{2,1,0:T(8,128)(2,1)S(1)}, bf16[64,256,128]{2,1,0:T(8,128)(2,1)}, u32[]{:S(2)}) copy-start(bf16[64,256,128]{2,1,0:T(8,128)(2,1)} %get-tuple-element.15) | copy-start | bytes 12582916
  97.5 32.1 %all-to-all-start.3 = ((f32[8,256,128]{2,1,0:T(8,128)}), f32[8,256,128]{2,1,0:T(8,128)S(1)}, u32[]{:S(2)}, u32[]{:S(2)}) async-start(f32[8,256,128]{2,1,0:T(8,128)} %bitcast.53), calls=%async_computation.4 | async-start | bytes 2097152 | tf_op jit(solution)/shard_map/all_to_all | solution.py:141
  103.4 6.1 %copy-start.4 = (bf16[64,256,128]{2,1,0:T(8,128)(2,1)S(1)}, bf16[64,256,128]{2,1,0:T(8,128)(2,1)}, u32[]{:S(2)}) copy-start(bf16[64,256,128]{2,1,0:T(8,128)(2,1)} %get-tuple-element.11) | copy-start | bytes 12582916
  168.0 18.7 %all-to-all-start.2 = ((bf16[8,256,128]{2,1,0:T(8,128)(2,1)}), bf16[8,256,128]{2,1,0:T(8,128)(2,1)S(1)}, u32[]{:S(2)}, u32[]{:S(2)}) async-start(bf16[8,256,128]{2,1,0:T(8,128)(2,1)} %broadcast_select_fusion.1), calls=%async_computation.2 | async-start | bytes 1048576 | tf_op jit(solution)/shard_map/all_to_all | solution.py:62
  171.9 59.0 %reduce-scatter.2.cloned.1.call-start = ((), (), s32[]{:S(2)}) async-start(), calls=%async_computation.5 | async-start | bytes 2621440 | tf_op jit(solution)/shard_map/reduce_scatter | solution.py:84
  195.2 6.2 %copy-start.16 = (f32[9,128,128]{2,1,0:T(8,128)S(1)}, f32[9,128,128]{2,1,0:T(8,128)}, u32[]{:S(2)}) copy-start(f32[9,128,128]{2,1,0:T(8,128)} %fusion.23) | copy-start | bytes 1769476
  201.4 222.3 %all-reduce.4.cloned.1.call-start = ((), (), s32[]{:S(2)}) async-start(), calls=%async_computation.7 | async-start | bytes 1769472 | tf_op jit(solution)/shard_map/psum | solution.py:163
  201.4 5.0 %copy-start.1 = (bf16[16384,128]{1,0:T(8,128)(2,1)S(1)}, bf16[16384,128]{1,0:T(8,128)(2,1)}, u32[]{:S(2)}) copy-start(bf16[16384,128]{1,0:T(8,128)(2,1)} %get-tuple-element.6) | copy-start | bytes 12582916
  201.4 6.7 %copy-start.11 = (bf16[64,256,128]{2,1,0:T(8,128)(2,1)S(1)}, bf16[64,256,128]{2,1,0:T(8,128)(2,1)}, u32[]{:S(2)}) copy-start(bf16[64,256,128]{2,1,0:T(8,128)(2,1)} %get-tuple-element.10) | copy-start | bytes 12582916
  232.7 45.7 %collective-permute-start.2 = (bf16[64,16,1]{2,0,1:T(8,128)(2,1)S(1)}, bf16[64,16,1]{2,0,1:T(8,128)(2,1)S(1)}, u32[]{:S(2)}, u32[]{:S(2)}) collective-permute-start(bf16[64,16,1]{2,0,1:T(8,128)(2,1)S(1)} %get-tuple-element.45), channel_id=1, source_target_pairs={{0,8},{8,16},{16,24},{1,9},{9,17},{17,25},{2,10},{10,18},{18,26},{... | collective-permute-start | bytes 6152 | tf_op jit(solution)/shard_map/ppermute | solution.py:18
  234.3 44.1 %collective-permute-start.3 = (bf16[64,16,1]{2,0,1:T(8,128)(2,1)S(1)}, bf16[64,16,1]{2,0,1:T(8,128)(2,1)S(1)}, u32[]{:S(2)}, u32[]{:S(2)}) collective-permute-start(bf16[64,16,1]{2,0,1:T(8,128)(2,1)S(1)} %get-tuple-element.46), channel_id=1, source_target_pairs={{8,0},{16,8},{24,16},{9,1},{17,9},{25,17},{10,2},{18,10},{26,18},{... | collective-permute-start | bytes 6152 | tf_op jit(solution)/shard_map/ppermute | solution.py:20
  278.5 5.8 %collective-permute-start.4 = (bf16[64,1,130]{2,0,1:T(8,128)(2,1)S(1)}, bf16[64,1,130]{2,0,1:T(8,128)(2,1)S(1)}, u32[]{:S(2)}, u32[]{:S(2)}) collective-permute-start(bf16[64,1,130]{2,0,1:T(8,128)(2,1)S(1)} %get-tuple-element.32), channel_id=1, source_target_pairs={{0,1},{1,2},{2,3},{3,4},{4,5},{5,6},{6,7},{8,9},{9,10},{10,11},{11... | collective-permute-start | bytes 49928 | tf_op jit(solution)/shard_map/ppermute | solution.py:18
  282.7 5.8 %collective-permute-start.5 = (bf16[64,1,130]{2,0,1:T(8,128)(2,1)S(1)}, bf16[64,1,130]{2,0,1:T(8,128)(2,1)S(1)}, u32[]{:S(2)}, u32[]{:S(2)}) collective-permute-start(bf16[64,1,130]{2,0,1:T(8,128)(2,1)S(1)} %get-tuple-element.31), channel_id=1, source_target_pairs={{1,0},{2,1},{3,2},{4,3},{5,4},{6,5},{7,6},{9,8},{10,9},{11,10},{12... | collective-permute-start | bytes 49928 | tf_op jit(solution)/shard_map/ppermute | solution.py:20
  (14 other events, 31.6 us)
Sparse Core Ops, SparseCore 0:
  73.2 20.5 all-gather.1
  201.5 29.4 reduce-scatter.1
  293.7 129.9 all-reduce.3
where the time goes:
time: 440 us; the launch traced here: 434 us
  waiting for transfers between devices  170 us (39%)
  matrix products  79 us (18%)
  local copies, waits for them, and re-layouts  51.4 us (12%)
  blocking collectives  42.8 us (10%)
  starting transfers between devices  42.7 us (10%)
  other arithmetic  33.3 us (8%)
  between operations  14.7 us (3%)
    psum x1, waiting for transfers between devices, shards(): lax.psum((range_local, proj_local, head_local), ('sweep', 'sector'))  128 us
    psum x1, blocking collectives, shards(): lax.psum((range_local, proj_local, head_local), ('sweep', 'sector'))  42.8 us
    dot_general x9, matrix products, shards(): jnp.dot(shifted(row_off, col_off), w_range[row_off, col_off], preferred_e...  42.2 us
    dot_general x9, matrix products, shards(): lax.dot_general(shifted(row_off, col_off), preact_grad, (((0,), (0,)), ((...  19.4 us
    unnamed x50, local copies, waits for them, and re-layouts  17.6 us
    scatter-add x1, other arithmetic, shards(): hidden_grad = jnp.zeros((pixel_total + 1, channels), jnp.float32).at[targ...  15.8 us
    ppermute x5, starting transfers between devices, extended(): lax.ppermute(tail, axis, [(i, (i + 1) % count) for i in range(ends)])  14.8 us
    all_to_all x1, waiting for transfers between devices, shards(): lax.all_to_all(row_grads, 'sector', split_axis=0, concat_axis=0, tiled=True)  13.4 us
  transfers between devices with their start and end apart: 17, of which 6 were waited for; matrix products, arithmetic and copies ran while one was open for 19% of the time, Pallas kernels for 0%

commit v1 on v0

v1 whole, which is shorter than its diff:
```python
import jax
import jax.numpy as jnp
from jax import lax
from jax.experimental import pallas as pl
from jax.experimental.pallas import tpu as pltpu
from jax.sharding import PartitionSpec as P

TILE = 16
CELLS = TILE * TILE
EDGE = 8
WIDE = 8
IDX_ROWS = 8
BF16 = jnp.bfloat16
F32 = jnp.float32
NT = (((1,), (1,)), ((), ()))
TN = (((0,), (0,)), ((), ()))


def dot(a, b, dims=(((1,), (0,)), ((), ()))):
    return lax.dot_general(a, b, dims, preferred_element_type=F32)


def gather_windows(base_ref, table, picked, first, slots, lines, pitch):
    def body(step, _):
        for k in range(8):
            slot = step * 8 + k
            base = base_ref[first + slot]
            for line in range(lines):
                picked[line, slot] = table[pl.ds(base + line * pitch, WIDE), :]
        return 0

    lax.fori_loop(0, slots // 8, body, 0)


def plane(picked, line, tap):
    return picked[line, :, tap, :]


def forward_kernel(
    base_ref, count_ref, image_ref, left_ref, right_ref, w_ref, wp_ref, idx_ref,
    patch_ref, slope_ref, rows_ref, send_ref, raw, table, picked, sem,
):
    step = pl.program_id(0)
    beams, columns, channels = image_ref.shape
    pitch = columns + 2 * EDGE
    slots = rows_ref.shape[0]
    chunks = raw.shape[0] // 8

    @pl.when(step == 0)
    def _():
        copies = []
        for c in range(chunks):
            part = pl.ds(c * 8, 8)
            copy = pltpu.make_async_copy(image_ref.at[part], raw.at[part], sem.at[c])
            copy.start()
            copies.append(copy)
        blank = jnp.zeros((pitch, channels), F32)
        table[pl.ds(0, pitch), :] = blank
        table[pl.ds((beams + 1) * pitch, pitch), :] = blank

        def edges(beam, _):
            line = (beam + 1) * pitch
            table[pl.ds(line + EDGE - 1, 1), :] = left_ref[pl.ds(beam, 1), :]
            table[pl.ds(line + EDGE + columns, 1), :] = right_ref[pl.ds(beam, 1), :]
            return 0

        lax.fori_loop(0, beams, edges, 0)
        for c in range(chunks):
            copies[c].wait()

            def widen(k, _):
                beam = c * 8 + k
                start = pl.multiple_of((beam + 1) * pitch + EDGE, 8)
                table[pl.ds(start, columns), :] = raw[beam].astype(F32)
                return 0

            lax.fori_loop(0, 8, widen, 0)

    @pl.when(step > 0)
    def _():
        band = step - 1
        gather_windows(base_ref, table, picked, band * slots, slots, 3, pitch)
        parts = [plane(picked, line, tap) for line in range(3) for tap in range(3)]
        patch = jnp.concatenate([p.astype(BF16) for p in parts], axis=1)
        patch_ref[...] = patch
        preact = dot(patch, w_ref[...])
        sigmoid = jax.nn.sigmoid(preact)
        slope_ref[...] = sigmoid * (1.0 + preact * (1.0 - sigmoid))
        live = lax.broadcasted_iota(jnp.int32, preact.shape, 0) < count_ref[band]
        rows = jnp.where(live, parts[4] + preact * sigmoid, 0.0).astype(BF16)
        rows_ref[...] = rows
        sent = dot(wp_ref[...], rows, NT)
        send_ref[0] = jnp.concatenate([sent, idx_ref[0]], axis=0).astype(BF16)


def forward(base, count, image, left, right, w_flat, wp_t, idx_rows):
    beams, columns, channels = image.shape
    bands, slots = base.shape
    head_ch = wp_t.shape[0]
    pitch = columns + 2 * EDGE
    taps = w_flat.shape[0]
    late = lambda i, *_: (jnp.maximum(i - 1, 0), 0)
    late3 = lambda i, *_: (jnp.maximum(i - 1, 0), 0, 0)
    whole = lambda i, *_: (0, 0)
    total = bands * slots
    return pl.pallas_call(
        forward_kernel,
        out_shape=(
            jax.ShapeDtypeStruct((total, taps), BF16),
            jax.ShapeDtypeStruct((total, channels), F32),
            jax.ShapeDtypeStruct((total, channels), BF16),
            jax.ShapeDtypeStruct((bands, head_ch + IDX_ROWS, slots), BF16),
        ),
        grid_spec=pltpu.PrefetchScalarGridSpec(
            num_scalar_prefetch=2,
            grid=(bands + 1,),
            in_specs=[
                pl.BlockSpec(memory_space=pl.ANY),
                pl.BlockSpec(left.shape, whole),
                pl.BlockSpec(right.shape, whole),
                pl.BlockSpec(w_flat.shape, whole),
                pl.BlockSpec(wp_t.shape, whole),
                pl.BlockSpec((1, IDX_ROWS, slots), late3),
            ],
            out_specs=[
                pl.BlockSpec((slots, taps), late),
                pl.BlockSpec((slots, channels), late),
                pl.BlockSpec((slots, channels), late),
                pl.BlockSpec((1, head_ch + IDX_ROWS, slots), late3),
            ],
            scratch_shapes=[
                pltpu.VMEM((beams, columns, channels), BF16),
                pltpu.VMEM(((beams + 2) * pitch, channels), F32),
                pltpu.VMEM((3, slots, WIDE, channels), F32),
                pltpu.SemaphoreType.DMA((beams // 8,)),
            ],
        ),
        compiler_params=pltpu.CompilerParams(dimension_semantics=("arbitrary",)),
        cost_estimate=pl.CostEstimate(
            flops=2 * total * taps * channels, bytes_accessed=24 << 20, transcendentals=0
        ),
        name="forward",
    )(base.reshape(-1), count, image, left, right, w_flat, wp_t, idx_rows)


def pick_kernel(base_ref, order_ref, cot_ref, wg_ref, window_ref, grad_ref, table, picked):
    step = pl.program_id(0)
    groups, lines, head_ch, columns = cot_ref.shape
    pitch = groups * columns + 2 * EDGE
    slots = window_ref.shape[0]

    @pl.when(step == 0)
    def _():
        blank = jnp.zeros((EDGE, 2 * head_ch), F32)

        def build(line, _):
            start = pl.multiple_of(line * pitch, 8)
            table[pl.ds(start, EDGE), :] = blank
            table[pl.ds(start + EDGE + groups * columns, EDGE), :] = blank
            for group in range(groups):
                held = order_ref[group]
                pair = jnp.concatenate([cot_ref[held, line], cot_ref[held, line + 1]], axis=0)
                at = pl.multiple_of(start + EDGE + group * columns, 8)
                table[pl.ds(at, columns), :] = pair.astype(F32).T
            return 0

        lax.fori_loop(0, lines - 1, build, 0)

    @pl.when(step > 0)
    def _():
        gather_windows(base_ref, table, picked, (step - 1) * slots, slots, 2, pitch)
        parts = [plane(picked, line, tap) for line in range(2) for tap in range(3)]
        window = jnp.concatenate([p.astype(BF16) for p in parts], axis=1)
        window_ref[...] = window
        grad_ref[0] = dot(wg_ref[...], window, NT).astype(BF16)


def pick(base, order, band_cot, wg):
    groups, lines, head_ch, columns = band_cot.shape
    sectors, slots = base.shape
    pitch = groups * columns + 2 * EDGE
    late = lambda i, *_: (jnp.maximum(i - 1, 0), 0)
    late3 = lambda i, *_: (jnp.maximum(i - 1, 0), 0, 0)
    total = sectors * slots
    return pl.pallas_call(
        pick_kernel,
        out_shape=(
            jax.ShapeDtypeStruct((total, 12 * head_ch), BF16),
            jax.ShapeDtypeStruct((sectors, head_ch, slots), BF16),
        ),
        grid_spec=pltpu.PrefetchScalarGridSpec(
            num_scalar_prefetch=2,
            grid=(sectors + 1,),
            in_specs=[
                pl.BlockSpec(band_cot.shape, lambda i, *_: (0, 0, 0, 0)),
                pl.BlockSpec(wg.shape, lambda i, *_: (0, 0)),
            ],
            out_specs=[
                pl.BlockSpec((slots, 12 * head_ch), late),
                pl.BlockSpec((1, head_ch, slots), late3),
            ],
            scratch_shapes=[
                pltpu.VMEM(((lines - 1) * pitch, 2 * head_ch), F32),
                pltpu.VMEM((2, slots, WIDE, 2 * head_ch), F32),
            ],
        ),
        compiler_params=pltpu.CompilerParams(dimension_semantics=("arbitrary",)),
        cost_estimate=pl.CostEstimate(
            flops=24 * total * head_ch * head_ch, bytes_accessed=12 << 20, transcendentals=0
        ),
        name="pick",
    )(base.reshape(-1), order, band_cot, wg)


def backward_kernel(
    count_ref, back_ref, sent_ref, slope_ref, rows_ref, patch_ref, window_ref, wp_ref,
    out_ref, range_acc, proj_acc, head_acc,
):
    step = pl.program_id(0)
    head_ch, slots = back_ref.shape[1:]
    channels = rows_ref.shape[1]

    @pl.when(step == 0)
    def _():
        range_acc[...] = jnp.zeros_like(range_acc)
        proj_acc[...] = jnp.zeros_like(proj_acc)
        head_acc[...] = jnp.zeros_like(head_acc)

    grads = back_ref[0]
    live = lax.broadcasted_iota(jnp.int32, grads.shape, 1) < count_ref[step]
    grads = jnp.where(live, grads.astype(F32), 0.0).astype(BF16)
    hidden_grad = dot(grads, wp_ref[...], TN)
    preact_grad = (hidden_grad * slope_ref[...]).T.astype(BF16)
    range_acc[...] += dot(preact_grad, patch_ref[...])
    proj_acc[...] += dot(grads, rows_ref[...])
    head_acc[...] += dot(sent_ref[0, :head_ch, :], window_ref[...])

    @pl.when(step == pl.num_programs(0) - 1)
    def _():
        taps = range_acc.shape[1] // channels
        for k in range(taps):
            out_ref[pl.ds(k * channels, channels), :] = (
                range_acc[:, k * channels : (k + 1) * channels].T.astype(BF16)
            )
        at = taps * channels
        out_ref[pl.ds(at, head_ch), :] = proj_acc[...].astype(BF16)
        wide = 2 * head_ch
        block = [head_acc[:, k * wide : (k + 1) * wide] for k in range(6)]
        first = lax.broadcasted_iota(jnp.int32, (head_ch, wide), 1) < head_ch
        both = jnp.where(first, pltpu.roll(block[3], head_ch, 1), block[4])
        for k, part in enumerate((block[0], block[1], block[2], both, block[5])):
            start = at + head_ch * (k + 1)
            out_ref[pl.ds(start, head_ch), :] = part.astype(BF16)


def backward(count, back, sent, slope, rows, patch, window, wp_t):
    bands, head_ch, slots = back.shape
    channels = rows.shape[1]
    taps = patch.shape[1]
    out_rows = taps + 6 * head_ch
    each = lambda i, *_: (i, 0)
    each3 = lambda i, *_: (i, 0, 0)
    total = bands * slots
    return pl.pallas_call(
        backward_kernel,
        out_shape=jax.ShapeDtypeStruct((out_rows, channels), BF16),
        grid_spec=pltpu.PrefetchScalarGridSpec(
            num_scalar_prefetch=1,
            grid=(bands,),
            in_specs=[
                pl.BlockSpec((1, head_ch, slots), each3),
                pl.BlockSpec((1,) + sent.shape[1:], each3),
                pl.BlockSpec((slots, channels), each),
                pl.BlockSpec((slots, channels), each),
                pl.BlockSpec((slots, taps), each),
                pl.BlockSpec((slots, window.shape[1]), each),
                pl.BlockSpec(wp_t.shape, lambda i, *_: (0, 0)),
            ],
            out_specs=pl.BlockSpec((out_rows, channels), lambda i, *_: (0, 0)),
            scratch_shapes=[
                pltpu.VMEM((channels, taps), F32),
                pltpu.VMEM((head_ch, channels), F32),
                pltpu.VMEM((head_ch, window.shape[1]), F32),
            ],
        ),
        compiler_params=pltpu.CompilerParams(dimension_semantics=("arbitrary",)),
        cost_estimate=pl.CostEstimate(
            flops=2 * total * taps * channels, bytes_accessed=10 << 20, transcendentals=0
        ),
        name="backward",
    )(count, back, sent, slope, rows, patch, window, wp_t)


def place_kernel(tile_ref, rows_ref, out_ref, acc):
    step = pl.program_id(0)
    tiles, head_ch, cells = acc.shape
    per_list = tile_ref.shape[0] // pl.num_programs(0)
    slot_len = rows_ref.shape[2] // per_list

    @pl.when(step == 0)
    def _():
        acc[...] = jnp.zeros_like(acc)

    for k in range(per_list):
        tile = tile_ref[step * per_list + k]

        @pl.when(jnp.logical_and(tile >= 0, tile < tiles))
        def _():
            part = rows_ref[0, :, k * slot_len : (k + 1) * slot_len]
            target = part[head_ch : head_ch + 1].astype(F32).astype(jnp.int32)
            places = lax.broadcasted_iota(jnp.int32, (cells, slot_len), 0)
            hot = jnp.where(places == target, 1.0, 0.0).astype(BF16)
            acc[tile] += dot(part[:head_ch], hot, NT)

    @pl.when(step == pl.num_programs(0) - 1)
    def _():
        out_ref[...] = acc[...].astype(BF16)


def place(tiles, rows, count, head_ch):
    lists, depth, slots = rows.shape
    return pl.pallas_call(
        place_kernel,
        out_shape=jax.ShapeDtypeStruct((count, head_ch, CELLS), BF16),
        grid_spec=pltpu.PrefetchScalarGridSpec(
            num_scalar_prefetch=1,
            grid=(lists,),
            in_specs=[pl.BlockSpec((1, depth, slots), lambda i, *_: (i, 0, 0))],
            out_specs=pl.BlockSpec((count, head_ch, CELLS), lambda i, *_: (0, 0, 0)),
            scratch_shapes=[pltpu.VMEM((count, head_ch, CELLS), F32)],
        ),
        compiler_params=pltpu.CompilerParams(dimension_semantics=("arbitrary",)),
        cost_estimate=pl.CostEstimate(
            flops=2 * lists * slots * head_ch * CELLS, bytes_accessed=2 << 20, transcendentals=0
        ),
        name="place",
    )(tiles, rows)


def gathered(block, axis):
    count = lax.axis_size(axis)
    places = jnp.arange(count, dtype=jnp.int32)
    if count & (count - 1):
        return lax.all_gather(block, axis), places
    held = block[None]
    bit = count // 2
    while bit:
        other = lax.ppermute(held, axis, [(i, i ^ bit) for i in range(count)])
        held = jnp.stack([held, other], axis=1).reshape((-1,) + block.shape)
        bit //= 2
    return held, places ^ lax.axis_index(axis)


def summed(rows, axes):
    count = 1
    for axis in axes:
        count *= lax.axis_size(axis)
    pieces = rows.reshape(count, rows.shape[0] // count, rows.shape[1])
    parts = lax.all_to_all(pieces, axes, split_axis=0, concat_axis=0, tiled=True)
    total = parts.astype(F32).sum(axis=0).astype(BF16)
    spread = jnp.broadcast_to(total[None], pieces.shape)
    return lax.all_to_all(spread, axes, split_axis=0, concat_axis=0, tiled=True).reshape(rows.shape)


def shards(
    range_image, send_pixel, send_cell, send_tile, send_count, w_range, w_proj, w_head, cotangent
):
    image = range_image[0]
    beams, columns, channels = image.shape
    head_ch, grid_rows, grid_cols = cotangent.shape
    count = send_count[0, 0]
    pixels, cells, tiles = send_pixel[0, 0], send_cell[0, 0], send_tile[0, 0]
    bands, slots = pixels.shape
    per_list = tiles.shape[1]
    sectors = lax.axis_size("sector")
    sweeps = lax.axis_size("sweep")
    sector, sweep = lax.axis_index("sector"), lax.axis_index("sweep")
    slot_tiles = jnp.repeat(tiles, slots // per_list, axis=1)

    cot_lines = cotangent.transpose(1, 0, 2)
    ahead = jnp.concatenate([image[:, columns - 1], cot_lines[grid_rows - 1]], axis=0)
    behind = jnp.concatenate([image[:, 0], cot_lines[0]], axis=0)
    from_left = lax.ppermute(ahead, "sector", [(i, (i + 1) % sectors) for i in range(sectors)])
    from_right = lax.ppermute(behind, "sector", [((i + 1) % sectors, i) for i in range(sectors)])
    targets_in = lax.all_to_all(
        slot_tiles * CELLS + cells, "sector", split_axis=0, concat_axis=0, tiled=True
    )

    none = jnp.zeros((), BF16)
    above = jnp.where(sector == 0, none, from_left[beams:])
    below = jnp.where(sector == sectors - 1, none, from_right[beams:])
    lines = jnp.concatenate([above[None], cot_lines, below[None]], axis=0)
    band_cot, order = gathered(lines, "sweep")
    band_pitch = sweeps * grid_cols + 2 * EDGE
    cell_in = targets_in % CELLS
    pick_base = (
        (cell_in // TILE) * band_pitch
        + (targets_in // CELLS) * TILE
        + cell_in % TILE
        + EDGE
        - 1
    )
    flipped = w_head[::-1, ::-1].transpose(2, 0, 1, 3)
    pair_low = jnp.concatenate([flipped[:, 0], flipped[:, 1]], axis=-1)
    pair_high = jnp.concatenate([jnp.zeros_like(flipped[:, 2]), flipped[:, 2]], axis=-1)
    wg = jnp.stack([pair_low, pair_high], axis=1).reshape(head_ch, -1)
    window, grad_out = pick(pick_base, order, band_cot, wg)
    back = lax.all_to_all(grad_out, "sector", split_axis=0, concat_axis=0, tiled=True)

    base = (pixels // columns) * (columns + 2 * EDGE) + pixels % columns + EDGE - 1
    idx_rows = jnp.pad(
        jnp.stack([cells, slot_tiles], axis=1).astype(F32), ((0, 0), (0, IDX_ROWS - 2), (0, 0))
    )
    wp_t = w_proj.T
    patch, slope, rows, sent = forward(
        base,
        count,
        image,
        from_left[:beams].astype(F32),
        from_right[:beams].astype(F32),
        w_range.reshape(-1, channels),
        wp_t,
        idx_rows,
    )
    sent_in = lax.all_to_all(sent, "sector", split_axis=0, concat_axis=0, tiled=True)

    local = backward(count, back, sent_in, slope, rows, patch, window, wp_t)
    total = summed(local, ("sweep", "sector")).astype(F32)
    taps = w_range.shape[0] * w_range.shape[1] * channels
    grad_range = total[:taps].reshape(w_range.shape)
    grad_proj = total[taps : taps + head_ch].T
    head_total = total[taps + head_ch :].reshape(5, head_ch, 2, head_ch)
    last = jnp.stack([head_total[3, :, 0], head_total[3, :, 1], head_total[4, :, 1]])
    by_a = jnp.stack([head_total[:3, :, 0], head_total[:3, :, 1], last])
    grad_head = by_a[::-1, ::-1]

    lists, _ = gathered(sent_in, "sweep")
    lists = lists.reshape((-1,) + sent_in.shape[1:])
    owned = grid_cols // TILE
    tile_rows = lists[:, head_ch + 1, :: slots // per_list].astype(jnp.int32).reshape(-1)
    ground = place(tile_rows - (sweep * owned - 1), lists, owned + 2, head_ch)
    ground = (
        ground.reshape(owned + 2, head_ch, TILE, TILE)
        .transpose(1, 2, 0, 3)
        .reshape(head_ch, TILE, (owned + 2) * TILE)[:, :, TILE - 1 : TILE + grid_cols + 1]
    )
    ground_pad = jnp.concatenate(
        [
            lax.ppermute(ground[:, -1:], "sector", [(i, i + 1) for i in range(sectors - 1)]),
            ground,
            lax.ppermute(ground[:, :1], "sector", [(i + 1, i) for i in range(sectors - 1)]),
        ],
        axis=1,
    )
    head_sum = jnp.zeros((head_ch, grid_rows * grid_cols), F32)
    for row_off in range(3):
        for col_off in range(3):
            view = ground_pad[:, row_off : row_off + grid_rows, col_off : col_off + grid_cols]
            head_sum = head_sum + dot(
                w_head[row_off, col_off].T, view.reshape(head_ch, -1)
            )
    head_out = head_sum.astype(BF16).reshape(head_ch, grid_rows, grid_cols)
    return head_out, grad_range, grad_proj, grad_head


def solution(mesh):
    return jax.shard_map(
        shards,
        mesh=mesh,
        in_specs=(
            P("sweep", None, "sector", None),
            P("sweep", "sector", None, None),
            P("sweep", "sector", None, None),
            P("sweep", "sector", None, None),
            P("sweep", "sector", None),
            P(),
            P(),
            P(),
            P(None, "sector", "sweep"),
        ),
        out_specs=(P(None, "sector", "sweep"), P(), P(), P()),
        check_vma=False,
    )
```

time: 440 us -> 166 us (0.38)
  waiting for transfers between devices: 170 us -> 35.4 us
  matrix products: 79 us -> 3 us
  Pallas kernels: 0 us -> 61.4 us
  blocking collectives: 42.8 us -> 0 us
  local copies, waits for them, and re-layouts: 51.4 us -> 16.7 us
  other arithmetic: 33.3 us -> 7.03 us
  between operations: 14.7 us -> 1.05 us
    psum x1 -> x0, waiting for transfers between devices: 128 us -> none  [shards(): lax.psum((range_local, proj_local, head_local), ('sweep', 'sector'))]
    dot_general x50 -> x9, matrix products: 79 us -> 3 us  [dot(): return lax.dot_general(a, b, dims, preferred_element_type=F32)]
    pallas_call x0 -> x4, Pallas kernels: none -> 61.4 us  [the longest x1 20.9 us: forward(): pl.pallas_call(forward_kernel, out_shape=(jax.ShapeDtypeStruct((total, ta...]
    psum x1 -> x0, blocking collectives: 42.8 us -> none  [shards(): lax.psum((range_local, proj_local, head_local), ('sweep', 'sector'))]
    scatter-add x2 -> x0, other arithmetic: 20.3 us -> none  [the longest x1 15.8 us: shards(): hidden_grad = jnp.zeros((pixel_total + 1, channels), jnp.float32).at[targ...]
    slice x5 -> x8, local copies, waits for them, and re-layouts: 16.1 us -> 1.88 us  [the longest x1 0.85 us: shards(): grad_range = total[:taps].reshape(w_range.shape)]
    all_to_all x4 -> x5, waiting for transfers between devices: 22.7 us -> 33.1 us  [the longest x1 11.3 us: summed(): lax.all_to_all(spread, axes, split_axis=0, concat_axis=0, tiled=True)]
    gather x2 -> x0, local copies, waits for them, and re-layouts: 10.1 us -> none  [the longest x1 8.32 us: shards(): hidden[pixels]]
  transfers between devices with their start and end apart: 17 -> 13, of which waited for: 6 -> 6; matrix products, arithmetic and copies ran while one was open for 19% -> 10% of each run, Pallas kernels for 0% -> 37%
where the time goes in v1:
time: 166 us; the launch traced here: 164 us
  Pallas kernels  61.4 us (37%)
  starting transfers between devices  39.4 us (24%)
  waiting for transfers between devices  35.4 us (21%)
  local copies, waits for them, and re-layouts  16.7 us (10%)
  other arithmetic  7.03 us (4%)
  matrix products  3 us (2%)
    pallas_call x1, Pallas kernels, forward(): pl.pallas_call(forward_kernel, out_shape=(jax.ShapeDtypeStruct((total, ta...  20.9 us
    pallas_call x1, Pallas kernels, pick(): pl.pallas_call(pick_kernel, out_shape=(jax.ShapeDtypeStruct((total, 12 *...  15.4 us
    pallas_call x1, Pallas kernels, place(): pl.pallas_call(place_kernel, out_shape=jax.ShapeDtypeStruct((count, head_...  15.1 us
    all_to_all x1, waiting for transfers between devices, summed(): lax.all_to_all(spread, axes, split_axis=0, concat_axis=0, tiled=True)  11.3 us
    pallas_call x1, Pallas kernels, backward(): pl.pallas_call(backward_kernel, out_shape=jax.ShapeDtypeStruct((out_rows,...  9.99 us
    all_to_all x1, waiting for transfers between devices, shards(): lax.all_to_all(grad_out, 'sector', split_axis=0, concat_axis=0, tiled=True)  9.57 us
    all_to_all x1, starting transfers between devices, summed(): lax.all_to_all(spread, axes, split_axis=0, concat_axis=0, tiled=True)  7.7 us
    unnamed x18, local copies, waits for them, and re-layouts  7.54 us
  transfers between devices with their start and end apart: 13, of which 6 were waited for; matrix products, arithmetic and copies ran while one was open for 10% of the time, Pallas kernels for 37%

profile of v1, /device:TPU:0, one launch (start us, length us, event | category | flops | bytes accessed | tf_op | source)
XLA Modules:
  0.0 164.0 jit_solution(12451142962425184280)
XLA Ops:
  1.7 5.0 %copy.41 = bf16[1,64,256,128]{3,1,2,0:T(8,128)(2,1)S(1)} copy(bf16[1,64,256,128]{3,2,1,0:T(8,128)(2,1)} %param.9) | data formatting | bytes 8388608 | tf_op args[0]
  6.7 3.0 %collective-permute-start = (bf16[128,128]{1,0:T(8,128)(2,1)S(1)}, bf16[128,128]{1,0:T(8,128)(2,1)S(1)}, u32[]{:S(2)}, u32[]{:S(2)}) collective-permute-start(bf16[128,128]{1,0:T(8,128)(2,1)S(1)} %pad_maximum_fusion.9), channel_id=1, source_target_pairs={{0,1},{1,2},{2,3},{3,4},{4,5},{5,6},{6,7},{7,0},{8,9},{9,10},{10,1... | collective-permute-start | bytes 98312 | tf_op jit(solution)/shard_map/ppermute | solution.py:383
  9.7 3.1 %collective-permute-start.1 = (bf16[128,128]{1,0:T(8,128)(2,1)S(1)}, bf16[128,128]{1,0:T(8,128)(2,1)S(1)}, u32[]{:S(2)}, u32[]{:S(2)}) collective-permute-start(bf16[128,128]{1,0:T(8,128)(2,1)S(1)} %pad_maximum_fusion.10), channel_id=1, source_target_pairs={{1,0},{2,1},{3,2},{4,3},{5,4},{6,5},{7,6},{0,7},{9,8},{10,9},{11,1... | collective-permute-start | bytes 98312 | tf_op jit(solution)/shard_map/ppermute | solution.py:384
  15.9 1.8 %collective-permute-start.6 = (bf16[1,18,64,128]{3,2,1,0:T(8,128)(2,1)S(1)}, bf16[1,18,64,128]{3,2,1,0:T(8,128)(2,1)S(1)}, u32[]{:S(2)}, u32[]{:S(2)}) collective-permute-start(bf16[1,18,64,128]{3,2,1,0:T(8,128)(2,1)S(1)} %get-tuple-element.42), channel_id=1, source_target_pairs={{0,16},{8,24},{16,0},{24,8},{1,17},{9,25},{17,1},{25,9},{2,18},{10... | collective-permute-start | bytes 884744 | tf_op jit(solution)/shard_map/ppermute | solution.py:348
  18.4 20.9 %forward.1 = (bf16[2048,1152]{1,0:T(8,128)(2,1)}, f32[2048,128]{1,0:T(8,128)}, bf16[2048,128]{1,0:T(8,128)(2,1)}, bf16[8,72,256]{2,1,0:T(8,128)(2,1)}) custom-call(s32[2048]{0:T(1024)} %fusion.37.base_ref, s32[8]{0:T(128)} %bitcast.176, bf16[64,256,128]{2,1,0:T(8,128)(2,1)} %bitcast.134, f32[64,128]{1,0:T(8,128)} %get-tuple-element.49.left_ref, ...), custom_call_target="tpu_custom_call" | custom-call | flops 603979776 | bytes 25165824 | tf_op jit(solution)/shard_map/forward/pallas_call | solution.py:106
  39.4 5.4 %all-to-all-start = ((bf16[8,72,256]{2,1,0:T(8,128)(2,1)}), bf16[8,72,256]{2,1,0:T(8,128)(2,1)S(1)}, u32[]{:S(2)}, u32[]{:S(2)}) async-start(bf16[8,72,256]{2,1,0:T(8,128)(2,1)} %get-tuple-element.10), calls=%async_computation | async-start | bytes 589824 | tf_op jit(solution)/shard_map/all_to_all | solution.py:425
  45.7 7.5 %all-to-all-done.sent_ref = bf16[8,72,256]{2,1,0:T(8,128)(2,1)S(1)} async-done(((bf16[8,72,256]{2,1,0:T(8,128)(2,1)}), bf16[8,72,256]{2,1,0:T(8,128)(2,1)S(1)}, u32[]{:S(2)}, u32[]{:S(2)}) %all-to-all-start) | async-done | bytes 294944 | tf_op jit(solution)/shard_map/all_to_all | solution.py:425
  53.2 3.3 %all-to-all-start.1 = ((s32[8,1,256]{2,1,0:T(1,128)}), s32[8,1,256]{2,1,0:T(1,128)S(1)}, u32[]{:S(2)}, u32[]{:S(2)}) async-start(s32[8,1,256]{2,1,0:T(1,128)} %multiply_add_fusion), calls=%async_computation.1 | async-start | bytes 16384 | tf_op jit(solution)/shard_map/all_to_all | solution.py:385
  58.3 4.7 %all-to-all-done.1 = s32[8,1,256]{2,1,0:T(1,128)S(1)} async-done(((s32[8,1,256]{2,1,0:T(1,128)}), s32[8,1,256]{2,1,0:T(1,128)S(1)}, u32[]{:S(2)}, u32[]{:S(2)}) %all-to-all-start.1) | async-done | bytes 8224 | tf_op jit(solution)/shard_map/all_to_all | solution.py:385
  63.8 1.2 pad_maximum_fusion.1
  65.0 1.2 copy.26
  66.2 15.4 %pick.1 = (bf16[2048,768]{1,0:T(8,128)(2,1)}, bf16[8,64,256]{2,1,0:T(8,128)(2,1)}) custom-call(s32[2048]{0:T(1024)} %fusion.41.base_ref, s32[4]{0:T(128)} %iota_xor_fusion.order_ref, bf16[4,18,64,128]{3,2,1,0:T(8,128)(2,1)} %bitcast.140, bf16[64,768]{1,0:T(8,128)(2,1)} %reshape.121.wg_ref), custom_call_target="tpu_custom_call" | custom-call | flops 201326592 | bytes 12582912 | tf_op jit(solution)/shard_map/pick/pallas_call | solution.py:185
  81.6 5.6 %all-to-all-start.2 = ((bf16[8,64,256]{2,1,0:T(8,128)(2,1)}), bf16[8,64,256]{2,1,0:T(8,128)(2,1)S(1)}, u32[]{:S(2)}, u32[]{:S(2)}) async-start(bf16[8,64,256]{2,1,0:T(8,128)(2,1)} %get-tuple-element.11), calls=%async_computation.2 | async-start | bytes 524288 | tf_op jit(solution)/shard_map/all_to_all | solution.py:408
  87.2 9.6 %all-to-all-done.2.back_ref = bf16[8,64,256]{2,1,0:T(8,128)(2,1)S(1)} async-done(((bf16[8,64,256]{2,1,0:T(8,128)(2,1)}), bf16[8,64,256]{2,1,0:T(8,128)(2,1)S(1)}, u32[]{:S(2)}, u32[]{:S(2)}) %all-to-all-start.2) | async-done | bytes 262176 | tf_op jit(solution)/shard_map/all_to_all | solution.py:408
  97.5 10.0 %backward.1 = bf16[1536,128]{1,0:T(8,128)(2,1)} custom-call(s32[8]{0:T(128)} %bitcast.177, bf16[8,64,256]{2,1,0:T(8,128)(2,1)} %copy-done.2, bf16[8,72,256]{2,1,0:T(8,128)(2,1)} %copy-done.1, f32[2048,128]{1,0:T(8,128)} %get-tuple-element.12.slope_ref, bf16[2048,128]{1,0:T(8,128)(2,1)} %get-tuple-element.13.rows_ref, ...), custom_call_target="tpu_custom_call" | custom-call | flops 603979776 | bytes 10485760 | tf_op jit(solution)/shard_map/backward/pallas_call | solution.py:264
  107.5 2.7 %all-to-all-start.3 = ((bf16[32,48,128]{2,1,0:T(8,128)(2,1)}), bf16[32,48,128]{2,1,0:T(8,128)(2,1)S(1)}, u32[]{:S(2)}, u32[]{:S(2)}) async-start(bf16[32,48,128]{2,1,0:T(8,128)(2,1)} %bitcast.154), calls=%async_computation.3 | async-start | bytes 786432 | tf_op jit(solution)/shard_map/all_to_all | solution.py:359
  110.2 1.2 pad_maximum_fusion
  112.5 15.1 %place.1 = bf16[10,64,256]{2,1,0:T(8,128)(2,1)} custom-call(s32[64]{0:T(128)} %sub.39.tile_ref, bf16[32,72,256]{2,1,0:T(8,128)(2,1)} %bitcast.139), custom_call_target="tpu_custom_call" | custom-call | flops 268435456 | bytes 2097152 | tf_op jit(solution)/shard_map/place/pallas_call | solution.py:322
  127.5 1.3 copy.24
  129.4 1.3 collective-permute-start.5
  130.7 4.9 %collective-permute-start.4 = (bf16[64,1,130]{0,2,1:T(8,128)(2,1)S(1)}, bf16[64,1,130]{0,2,1:T(8,128)(2,1)S(1)}, u32[]{:S(2)}, u32[]{:S(2)}) collective-permute-start(bf16[64,1,130]{0,2,1:T(8,128)(2,1)S(1)} %get-tuple-element.19), channel_id=1, source_target_pairs={{0,1},{1,2},{2,3},{3,4},{4,5},{5,6},{6,7},{8,9},{9,10},{10,11},{11... | collective-permute-start | bytes 49928 | tf_op jit(solution)/shard_map/ppermute | solution.py:449
  136.1 1.2 collective-permute-done.4
  140.1 7.7 %all-to-all-start.4 = ((bf16[32,48,128]{2,1,0:T(8,128)(2,1)}), bf16[32,48,128]{2,1,0:T(8,128)(2,1)S(1)}, u32[]{:S(2)}, u32[]{:S(2)}) async-start(bf16[32,48,128]{2,1,0:T(8,128)(2,1)} %broadcast_in_dim.33), calls=%async_computation.4 | async-start | bytes 786432 | tf_op jit(solution)/shard_map/all_to_all | solution.py:362
  149.9 11.3 %all-to-all-done.4 = bf16[32,48,128]{2,1,0:T(8,128)(2,1)S(1)} async-done(((bf16[32,48,128]{2,1,0:T(8,128)(2,1)}), bf16[32,48,128]{2,1,0:T(8,128)(2,1)S(1)}, u32[]{:S(2)}, u32[]{:S(2)}) %all-to-all-start.4) | async-done | bytes 393248 | tf_op jit(solution)/shard_map/all_to_all | solution.py:362
  (82 shorter events, 18.6 us)
Async XLA Ops:
  1.7 11.2 %copy-start.5 = (s32[1,1,8,256]{3,2,1,0:T(8,128)S(1)}, s32[1,1,8,256]{3,2,1,0:T(8,128)}, u32[]{:S(2)}) copy-start(s32[1,1,8,256]{3,2,1,0:T(8,128)} %param.10) | copy-start | bytes 24580
  1.7 11.2 %copy-start.3 = (bf16[3,3,64,64]{3,2,1,0:T(8,128)(2,1)S(1)}, bf16[3,3,64,64]{3,2,1,0:T(8,128)(2,1)}, u32[]{:S(2)}) copy-start(bf16[3,3,64,64]{3,2,1,0:T(8,128)(2,1)} %param.16) | copy-start | bytes 221188
  1.7 11.8 %copy-start.6 = (s32[1,1,8,2]{2,3,1,0:T(2,128)S(1)}, s32[1,1,8,2]{2,3,1,0:T(2,128)}, u32[]{:S(2)}) copy-start(s32[1,1,8,2]{2,3,1,0:T(2,128)} %param.12) | copy-start | bytes 196
  1.7 11.9 %copy-start.4 = (s32[1,1,8,256]{3,2,1,0:T(8,128)S(1)}, s32[1,1,8,256]{3,2,1,0:T(8,128)}, u32[]{:S(2)}) copy-start(s32[1,1,8,256]{3,2,1,0:T(8,128)} %param.11) | copy-start | bytes 24580
  6.7 8.0 %collective-permute-start = (bf16[128,128]{1,0:T(8,128)(2,1)S(1)}, bf16[128,128]{1,0:T(8,128)(2,1)S(1)}, u32[]{:S(2)}, u32[]{:S(2)}) collective-permute-start(bf16[128,128]{1,0:T(8,128)(2,1)S(1)} %pad_maximum_fusion.9), channel_id=1, source_target_pairs={{0,1},{1,2},{2,3},{3,4},{4,5},{5,6},{6,7},{7,0},{8,9},{9,10},{10,1... | collective-permute-start | bytes 98312 | tf_op jit(solution)/shard_map/ppermute | solution.py:383
  9.7 5.6 %collective-permute-start.1 = (bf16[128,128]{1,0:T(8,128)(2,1)S(1)}, bf16[128,128]{1,0:T(8,128)(2,1)S(1)}, u32[]{:S(2)}, u32[]{:S(2)}) collective-permute-start(bf16[128,128]{1,0:T(8,128)(2,1)S(1)} %pad_maximum_fusion.10), channel_id=1, source_target_pairs={{1,0},{2,1},{3,2},{4,3},{5,4},{6,5},{7,6},{0,7},{9,8},{10,9},{11,1... | collective-permute-start | bytes 98312 | tf_op jit(solution)/shard_map/ppermute | solution.py:384
  15.9 29.4 %collective-permute-start.6 = (bf16[1,18,64,128]{3,2,1,0:T(8,128)(2,1)S(1)}, bf16[1,18,64,128]{3,2,1,0:T(8,128)(2,1)S(1)}, u32[]{:S(2)}, u32[]{:S(2)}) collective-permute-start(bf16[1,18,64,128]{3,2,1,0:T(8,128)(2,1)S(1)} %get-tuple-element.42), channel_id=1, source_target_pairs={{0,16},{8,24},{16,0},{24,8},{1,17},{9,25},{17,1},{25,9},{2,18},{10... | collective-permute-start | bytes 884744 | tf_op jit(solution)/shard_map/ppermute | solution.py:348
  39.4 13.8 %all-to-all-start = ((bf16[8,72,256]{2,1,0:T(8,128)(2,1)}), bf16[8,72,256]{2,1,0:T(8,128)(2,1)S(1)}, u32[]{:S(2)}, u32[]{:S(2)}) async-start(bf16[8,72,256]{2,1,0:T(8,128)(2,1)} %get-tuple-element.10), calls=%async_computation | async-start | bytes 589824 | tf_op jit(solution)/shard_map/all_to_all | solution.py:425
  45.5 18.3 %collective-permute-start.7 = (bf16[2,18,64,128]{3,2,1,0:T(8,128)(2,1)S(1)}, bf16[2,18,64,128]{3,2,1,0:T(8,128)(2,1)}, u32[]{:S(2)}, u32[]{:S(2)}) collective-permute-start(bf16[2,18,64,128]{3,2,1,0:T(8,128)(2,1)S(1)} %get-tuple-element.30), channel_id=1, source_target_pairs={{0,8},{8,0},{16,24},{24,16},{1,9},{9,1},{17,25},{25,17},{2,10},{10... | collective-permute-start | bytes 1769480 | tf_op jit(solution)/shard_map/ppermute | solution.py:348
  53.2 11.8 %copy-start.1 = (bf16[8,72,256]{2,1,0:T(8,128)(2,1)}, bf16[8,72,256]{2,1,0:T(8,128)(2,1)S(1)}, u32[]{:S(2)}) copy-start(bf16[8,72,256]{2,1,0:T(8,128)(2,1)S(1)} %all-to-all-done.sent_ref) | copy-start | bytes 884740
  53.2 9.8 %all-to-all-start.1 = ((s32[8,1,256]{2,1,0:T(1,128)}), s32[8,1,256]{2,1,0:T(1,128)S(1)}, u32[]{:S(2)}, u32[]{:S(2)}) async-start(s32[8,1,256]{2,1,0:T(1,128)} %multiply_add_fusion), calls=%async_computation.1 | async-start | bytes 16384 | tf_op jit(solution)/shard_map/all_to_all | solution.py:385
  56.6 7.1 %collective-permute-start.2 = (bf16[1,8,72,256]{3,2,1,0:T(8,128)(2,1)S(1)}, bf16[1,8,72,256]{3,2,1,0:T(8,128)(2,1)S(1)}, u32[]{:S(2)}, u32[]{:S(2)}) collective-permute-start(bf16[1,8,72,256]{3,2,1,0:T(8,128)(2,1)S(1)} %bitcast.142), channel_id=1, source_target_pairs={{0,16},{8,24},{16,0},{24,8},{1,17},{9,25},{17,1},{25,9},{2,18},{10... | collective-permute-start | bytes 884744 | tf_op jit(solution)/shard_map/ppermute | solution.py:348
  63.7 46.4 %collective-permute-start.3 = (bf16[2,8,72,256]{3,2,1,0:T(8,128)(2,1)S(1)}, bf16[2,8,72,256]{3,2,1,0:T(8,128)(2,1)}, u32[]{:S(2)}, u32[]{:S(2)}) collective-permute-start(bf16[2,8,72,256]{3,2,1,0:T(8,128)(2,1)S(1)} %get-tuple-element.32), channel_id=1, source_target_pairs={{0,8},{8,0},{16,24},{24,16},{1,9},{9,1},{17,25},{25,17},{2,10},{10... | collective-permute-start | bytes 1769480 | tf_op jit(solution)/shard_map/ppermute | solution.py:348
  81.6 15.1 %all-to-all-start.2 = ((bf16[8,64,256]{2,1,0:T(8,128)(2,1)}), bf16[8,64,256]{2,1,0:T(8,128)(2,1)S(1)}, u32[]{:S(2)}, u32[]{:S(2)}) async-start(bf16[8,64,256]{2,1,0:T(8,128)(2,1)} %get-tuple-element.11), calls=%async_computation.2 | async-start | bytes 524288 | tf_op jit(solution)/shard_map/all_to_all | solution.py:408
  96.8 0.7 copy-start.2
  107.5 31.7 %all-to-all-start.3 = ((bf16[32,48,128]{2,1,0:T(8,128)(2,1)}), bf16[32,48,128]{2,1,0:T(8,128)(2,1)S(1)}, u32[]{:S(2)}, u32[]{:S(2)}) async-start(bf16[32,48,128]{2,1,0:T(8,128)(2,1)} %bitcast.154), calls=%async_computation.3 | async-start | bytes 786432 | tf_op jit(solution)/shard_map/all_to_all | solution.py:359
  111.4 1.0 copy-start
  129.4 6.7 %collective-permute-start.5 = (bf16[64,1,130]{0,2,1:T(8,128)(2,1)S(1)}, bf16[64,1,130]{0,2,1:T(8,128)(2,1)S(1)}, u32[]{:S(2)}, u32[]{:S(2)}) collective-permute-start(bf16[64,1,130]{0,2,1:T(8,128)(2,1)S(1)} %get-tuple-element.18), channel_id=1, source_target_pairs={{1,0},{2,1},{3,2},{4,3},{5,4},{6,5},{7,6},{9,8},{10,9},{11,10},{12... | collective-permute-start | bytes 49928 | tf_op jit(solution)/shard_map/ppermute | solution.py:451
  130.7 6.6 %collective-permute-start.4 = (bf16[64,1,130]{0,2,1:T(8,128)(2,1)S(1)}, bf16[64,1,130]{0,2,1:T(8,128)(2,1)S(1)}, u32[]{:S(2)}, u32[]{:S(2)}) collective-permute-start(bf16[64,1,130]{0,2,1:T(8,128)(2,1)S(1)} %get-tuple-element.19), channel_id=1, source_target_pairs={{0,1},{1,2},{2,3},{3,4},{4,5},{5,6},{6,7},{8,9},{9,10},{10,11},{11... | collective-permute-start | bytes 49928 | tf_op jit(solution)/shard_map/ppermute | solution.py:449
  140.1 21.1 %all-to-all-start.4 = ((bf16[32,48,128]{2,1,0:T(8,128)(2,1)}), bf16[32,48,128]{2,1,0:T(8,128)(2,1)S(1)}, u32[]{:S(2)}, u32[]{:S(2)}) async-start(bf16[32,48,128]{2,1,0:T(8,128)(2,1)} %broadcast_in_dim.33), calls=%async_computation.4 | async-start | bytes 786432 | tf_op jit(solution)/shard_map/all_to_all | solution.py:362

commit v2 on v1

v2 whole, which is shorter than its diff:
```python
import functools

import jax
import jax.numpy as jnp
from jax import lax
from jax.experimental import pallas as pl
from jax.experimental.pallas import tpu as pltpu
from jax.sharding import PartitionSpec as P


TILE = 16
CELLS = TILE * TILE
EDGE = 8
WIDE = 8
IDX_ROWS = 8
BF16 = jnp.bfloat16
F32 = jnp.float32
NT = (((1,), (1,)), ((), ()))
TN = (((0,), (0,)), ((), ()))


def dot(a, b, dims=(((1,), (0,)), ((), ()))):
    return lax.dot_general(a, b, dims, preferred_element_type=F32)


def gather_windows(base_ref, table, picked, first, slots, lines, pitch):
    def body(step, _):
        for k in range(8):
            slot = step * 8 + k
            base = base_ref[first + slot]
            for line in range(lines):
                at = pl.multiple_of((line * slots + slot) * WIDE, WIDE)
                picked[pl.ds(at, WIDE), :] = table[pl.ds(base + line * pitch, WIDE), :]
        return 0

    lax.fori_loop(0, slots // 8, body, 0)


def plane(picked, slots, line, tap):
    return picked[pl.ds(line * slots * WIDE + tap, slots, stride=WIDE), :]


def edges_kernel(sectors, image_ref, cot_ref, ahead_ref, behind_ref, lines_ref, raw, cot, wide, sem):
    beams, columns, channels = image_ref.shape
    head_ch, rows, grid_cols = cot_ref.shape
    span = raw.shape[2]
    sector = lax.axis_index("sector")
    cot_copy = pltpu.make_async_copy(cot_ref, cot, sem.at[2])
    cot_copy.start()
    copies = []
    for k, first in enumerate((0, columns - span)):
        part = image_ref.at[:, pl.ds(first, span), :]
        copy = pltpu.make_async_copy(part, raw.at[k], sem.at[k])
        copy.start()
        copies.append(copy)
    cot_copy.wait()
    wide[pl.ds(0, head_ch * rows), :] = cot[...].astype(F32).reshape(head_ch * rows, grid_cols)
    for row in range(rows):
        line = wide[pl.ds(row, head_ch, stride=rows), :].astype(BF16)
        lines_ref[row] = line
        if row == 0:
            behind_ref[pl.ds(beams, head_ch), :] = jnp.where(sector > 0, line, 0)
        if row == rows - 1:
            ahead_ref[pl.ds(beams, head_ch), :] = jnp.where(sector < sectors - 1, line, 0)
    for k, (out_ref, at) in enumerate(((behind_ref, 0), (ahead_ref, span - 1))):
        copies[k].wait()
        wide[pl.ds(0, beams * span), :] = raw[k].astype(F32).reshape(beams * span, channels)
        out_ref[pl.ds(0, beams), :] = wide[pl.ds(at, beams, stride=span), :].astype(BF16)


def edges(image, cot):
    beams, _, channels = image.shape
    head_ch, rows, grid_cols = cot.shape
    edge = jax.ShapeDtypeStruct((beams + head_ch, channels), BF16)
    vmem = pl.BlockSpec(memory_space=pltpu.VMEM)
    return pl.pallas_call(
        functools.partial(edges_kernel, lax.axis_size("sector")),
        out_shape=(edge, edge, jax.ShapeDtypeStruct((rows, head_ch, grid_cols), BF16)),
        in_specs=[pl.BlockSpec(memory_space=pltpu.HBM)] * 2,
        out_specs=(vmem, vmem, vmem),
        scratch_shapes=[
            pltpu.VMEM((2, beams, TILE, channels), BF16),
            pltpu.VMEM(cot.shape, BF16),
            pltpu.VMEM((max(beams * TILE, head_ch * rows), channels), F32),
            pltpu.SemaphoreType.DMA((3,)),
        ],
        compiler_params=pltpu.CompilerParams(vmem_limit_bytes=4 << 20),
        name="edges",
    )(image, cot)


def forward_kernel(
    base_ref, count_ref, image_ref, left_ref, right_ref, w_ref, wp_ref, target_ref,
    patch_ref, slope_ref, rows_ref, send_ref, raw, table, ends, picked, sem,
):
    step = pl.program_id(0)
    beams, columns, channels = image_ref.shape
    pitch = columns + 2 * EDGE
    slots = rows_ref.shape[0]
    chunks = raw.shape[0] // 8

    @pl.when(step == 0)
    def _():
        copies = []
        for c in range(chunks):
            part = pl.ds(c * 8, 8)
            copy = pltpu.make_async_copy(image_ref.at[part], raw.at[part], sem.at[c])
            copy.start()
            copies.append(copy)
        blank = jnp.zeros((pitch, channels), F32)
        table[pl.ds(0, pitch), :] = blank
        table[pl.ds((beams + 1) * pitch, pitch), :] = blank
        ends[0] = left_ref[pl.ds(0, beams), :].astype(F32)
        ends[1] = right_ref[pl.ds(0, beams), :].astype(F32)

        def sides(beam, _):
            line = (beam + 1) * pitch
            table[pl.ds(line + EDGE - 1, 1), :] = ends[0, pl.ds(beam, 1), :]
            table[pl.ds(line + EDGE + columns, 1), :] = ends[1, pl.ds(beam, 1), :]
            return 0

        lax.fori_loop(0, beams, sides, 0, unroll=8)
        for c in range(chunks):
            copies[c].wait()

            def widen(k, _):
                beam = c * 8 + k
                start = pl.multiple_of((beam + 1) * pitch + EDGE, 8)
                table[pl.ds(start, columns), :] = raw[beam].astype(F32)
                return 0

            lax.fori_loop(0, 8, widen, 0)

    @pl.when(step > 0)
    def _():
        band = step - 1
        gather_windows(base_ref, table, picked, band * slots, slots, 3, pitch)
        parts = [plane(picked, slots, line, tap) for line in range(3) for tap in range(3)]
        patch = jnp.concatenate([p.astype(BF16) for p in parts], axis=1)
        patch_ref[...] = patch
        preact = dot(patch, w_ref[...])
        sigmoid = jax.nn.sigmoid(preact)
        slope_ref[...] = sigmoid * (1.0 + preact * (1.0 - sigmoid))
        live = lax.broadcasted_iota(jnp.int32, preact.shape, 0) < count_ref[band]
        rows = jnp.where(live, parts[4] + preact * sigmoid, 0.0).astype(BF16)
        rows_ref[...] = rows
        sent = dot(wp_ref[...], rows, NT)
        target = jnp.broadcast_to(target_ref[0], (IDX_ROWS, slots))
        row = lax.broadcasted_iota(jnp.int32, target.shape, 0)
        tile = lax.div(target, CELLS)
        whole = jnp.where(row == 0, target - tile * CELLS, jnp.where(row == 1, tile, 0))
        send_ref[0, 0] = jnp.concatenate([sent, whole.astype(F32)], axis=0).astype(BF16)


def forward(base, count, image, left, right, w_flat, wp_t, targets):
    beams, columns, channels = image.shape
    bands, slots = base.shape
    head_ch = wp_t.shape[0]
    pitch = columns + 2 * EDGE
    taps = w_flat.shape[0]
    late = lambda i, *_: (jnp.maximum(i - 1, 0), 0)
    late3 = lambda i, *_: (jnp.maximum(i - 1, 0), 0, 0)
    late4 = lambda i, *_: (jnp.maximum(i - 1, 0), 0, 0, 0)
    whole = lambda i, *_: (0, 0)
    total = bands * slots
    return pl.pallas_call(
        forward_kernel,
        out_shape=(
            jax.ShapeDtypeStruct((total, taps), BF16),
            jax.ShapeDtypeStruct((total, channels), F32),
            jax.ShapeDtypeStruct((total, channels), BF16),
            jax.ShapeDtypeStruct((bands, 2, head_ch + IDX_ROWS, slots), BF16),
        ),
        grid_spec=pltpu.PrefetchScalarGridSpec(
            num_scalar_prefetch=2,
            grid=(bands + 1,),
            in_specs=[
                pl.BlockSpec(memory_space=pltpu.HBM),
                pl.BlockSpec(left.shape, whole),
                pl.BlockSpec(right.shape, whole),
                pl.BlockSpec(w_flat.shape, whole),
                pl.BlockSpec(wp_t.shape, whole),
                pl.BlockSpec((1, 1, slots), late3),
            ],
            out_specs=[
                pl.BlockSpec((slots, taps), late),
                pl.BlockSpec((slots, channels), late),
                pl.BlockSpec((slots, channels), late),
                pl.BlockSpec((1, 1, head_ch + IDX_ROWS, slots), late4),
            ],
            scratch_shapes=[
                pltpu.VMEM((beams, columns, channels), BF16),
                pltpu.VMEM(((beams + 2) * pitch, channels), F32),
                pltpu.VMEM((2, beams, channels), F32),
                pltpu.VMEM((3 * slots * WIDE, channels), F32),
                pltpu.SemaphoreType.DMA((beams // 8,)),
            ],
        ),
        compiler_params=pltpu.CompilerParams(
            dimension_semantics=("arbitrary",), vmem_limit_bytes=24 << 20
        ),
        cost_estimate=pl.CostEstimate(
            flops=2 * total * taps * channels, bytes_accessed=24 << 20, transcendentals=0
        ),
        name="forward",
    )(base.reshape(-1), count, image, left, right, w_flat, wp_t, targets[:, None])


def pick_kernel(
    base_ref, order_ref, cot_ref, wg_ref, send_ref, window_ref, grad_ref, table, picked
):
    step = pl.program_id(0)
    groups, lines, head_ch, columns = cot_ref.shape
    pitch = groups * columns + 2 * EDGE
    slots = window_ref.shape[0]

    @pl.when(step == 0)
    def _():
        blank = jnp.zeros((EDGE, 2 * head_ch), F32)

        def build(line, _):
            start = pl.multiple_of(line * pitch, 8)
            table[pl.ds(start, EDGE), :] = blank
            table[pl.ds(start + EDGE + groups * columns, EDGE), :] = blank
            for group in range(groups):
                held = order_ref[group]
                pair = jnp.concatenate([cot_ref[held, line], cot_ref[held, line + 1]], axis=0)
                at = pl.multiple_of(start + EDGE + group * columns, 8)
                table[pl.ds(at, columns), :] = pair.astype(F32).T
            return 0

        lax.fori_loop(0, lines - 1, build, 0)

    @pl.when(step > 0)
    def _():
        gather_windows(base_ref, table, picked, (step - 1) * slots, slots, 2, pitch)
        parts = [plane(picked, slots, line, tap) for line in range(2) for tap in range(3)]
        window = jnp.concatenate([p.astype(BF16) for p in parts], axis=1)
        window_ref[...] = window
        grad = dot(wg_ref[...], window, NT)
        spare = jnp.zeros((IDX_ROWS, slots), F32)
        grad_ref[0, 0] = jnp.concatenate([grad, spare], axis=0).astype(BF16)


def pick(base, order, band_cot, wg, send):
    groups, lines, head_ch, columns = band_cot.shape
    sectors, slots = base.shape
    pitch = groups * columns + 2 * EDGE
    late = lambda i, *_: (jnp.maximum(i - 1, 0), 0)
    late4 = lambda i, *_: (jnp.maximum(i - 1, 0), 1, 0, 0)
    total = sectors * slots
    return pl.pallas_call(
        pick_kernel,
        out_shape=(
            jax.ShapeDtypeStruct((total, 12 * head_ch), BF16),
            jax.ShapeDtypeStruct(send.shape, BF16),
        ),
        grid_spec=pltpu.PrefetchScalarGridSpec(
            num_scalar_prefetch=2,
            grid=(sectors + 1,),
            in_specs=[
                pl.BlockSpec(band_cot.shape, lambda i, *_: (0, 0, 0, 0)),
                pl.BlockSpec(wg.shape, lambda i, *_: (0, 0)),
                pl.BlockSpec(memory_space=pl.ANY),
            ],
            out_specs=[
                pl.BlockSpec((slots, 12 * head_ch), late),
                pl.BlockSpec((1, 1) + send.shape[2:], late4),
            ],
            scratch_shapes=[
                pltpu.VMEM(((lines - 1) * pitch, 2 * head_ch), F32),
                pltpu.VMEM((2 * slots * WIDE, 2 * head_ch), F32),
            ],
        ),
        input_output_aliases={4: 1},
        compiler_params=pltpu.CompilerParams(
            dimension_semantics=("arbitrary",), vmem_limit_bytes=16 << 20
        ),
        cost_estimate=pl.CostEstimate(
            flops=24 * total * head_ch * head_ch, bytes_accessed=12 << 20, transcendentals=0
        ),
        name="pick",
    )(base.reshape(-1), order, band_cot, wg, send)


def backward_kernel(
    count_ref, back_ref, sent_ref, slope_ref, rows_ref, patch_ref, window_ref, wp_ref,
    out_ref, range_acc, proj_acc, head_acc,
):
    step = pl.program_id(0)
    head_ch = wp_ref.shape[0]
    channels = rows_ref.shape[1]

    @pl.when(step == 0)
    def _():
        range_acc[...] = jnp.zeros_like(range_acc)
        proj_acc[...] = jnp.zeros_like(proj_acc)
        head_acc[...] = jnp.zeros_like(head_acc)

    grads = back_ref[0, 0, :head_ch, :]
    live = lax.broadcasted_iota(jnp.int32, grads.shape, 1) < count_ref[step]
    grads = jnp.where(live, grads.astype(F32), 0.0).astype(BF16)
    hidden_grad = dot(grads, wp_ref[...], TN)
    preact_grad = (hidden_grad * slope_ref[...]).T.astype(BF16)
    range_acc[...] += dot(preact_grad, patch_ref[...])
    proj_acc[...] += dot(grads, rows_ref[...])
    head_acc[...] += dot(sent_ref[0, 0, :head_ch, :], window_ref[...])

    @pl.when(step == pl.num_programs(0) - 1)
    def _():
        taps = range_acc.shape[1] // channels
        for k in range(taps):
            out_ref[pl.ds(k * channels, channels), :] = (
                range_acc[:, k * channels : (k + 1) * channels].T.astype(BF16)
            )
        at = taps * channels
        out_ref[pl.ds(at, head_ch), :] = proj_acc[...].astype(BF16)
        wide = 2 * head_ch
        block = [head_acc[:, k * wide : (k + 1) * wide] for k in range(6)]
        first = lax.broadcasted_iota(jnp.int32, (head_ch, wide), 1) < head_ch
        both = jnp.where(first, pltpu.roll(block[3], head_ch, 1), block[4])
        for k, part in enumerate((block[0], block[1], block[2], both, block[5])):
            start = at + head_ch * (k + 1)
            out_ref[pl.ds(start, head_ch), :] = part.astype(BF16)


def backward(count, mixed, slope, rows, patch, window, wp_t):
    bands, _, depth, slots = mixed.shape
    head_ch, channels = wp_t.shape
    taps = patch.shape[1]
    out_rows = taps + 6 * head_ch
    each = lambda i, *_: (i, 0)
    total = bands * slots
    return pl.pallas_call(
        backward_kernel,
        out_shape=jax.ShapeDtypeStruct((out_rows, channels), BF16),
        grid_spec=pltpu.PrefetchScalarGridSpec(
            num_scalar_prefetch=1,
            grid=(bands,),
            in_specs=[
                pl.BlockSpec((1, 1, depth, slots), lambda i, *_: (i, 1, 0, 0)),
                pl.BlockSpec((1, 1, depth, slots), lambda i, *_: (i, 0, 0, 0)),
                pl.BlockSpec((slots, channels), each),
                pl.BlockSpec((slots, channels), each),
                pl.BlockSpec((slots, taps), each),
                pl.BlockSpec((slots, window.shape[1]), each),
                pl.BlockSpec(wp_t.shape, lambda i, *_: (0, 0)),
            ],
            out_specs=pl.BlockSpec((out_rows, channels), lambda i, *_: (0, 0)),
            scratch_shapes=[
                pltpu.VMEM((channels, taps), F32),
                pltpu.VMEM((head_ch, channels), F32),
                pltpu.VMEM((head_ch, window.shape[1]), F32),
            ],
        ),
        compiler_params=pltpu.CompilerParams(
            dimension_semantics=("arbitrary",), vmem_limit_bytes=12 << 20
        ),
        cost_estimate=pl.CostEstimate(
            flops=2 * total * taps * channels, bytes_accessed=10 << 20, transcendentals=0
        ),
        name="backward",
    )(count, mixed, mixed, slope, rows, patch, window, wp_t)


def place_kernel(tile_ref, rows_ref, out_ref, acc):
    tiles, head_ch, cells = acc.shape
    lists, _, slots = rows_ref.shape
    per_list = tile_ref.shape[0] // lists
    slot_len = slots // per_list
    acc[...] = jnp.zeros_like(acc)

    def body(step, _):
        for k in range(per_list):
            tile = tile_ref[step * per_list + k]

            @pl.when(jnp.logical_and(tile >= 0, tile < tiles))
            def _():
                part = rows_ref[step, :, k * slot_len : (k + 1) * slot_len]
                target = part[head_ch : head_ch + 1].astype(F32).astype(jnp.int32)
                places = lax.broadcasted_iota(jnp.int32, (cells, slot_len), 0)
                hot = jnp.where(places == target, 1.0, 0.0).astype(BF16)
                acc[tile] += dot(part[:head_ch], hot, NT)

        return 0

    lax.fori_loop(0, lists, body, 0)
    out_ref[...] = acc[...].astype(BF16)


def place(tiles, rows, count, head_ch):
    lists, _, slots = rows.shape
    return pl.pallas_call(
        place_kernel,
        out_shape=jax.ShapeDtypeStruct((count, head_ch, CELLS), BF16),
        in_specs=[
            pl.BlockSpec(memory_space=pltpu.SMEM),
            pl.BlockSpec(memory_space=pltpu.VMEM),
        ],
        out_specs=pl.BlockSpec(memory_space=pltpu.VMEM),
        scratch_shapes=[pltpu.VMEM((count, head_ch, CELLS), F32)],
        compiler_params=pltpu.CompilerParams(vmem_limit_bytes=12 << 20),
        cost_estimate=pl.CostEstimate(
            flops=2 * lists * slots * head_ch * CELLS, bytes_accessed=2 << 20, transcendentals=0
        ),
        name="place",
    )(tiles, rows)


def gathered(block, axis):
    count = lax.axis_size(axis)
    places = jnp.arange(count, dtype=jnp.int32)
    if count & (count - 1):
        return lax.all_gather(block, axis), places
    held = block[None]
    bit = count // 2
    while bit:
        other = lax.ppermute(held, axis, [(i, i ^ bit) for i in range(count)])
        held = jnp.stack([held, other], axis=1).reshape((-1,) + block.shape)
        bit //= 2
    return held, places ^ lax.axis_index(axis)


def exchanged(block, axis):
    count = lax.axis_size(axis)
    places = jnp.arange(count, dtype=jnp.int32)
    steps = [
        lax.ppermute(block, axis, [(i, (i + k) % count) for i in range(count)])
        for k in range(1, count)
    ]
    return jnp.stack([block] + steps), (lax.axis_index(axis) - places) % count


def summed(rows, axes):
    count = 1
    for axis in axes:
        count *= lax.axis_size(axis)
    pieces = rows.reshape(count, rows.shape[0] // count, rows.shape[1])
    parts = lax.all_to_all(pieces, axes, split_axis=0, concat_axis=0, tiled=True)
    total = parts.astype(F32).sum(axis=0).astype(BF16)
    spread = jnp.broadcast_to(total[None], pieces.shape)
    spread = lax.all_to_all(spread, axes, split_axis=0, concat_axis=0, tiled=True)
    return spread.reshape(rows.shape)


def shards(
    range_image, send_pixel, send_cell, send_tile, send_count, w_range, w_proj, w_head, cotangent
):
    image = pltpu.with_memory_space_constraint(range_image[0], pltpu.HBM)
    beams, columns, channels = image.shape
    head_ch, grid_rows, grid_cols = cotangent.shape
    count = send_count[0, 0]
    pixels, cells, tiles = send_pixel[0, 0], send_cell[0, 0], send_tile[0, 0]
    _, slots = pixels.shape
    per_list = tiles.shape[1]
    sectors = lax.axis_size("sector")
    sweeps = lax.axis_size("sweep")
    sweep = lax.axis_index("sweep")
    slot_tiles = jnp.repeat(tiles, slots // per_list, axis=1)

    ahead, behind, cot_lines = edges(image, pltpu.with_memory_space_constraint(cotangent, pltpu.HBM))
    ring = [(i, (i + 1) % sectors) for i in range(sectors)]
    from_left = lax.ppermute(ahead, "sector", ring)
    from_right = lax.ppermute(behind, "sector", [(j, i) for i, j in ring])
    targets = slot_tiles * CELLS + cells
    targets_in = lax.all_to_all(targets, "sector", split_axis=0, concat_axis=0, tiled=True)

    base = (pixels // columns) * (columns + 2 * EDGE) + pixels % columns + EDGE - 1
    wp_t = w_proj.T
    lines = jnp.concatenate(
        [from_left[beams:][None], cot_lines, from_right[beams:][None]], axis=0
    )
    band_cot, order = exchanged(lines, "sweep")
    patch, slope, rows, send = forward(
        base, count, image, from_left, from_right, w_range.reshape(-1, channels), wp_t, targets
    )

    band_pitch = sweeps * grid_cols + 2 * EDGE
    cell_in = targets_in % CELLS
    pick_base = (
        (cell_in // TILE) * band_pitch
        + (targets_in // CELLS) * TILE
        + cell_in % TILE
        + EDGE
        - 1
    )
    flipped = w_head[::-1, ::-1].transpose(2, 0, 1, 3)
    pair_low = jnp.concatenate([flipped[:, 0], flipped[:, 1]], axis=-1)
    pair_high = jnp.concatenate([jnp.zeros_like(flipped[:, 2]), flipped[:, 2]], axis=-1)
    wg = jnp.stack([pair_low, pair_high], axis=1).reshape(head_ch, -1)
    window, send = pick(pick_base, order, band_cot, wg, send)
    mixed = lax.all_to_all(send, "sector", split_axis=0, concat_axis=0, tiled=True)
    sent_in = mixed[:, 0]

    lists, _ = gathered(sent_in, "sweep")
    lists = lists.reshape((-1,) + sent_in.shape[1:])
    owned = grid_cols // TILE
    tile_rows = lists[:, head_ch + 1, :: slots // per_list].astype(jnp.int32).reshape(-1)
    ground = place(tile_rows - (sweep * owned - 1), lists, owned + 2, head_ch)
    local = backward(count, mixed, slope, rows, patch, window, wp_t)
    total = summed(local, ("sweep", "sector")).astype(F32)
    taps = w_range.shape[0] * w_range.shape[1] * channels
    grad_range = total[:taps].reshape(w_range.shape)
    grad_proj = total[taps : taps + head_ch].T
    head_total = total[taps + head_ch :].reshape(5, head_ch, 2, head_ch)
    last = jnp.stack([head_total[3, :, 0], head_total[3, :, 1], head_total[4, :, 1]])
    by_a = jnp.stack([head_total[:3, :, 0], head_total[:3, :, 1], last])
    grad_head = by_a[::-1, ::-1]

    ground = (
        ground.reshape(owned + 2, head_ch, TILE, TILE)
        .transpose(1, 2, 0, 3)
        .reshape(head_ch, TILE, (owned + 2) * TILE)[:, :, TILE - 1 : TILE + grid_cols + 1]
    )
    over = lax.ppermute(ground[:, -1:], "sector", ring[:-1])
    under = lax.ppermute(ground[:, :1], "sector", [(j, i) for i, j in ring[:-1]])
    ground_pad = jnp.concatenate([over, ground, under], axis=1)
    head_sum = jnp.zeros((head_ch, grid_rows * grid_cols), F32)
    for row_off in range(3):
        for col_off in range(3):
            view = ground_pad[:, row_off : row_off + grid_rows, col_off : col_off + grid_cols]
            head_sum = head_sum + dot(
                w_head[row_off, col_off].T, view.reshape(head_ch, -1)
            )
    head_out = head_sum.astype(BF16).reshape(head_ch, grid_rows, grid_cols)
    return head_out, grad_range, grad_proj, grad_head


def solution(mesh):
    return jax.shard_map(
        shards,
        mesh=mesh,
        in_specs=(
            P("sweep", None, "sector", None),
            P("sweep", "sector", None, None),
            P("sweep", "sector", None, None),
            P("sweep", "sector", None, None),
            P("sweep", "sector", None),
            P(),
            P(),
            P(),
            P(None, "sector", "sweep"),
        ),
        out_specs=(P(None, "sector", "sweep"), P(), P(), P()),
        check_vma=False,
    )
```

time: 166 us -> 113 us (0.68)
  Pallas kernels: 61.4 us -> 31.8 us
  blocking collectives: 0 us -> 21.4 us
  waiting for transfers between devices: 35.4 us -> 15.9 us
  starting transfers between devices: 39.4 us -> 28.2 us
  local copies, waits for them, and re-layouts: 16.7 us -> 6.06 us
  other arithmetic: 7.03 us -> 3.56 us
    all_to_all x3 -> x1, waiting for transfers between devices: 21.8 us -> 0.01 us  [shards(): lax.all_to_all(targets, 'sector', split_axis=0, concat_axis=0, tiled=True)]
    all_to_all x0 -> x1, blocking collectives: none -> 21.4 us  [shards(): lax.all_to_all(send, 'sector', split_axis=0, concat_axis=0, tiled=True)]
    all_to_all x1, waiting for transfers between devices: 0.01 us -> 13.1 us  [summed(): lax.all_to_all(pieces, axes, split_axis=0, concat_axis=0, tiled=True)]
    all_to_all x1, waiting for transfers between devices: 11.3 us -> 0.01 us  [summed(): lax.all_to_all(spread, axes, split_axis=0, concat_axis=0, tiled=True)]
    pallas_call x1, Pallas kernels: 15.1 us -> 4.52 us  [place(): pl.pallas_call(place_kernel, out_shape=jax.ShapeDtypeStruct((count, head_...]
    pallas_call x1, Pallas kernels: 20.9 us -> 11.7 us  [forward(): pl.pallas_call(forward_kernel, out_shape=(jax.ShapeDtypeStruct((total, ta...]
    pallas_call x1, Pallas kernels: 15.4 us -> 8.13 us  [pick(): pl.pallas_call(pick_kernel, out_shape=(jax.ShapeDtypeStruct((total, 12 *...]
    all_to_all x3 -> x1, starting transfers between devices: 14.3 us -> 7.28 us  [shards(): lax.all_to_all(targets, 'sector', split_axis=0, concat_axis=0, tiled=True)]
  transfers between devices with their start and end apart: 13 -> 12, of which waited for: 6 -> 3; matrix products, arithmetic and copies ran while one was open for 10% -> 7% of each run, Pallas kernels for 37% -> 21%
where the time goes in v2:
time: 113 us; the launch traced here: 111 us
  Pallas kernels  31.8 us (28%)
  starting transfers between devices  28.2 us (25%)
  blocking collectives  21.4 us (19%)
  waiting for transfers between devices  15.9 us (14%)
  local copies, waits for them, and re-layouts  6.06 us (5%)
  other arithmetic  3.56 us (3%)
  matrix products  2.98 us (3%)
    all_to_all x1, blocking collectives, shards(): lax.all_to_all(send, 'sector', split_axis=0, concat_axis=0, tiled=True)  21.4 us
    all_to_all x1, waiting for transfers between devices, summed(): lax.all_to_all(pieces, axes, split_axis=0, concat_axis=0, tiled=True)  13.1 us
    pallas_call x1, Pallas kernels, forward(): pl.pallas_call(forward_kernel, out_shape=(jax.ShapeDtypeStruct((total, ta...  11.7 us
    pallas_call x1, Pallas kernels, pick(): pl.pallas_call(pick_kernel, out_shape=(jax.ShapeDtypeStruct((total, 12 *...  8.13 us
    all_to_all x1, starting transfers between devices, shards(): lax.all_to_all(targets, 'sector', split_axis=0, concat_axis=0, tiled=True)  7.28 us
    pallas_call x1, Pallas kernels, backward(): pl.pallas_call(backward_kernel, out_shape=jax.ShapeDtypeStruct((out_rows,...  6.12 us
    ppermute x1, starting transfers between devices, shards(): over = lax.ppermute(ground[:, -1:], 'sector', ring[:-1])  4.55 us
    pallas_call x1, Pallas kernels, place(): pl.pallas_call(place_kernel, out_shape=jax.ShapeDtypeStruct((count, head_...  4.52 us
  transfers between devices with their start and end apart: 12, of which 3 were waited for; matrix products, arithmetic and copies ran while one was open for 7% of the time, Pallas kernels for 21%

profile of v2, /device:TPU:0, one launch (start us, length us, event | category | flops | bytes accessed | tf_op | source)
XLA Modules:
  0.0 111.0 jit_solution(3731212789788268497)
XLA Ops:
  1.5 1.3 %reshape_add_fusion.target_ref = s32[8,1,256]{2,1,0:T(1,128)} fusion(s32[8,1,256]{2,1,0:T(1,128)S(1)} %bitcast.152, s32[1,1,8,256]{3,2,1,0:T(8,128)} %param.11), kind=kLoop, calls=%fused_computation.95 | loop fusion | flops 2048 | bytes 24576 | tf_op jit(solution)/shard_map/add | solution.py:465
  2.8 7.3 %all-to-all-start = ((s32[8,1,256]{2,1,0:T(1,128)}), s32[8,1,256]{2,1,0:T(1,128)S(1)}, u32[]{:S(2)}, u32[]{:S(2)}) async-start(s32[8,1,256]{2,1,0:T(1,128)} %reshape_add_fusion.target_ref), calls=%async_computation | async-start | bytes 16384 | tf_op jit(solution)/shard_map/all_to_all | solution.py:466
  10.1 1.3 %edges.1 = (bf16[128,128]{1,0:T(8,128)(2,1)S(1)}, bf16[128,128]{1,0:T(8,128)(2,1)S(1)}, bf16[16,64,128]{2,1,0:T(8,128)(2,1)S(1)}) custom-call(bf16[64,256,128]{2,1,0:T(8,128)(2,1)} %bitcast.123, bf16[64,16,128]{2,1,0:T(8,128)(2,1)} %cot_ref.1), custom_call_target="tpu_custom_call" | custom-call | tf_op jit(solution)/shard_map/edges/pallas_call | solution.py:76
  11.4 2.1 %collective-permute-start = (bf16[128,128]{1,0:T(8,128)(2,1)S(1)}, bf16[128,128]{1,0:T(8,128)(2,1)S(1)}, u32[]{:S(2)}, u32[]{:S(2)}) collective-permute-start(bf16[128,128]{1,0:T(8,128)(2,1)S(1)} %get-tuple-element.13), channel_id=1, source_target_pairs={{0,1},{1,2},{2,3},{3,4},{4,5},{5,6},{6,7},{7,0},{8,9},{9,10},{10,1... | collective-permute-start | bytes 98312 | tf_op jit(solution)/shard_map/ppermute | solution.py:463
  13.5 2.8 %collective-permute-start.1 = (bf16[128,128]{1,0:T(8,128)(2,1)S(1)}, bf16[128,128]{1,0:T(8,128)(2,1)S(1)}, u32[]{:S(2)}, u32[]{:S(2)}) collective-permute-start(bf16[128,128]{1,0:T(8,128)(2,1)S(1)} %get-tuple-element.15), channel_id=1, source_target_pairs={{1,0},{2,1},{3,2},{4,3},{5,4},{6,5},{7,6},{0,7},{9,8},{10,9},{11,1... | collective-permute-start | bytes 98312 | tf_op jit(solution)/shard_map/ppermute | solution.py:464
  16.5 1.6 %collective-permute-done.left_ref = bf16[128,128]{1,0:T(8,128)(2,1)S(1)} collective-permute-done((bf16[128,128]{1,0:T(8,128)(2,1)S(1)}, bf16[128,128]{1,0:T(8,128)(2,1)S(1)}, u32[]{:S(2)}, u32[]{:S(2)}) %collective-permute-start) | collective-permute-done | bytes 32800 | tf_op jit(solution)/shard_map/ppermute | solution.py:463
  18.1 1.6 %collective-permute-start.3 = (bf16[18,64,128]{2,1,0:T(8,128)(2,1)S(1)}, bf16[18,64,128]{2,1,0:T(8,128)(2,1)S(1)}, u32[]{:S(2)}, u32[]{:S(2)}) collective-permute-start(bf16[18,64,128]{2,1,0:T(8,128)(2,1)S(1)} %get-tuple-element.46), channel_id=1, source_target_pairs={{0,16},{8,24},{16,0},{24,8},{1,17},{9,25},{17,1},{25,9},{2,18},{10... | collective-permute-start | bytes 884744 | tf_op jit(solution)/shard_map/ppermute | solution.py:428
  19.7 1.7 %collective-permute-start.4 = (bf16[18,64,128]{2,1,0:T(8,128)(2,1)S(1)}, bf16[18,64,128]{2,1,0:T(8,128)(2,1)S(1)}, u32[]{:S(2)}, u32[]{:S(2)}) collective-permute-start(bf16[18,64,128]{2,1,0:T(8,128)(2,1)S(1)} %get-tuple-element.46), channel_id=1, source_target_pairs={{0,24},{8,0},{16,8},{24,16},{1,25},{9,1},{17,9},{25,17},{2,26},{10... | collective-permute-start | bytes 884744 | tf_op jit(solution)/shard_map/ppermute | solution.py:428
  21.7 11.7 %forward.1 = (bf16[2048,1152]{1,0:T(8,128)(2,1)S(1)}, f32[2048,128]{1,0:T(8,128)S(1)}, bf16[2048,128]{1,0:T(8,128)(2,1)S(1)}, bf16[8,2,72,256]{3,2,1,0:T(8,128)(2,1)S(1)}) custom-call(s32[2048]{0:T(1024)S(1)} %fusion.36.base_ref, s32[8]{0:T(128)S(1)} %bitcast.121, bf16[64,256,128]{2,1,0:T(8,128)(2,1)} %bitcast.124, ...), custom_call_target="tpu_custom_call" | custom-call | flops 603979776 | bytes 25165824 | tf_op jit(solution)/shard_map/forward/pallas_call | solution.py:166
  33.6 8.1 %pick.1 = (bf16[2048,768]{1,0:T(8,128)(2,1)S(1)}, bf16[8,2,72,256]{3,2,1,0:T(8,128)(2,1)S(1)}) custom-call(s32[2048]{0:T(1024)S(1)} %fusion.32.base_ref, s32[4]{0:T(128)S(1)} %and_select_fusion.order_ref, bf16[4,18,64,128]{3,2,1,0:T(8,128)(2,1)S(1)} %pad_maximum_fusion.cot_ref, ...), custom_call_target="tpu_custom_call", output_to_operand_aliasing={{1}: (4, {})} | custom-call | flops 201326592 | bytes 12582912 | tf_op jit(solution)/shard_map/pick/pallas_call | solution.py:252
  41.7 21.4 %all_to_all.24.back_ref.sent_ref = bf16[8,2,72,256]{3,2,1,0:T(8,128)(2,1)S(1)} all-to-all(bf16[8,2,72,256]{3,2,1,0:T(8,128)(2,1)S(1)} %get-tuple-element.17), channel_id=1, replica_groups=mesh['sweep'=4,'sector'=8] {'sector'}, dimensions={0} | all-to-all | bytes 1179648 | tf_op jit(solution)/shard_map/all_to_all | solution.py:492
  63.2 1.6 %collective-permute-start.5 = (bf16[1,8,72,256]{3,2,1,0:T(8,128)(2,1)S(1)}, bf16[1,8,72,256]{3,2,1,0:T(8,128)(2,1)S(1)}, u32[]{:S(2)}, u32[]{:S(2)}) collective-permute-start(bf16[1,8,72,256]{3,2,1,0:T(8,128)(2,1)S(1)} %get-tuple-element.36), channel_id=1, source_target_pairs={{0,16},{8,24},{16,0},{24,8},{1,17},{9,25},{17,1},{25,9},{2,18},{10... | collective-permute-start | bytes 884744 | tf_op jit(solution)/shard_map/ppermute | solution.py:418
  64.8 6.1 %backward.1 = bf16[1536,128]{1,0:T(8,128)(2,1)} custom-call(s32[8]{0:T(128)S(1)} %bitcast.122, bf16[8,2,72,256]{3,2,1,0:T(8,128)(2,1)S(1)} %all_to_all.24.back_ref.sent_ref, bf16[8,2,72,256]{3,2,1,0:T(8,128)(2,1)S(1)} %all_to_all.24.back_ref.sent_ref, f32[2048,128]{1,0:T(8,128)S(1)} %get-tuple-element.18.slope_ref, ...), custom_call_target="tpu_custom_call" | custom-call | flops 603979776 | bytes 10485760 | tf_op jit(solution)/shard_map/backward/pallas_call | solution.py:334
  70.9 2.6 %all-to-all-start.2 = ((bf16[32,48,128]{2,1,0:T(8,128)(2,1)}), bf16[32,48,128]{2,1,0:T(8,128)(2,1)S(1)}, u32[]{:S(2)}, u32[]{:S(2)}) async-start(bf16[32,48,128]{2,1,0:T(8,128)(2,1)} %bitcast.48), calls=%async_computation.2 | async-start | bytes 786432 | tf_op jit(solution)/shard_map/all_to_all | solution.py:439
  73.8 13.1 %all-to-all-done.2 = bf16[32,48,128]{2,1,0:T(8,128)(2,1)S(1)} async-done(((bf16[32,48,128]{2,1,0:T(8,128)(2,1)}), bf16[32,48,128]{2,1,0:T(8,128)(2,1)S(1)}, u32[]{:S(2)}, u32[]{:S(2)}) %all-to-all-start.2) | async-done | bytes 393248 | tf_op jit(solution)/shard_map/all_to_all | solution.py:439
  87.0 0.8 broadcast_in_dim.20
  87.8 2.6 %all-to-all-start.3 = ((bf16[32,48,128]{2,1,0:T(8,128)(2,1)}), bf16[32,48,128]{2,1,0:T(8,128)(2,1)S(1)}, u32[]{:S(2)}, u32[]{:S(2)}) async-start(bf16[32,48,128]{2,1,0:T(8,128)(2,1)} %broadcast_in_dim.20), calls=%async_computation.3 | async-start | bytes 786432 | tf_op jit(solution)/shard_map/all_to_all | solution.py:442
  91.1 4.5 %place.1 = bf16[10,64,256]{2,1,0:T(8,128)(2,1)S(1)} custom-call(s32[64]{0:T(128)S(1)} %sub.50.tile_ref, bf16[32,72,256]{2,1,0:T(8,128)(2,1)S(1)} %bitcast.117), custom_call_target="tpu_custom_call" | custom-call | flops 268435456 | bytes 2097152 | tf_op jit(solution)/shard_map/place/pallas_call | solution.py:393
  96.4 1.3 %collective-permute-start.8 = (bf16[64,1,130]{0,2,1:T(8,128)(2,1)S(1)}, bf16[64,1,130]{0,2,1:T(8,128)(2,1)S(1)}, u32[]{:S(2)}, u32[]{:S(2)}) collective-permute-start(bf16[64,1,130]{0,2,1:T(8,128)(2,1)S(1)} %get-tuple-element.22), channel_id=1, source_target_pairs={{1,0},{2,1},{3,2},{4,3},{5,4},{6,5},{7,6},{9,8},{10,9},{11,10},{12... | collective-permute-start | bytes 49928 | tf_op jit(solution)/shard_map/ppermute | solution.py:516
  97.7 4.5 %collective-permute-start.7 = (bf16[64,1,130]{0,2,1:T(8,128)(2,1)S(1)}, bf16[64,1,130]{0,2,1:T(8,128)(2,1)S(1)}, u32[]{:S(2)}, u32[]{:S(2)}) collective-permute-start(bf16[64,1,130]{0,2,1:T(8,128)(2,1)S(1)} %get-tuple-element.23), channel_id=1, source_target_pairs={{0,1},{1,2},{2,3},{3,4},{4,5},{5,6},{6,7},{8,9},{9,10},{10,11},{11... | collective-permute-start | bytes 49928 | tf_op jit(solution)/shard_map/ppermute | solution.py:515
  102.8 1.1 collective-permute-done.7
  103.9 0.8 pad_maximum_fusion.3
  107.4 0.7 copy.30
  110.1 0.9 slice.176
  (69 shorter events, 8.3 us)
Async XLA Ops:
  2.8 18.9 %all-to-all-start = ((s32[8,1,256]{2,1,0:T(1,128)}), s32[8,1,256]{2,1,0:T(1,128)S(1)}, u32[]{:S(2)}, u32[]{:S(2)}) async-start(s32[8,1,256]{2,1,0:T(1,128)} %reshape_add_fusion.target_ref), calls=%async_computation | async-start | bytes 16384 | tf_op jit(solution)/shard_map/all_to_all | solution.py:466
  10.1 6.2 %copy-start.4 = (s32[1,1,8,256]{3,2,1,0:T(8,128)S(1)}, s32[1,1,8,256]{3,2,1,0:T(8,128)}, u32[]{:S(2)}) copy-start(s32[1,1,8,256]{3,2,1,0:T(8,128)} %param.10) | copy-start | bytes 24580
  10.1 6.2 %copy-start.3 = (bf16[3,3,64,64]{3,2,1,0:T(8,128)(2,1)S(1)}, bf16[3,3,64,64]{3,2,1,0:T(8,128)(2,1)}, u32[]{:S(2)}) copy-start(bf16[3,3,64,64]{3,2,1,0:T(8,128)(2,1)} %param.16) | copy-start | bytes 221188
  11.4 6.7 %collective-permute-start = (bf16[128,128]{1,0:T(8,128)(2,1)S(1)}, bf16[128,128]{1,0:T(8,128)(2,1)S(1)}, u32[]{:S(2)}, u32[]{:S(2)}) collective-permute-start(bf16[128,128]{1,0:T(8,128)(2,1)S(1)} %get-tuple-element.13), channel_id=1, source_target_pairs={{0,1},{1,2},{2,3},{3,4},{4,5},{5,6},{6,7},{7,0},{8,9},{9,10},{10,1... | collective-permute-start | bytes 98312 | tf_op jit(solution)/shard_map/ppermute | solution.py:463
  13.5 4.6 %collective-permute-start.1 = (bf16[128,128]{1,0:T(8,128)(2,1)S(1)}, bf16[128,128]{1,0:T(8,128)(2,1)S(1)}, u32[]{:S(2)}, u32[]{:S(2)}) collective-permute-start(bf16[128,128]{1,0:T(8,128)(2,1)S(1)} %get-tuple-element.15), channel_id=1, source_target_pairs={{1,0},{2,1},{3,2},{4,3},{5,4},{6,5},{7,6},{0,7},{9,8},{10,9},{11,1... | collective-permute-start | bytes 98312 | tf_op jit(solution)/shard_map/ppermute | solution.py:464
  16.3 5.4 %copy-start = (bf16[3,3,128,128]{3,2,1,0:T(8,128)(2,1)S(1)}, bf16[3,3,128,128]{3,2,1,0:T(8,128)(2,1)}, u32[]{:S(2)}) copy-start(bf16[3,3,128,128]{3,2,1,0:T(8,128)(2,1)} %param.14) | copy-start | bytes 884740
  16.3 5.4 %copy-start.1 = (bf16[128,64]{0,1:T(8,128)(2,1)S(1)}, bf16[128,64]{0,1:T(8,128)(2,1)}, u32[]{:S(2)}) copy-start(bf16[128,64]{0,1:T(8,128)(2,1)} %param.15) | copy-start | bytes 49156
  16.3 5.4 %copy-start.2 = (s32[1,1,8]{2,1,0:T(1,128)S(1)}, s32[1,1,8]{2,1,0:T(1,128)}, u32[]{:S(2)}) copy-start(s32[1,1,8]{2,1,0:T(1,128)} %param.13) | copy-start | bytes 100
  18.1 15.3 %collective-permute-start.3 = (bf16[18,64,128]{2,1,0:T(8,128)(2,1)S(1)}, bf16[18,64,128]{2,1,0:T(8,128)(2,1)S(1)}, u32[]{:S(2)}, u32[]{:S(2)}) collective-permute-start(bf16[18,64,128]{2,1,0:T(8,128)(2,1)S(1)} %get-tuple-element.46), channel_id=1, source_target_pairs={{0,16},{8,24},{16,0},{24,8},{1,17},{9,25},{17,1},{25,9},{2,18},{10... | collective-permute-start | bytes 884744 | tf_op jit(solution)/shard_map/ppermute | solution.py:428
  19.7 13.7 %collective-permute-start.2 = (bf16[18,64,128]{2,1,0:T(8,128)(2,1)S(1)}, bf16[18,64,128]{2,1,0:T(8,128)(2,1)S(1)}, u32[]{:S(2)}, u32[]{:S(2)}) collective-permute-start(bf16[18,64,128]{2,1,0:T(8,128)(2,1)S(1)} %get-tuple-element.46), channel_id=1, source_target_pairs={{0,8},{8,16},{16,24},{24,0},{1,9},{9,17},{17,25},{25,1},{2,10},{10... | collective-permute-start | bytes 884744 | tf_op jit(solution)/shard_map/ppermute | solution.py:428
  19.7 13.7 %collective-permute-start.4 = (bf16[18,64,128]{2,1,0:T(8,128)(2,1)S(1)}, bf16[18,64,128]{2,1,0:T(8,128)(2,1)S(1)}, u32[]{:S(2)}, u32[]{:S(2)}) collective-permute-start(bf16[18,64,128]{2,1,0:T(8,128)(2,1)S(1)} %get-tuple-element.46), channel_id=1, source_target_pairs={{0,24},{8,0},{16,8},{24,16},{1,25},{9,1},{17,9},{25,17},{2,26},{10... | collective-permute-start | bytes 884744 | tf_op jit(solution)/shard_map/ppermute | solution.py:428
  63.2 10.3 %collective-permute-start.5 = (bf16[1,8,72,256]{3,2,1,0:T(8,128)(2,1)S(1)}, bf16[1,8,72,256]{3,2,1,0:T(8,128)(2,1)S(1)}, u32[]{:S(2)}, u32[]{:S(2)}) collective-permute-start(bf16[1,8,72,256]{3,2,1,0:T(8,128)(2,1)S(1)} %get-tuple-element.36), channel_id=1, source_target_pairs={{0,16},{8,24},{16,0},{24,8},{1,17},{9,25},{17,1},{25,9},{2,18},{10... | collective-permute-start | bytes 884744 | tf_op jit(solution)/shard_map/ppermute | solution.py:418
  70.9 16.0 %all-to-all-start.2 = ((bf16[32,48,128]{2,1,0:T(8,128)(2,1)}), bf16[32,48,128]{2,1,0:T(8,128)(2,1)S(1)}, u32[]{:S(2)}, u32[]{:S(2)}) async-start(bf16[32,48,128]{2,1,0:T(8,128)(2,1)} %bitcast.48), calls=%async_computation.2 | async-start | bytes 786432 | tf_op jit(solution)/shard_map/all_to_all | solution.py:439
  73.6 16.8 %collective-permute-start.6 = (bf16[2,8,72,256]{3,2,1,0:T(8,128)(2,1)S(1)}, bf16[2,8,72,256]{3,2,1,0:T(8,128)(2,1)S(1)}, u32[]{:S(2)}, u32[]{:S(2)}) collective-permute-start(bf16[2,8,72,256]{3,2,1,0:T(8,128)(2,1)S(1)} %get-tuple-element.34), channel_id=1, source_target_pairs={{0,8},{8,0},{16,24},{24,16},{1,9},{9,1},{17,25},{25,17},{2,10},{10... | collective-permute-start | bytes 1769480 | tf_op jit(solution)/shard_map/ppermute | solution.py:418
  87.8 20.3 %all-to-all-start.3 = ((bf16[32,48,128]{2,1,0:T(8,128)(2,1)}), bf16[32,48,128]{2,1,0:T(8,128)(2,1)S(1)}, u32[]{:S(2)}, u32[]{:S(2)}) async-start(bf16[32,48,128]{2,1,0:T(8,128)(2,1)} %broadcast_in_dim.20), calls=%async_computation.3 | async-start | bytes 786432 | tf_op jit(solution)/shard_map/all_to_all | solution.py:442
  96.4 6.4 %collective-permute-start.8 = (bf16[64,1,130]{0,2,1:T(8,128)(2,1)S(1)}, bf16[64,1,130]{0,2,1:T(8,128)(2,1)S(1)}, u32[]{:S(2)}, u32[]{:S(2)}) collective-permute-start(bf16[64,1,130]{0,2,1:T(8,128)(2,1)S(1)} %get-tuple-element.22), channel_id=1, source_target_pairs={{1,0},{2,1},{3,2},{4,3},{5,4},{6,5},{7,6},{9,8},{10,9},{11,10},{12... | collective-permute-start | bytes 49928 | tf_op jit(solution)/shard_map/ppermute | solution.py:516
  97.7 6.2 %collective-permute-start.7 = (bf16[64,1,130]{0,2,1:T(8,128)(2,1)S(1)}, bf16[64,1,130]{0,2,1:T(8,128)(2,1)S(1)}, u32[]{:S(2)}, u32[]{:S(2)}) collective-permute-start(bf16[64,1,130]{0,2,1:T(8,128)(2,1)S(1)} %get-tuple-element.23), channel_id=1, source_target_pairs={{0,1},{1,2},{2,3},{3,4},{4,5},{5,6},{6,7},{8,9},{9,10},{10,11},{11... | collective-permute-start | bytes 49928 | tf_op jit(solution)/shard_map/ppermute | solution.py:515

commit v3 on v2

--- a/solution.py
+++ b/solution.py
@@ -11,7 +11,7 @@
 TILE = 16
 CELLS = TILE * TILE
 EDGE = 8
-WIDE = 8
+WIDE = 4
 IDX_ROWS = 8
 BF16 = jnp.bfloat16
 F32 = jnp.float32
@@ -23,17 +23,36 @@
     return lax.dot_general(a, b, dims, preferred_element_type=F32)
 
 
+def gather_slot(base_ref, table, picked, first, slot, slots, lines, pitch):
+    base = base_ref[first + slot]
+    for line in range(lines):
+        at = (line * slots + slot) * WIDE
+        if not isinstance(at, int):
+            at = pl.multiple_of(at, WIDE)
+        picked[pl.ds(at, WIDE), :] = table[pl.ds(base + line * pitch, WIDE), :]
+
+
 def gather_windows(base_ref, table, picked, first, slots, lines, pitch):
     def body(step, _):
         for k in range(8):
-            slot = step * 8 + k
-            base = base_ref[first + slot]
-            for line in range(lines):
-                at = pl.multiple_of((line * slots + slot) * WIDE, WIDE)
-                picked[pl.ds(at, WIDE), :] = table[pl.ds(base + line * pitch, WIDE), :]
+            gather_slot(base_ref, table, picked, first, step * 8 + k, slots, lines, pitch)
         return 0
 
     lax.fori_loop(0, slots // 8, body, 0)
+
+
+def in_turn(step, lists, slots, base_ref, table, buffers, lines, pitch, compute):
+    now = step - 1
+    first = jnp.minimum(step, lists - 1) * slots
+    for parity in range(2):
+
+        @pl.when(jnp.logical_and(step > 0, lax.rem(now, 2) == parity))
+        def _():
+            for slot in range(slots):
+                gather_slot(
+                    base_ref, table, buffers[1 - parity], first, slot, slots, lines, pitch
+                )
+            compute(now, buffers[parity])
 
 
 def plane(picked, slots, line, tap):
@@ -91,7 +110,7 @@
 
 def forward_kernel(
     base_ref, count_ref, image_ref, left_ref, right_ref, w_ref, wp_ref, target_ref,
-    patch_ref, slope_ref, rows_ref, send_ref, raw, table, ends, picked, sem,
+    patch_ref, slope_ref, rows_ref, send_ref, raw, table, ends, even, odd, sem,
 ):
     step = pl.program_id(0)
     beams, columns, channels = image_ref.shape
@@ -130,19 +149,21 @@
                 return 0
 
             lax.fori_loop(0, 8, widen, 0)
-
-    @pl.when(step > 0)
-    def _():
-        band = step - 1
-        gather_windows(base_ref, table, picked, band * slots, slots, 3, pitch)
-        parts = [plane(picked, slots, line, tap) for line in range(3) for tap in range(3)]
-        patch = jnp.concatenate([p.astype(BF16) for p in parts], axis=1)
-        patch_ref[...] = patch
-        preact = dot(patch, w_ref[...])
+        gather_windows(base_ref, table, even, 0, slots, 3, pitch)
+
+    def compute(band, picked):
+        preact = None
+        for k in range(0, 9, 2):
+            parts = [plane(picked, slots, j // 3, j % 3) for j in range(k, min(k + 2, 9))]
+            part = jnp.concatenate([p.astype(BF16) for p in parts], axis=1)
+            columns = slice(k * channels, k * channels + part.shape[1])
+            patch_ref[:, columns] = part
+            term = dot(part, w_ref[columns, :])
+            preact = term if preact is None else preact + term
         sigmoid = jax.nn.sigmoid(preact)
         slope_ref[...] = sigmoid * (1.0 + preact * (1.0 - sigmoid))
         live = lax.broadcasted_iota(jnp.int32, preact.shape, 0) < count_ref[band]
-        rows = jnp.where(live, parts[4] + preact * sigmoid, 0.0).astype(BF16)
+        rows = jnp.where(live, plane(picked, slots, 1, 1) + preact * sigmoid, 0.0).astype(BF16)
         rows_ref[...] = rows
         sent = dot(wp_ref[...], rows, NT)
         target = jnp.broadcast_to(target_ref[0], (IDX_ROWS, slots))
@@ -150,6 +171,9 @@
         tile = lax.div(target, CELLS)
         whole = jnp.where(row == 0, target - tile * CELLS, jnp.where(row == 1, tile, 0))
         send_ref[0, 0] = jnp.concatenate([sent, whole.astype(F32)], axis=0).astype(BF16)
+
+    lists = pl.num_programs(0) - 1
+    in_turn(step, lists, slots, base_ref, table, (even, odd), 3, pitch, compute)
 
 
 def forward(base, count, image, left, right, w_flat, wp_t, targets):
@@ -193,6 +217,7 @@
                 pltpu.VMEM(((beams + 2) * pitch, channels), F32),
                 pltpu.VMEM((2, beams, channels), F32),
                 pltpu.VMEM((3 * slots * WIDE, channels), F32),
+                pltpu.VMEM((3 * slots * WIDE, channels), F32),
                 pltpu.SemaphoreType.DMA((beams // 8,)),
             ],
         ),
@@ -207,7 +232,7 @@
 
 
 def pick_kernel(
-    base_ref, order_ref, cot_ref, wg_ref, send_ref, window_ref, grad_ref, table, picked
+    base_ref, order_ref, cot_ref, wg_ref, send_ref, window_ref, grad_ref, table, even, odd
 ):
     step = pl.program_id(0)
     groups, lines, head_ch, columns = cot_ref.shape
@@ -230,16 +255,18 @@
             return 0
 
         lax.fori_loop(0, lines - 1, build, 0)
-
-    @pl.when(step > 0)
-    def _():
-        gather_windows(base_ref, table, picked, (step - 1) * slots, slots, 2, pitch)
+        gather_windows(base_ref, table, even, 0, slots, 2, pitch)
+
+    def compute(_, picked):
         parts = [plane(picked, slots, line, tap) for line in range(2) for tap in range(3)]
         window = jnp.concatenate([p.astype(BF16) for p in parts], axis=1)
         window_ref[...] = window
         grad = dot(wg_ref[...], window, NT)
         spare = jnp.zeros((IDX_ROWS, slots), F32)
         grad_ref[0, 0] = jnp.concatenate([grad, spare], axis=0).astype(BF16)
+
+    lists = pl.num_programs(0) - 1
+    in_turn(step, lists, slots, base_ref, table, (even, odd), 2, pitch, compute)
 
 
 def pick(base, order, band_cot, wg, send):
@@ -270,11 +297,12 @@
             scratch_shapes=[
                 pltpu.VMEM(((lines - 1) * pitch, 2 * head_ch), F32),
                 pltpu.VMEM((2 * slots * WIDE, 2 * head_ch), F32),
+                pltpu.VMEM((2 * slots * WIDE, 2 * head_ch), F32),
             ],
         ),
         input_output_aliases={4: 1},
         compiler_params=pltpu.CompilerParams(
-            dimension_semantics=("arbitrary",), vmem_limit_bytes=16 << 20
+            dimension_semantics=("arbitrary",), vmem_limit_bytes=14 << 20
         ),
         cost_estimate=pl.CostEstimate(
             flops=24 * total * head_ch * head_ch, bytes_accessed=12 << 20, transcendentals=0
@@ -354,13 +382,42 @@
             ],
         ),
         compiler_params=pltpu.CompilerParams(
-            dimension_semantics=("arbitrary",), vmem_limit_bytes=12 << 20
+            dimension_semantics=("arbitrary",), vmem_limit_bytes=8 << 20
         ),
         cost_estimate=pl.CostEstimate(
             flops=2 * total * taps * channels, bytes_accessed=10 << 20, transcendentals=0
         ),
         name="backward",
     )(count, mixed, mixed, slope, rows, patch, window, wp_t)
+
+
+def unpack_kernel(sum_ref, range_ref, proj_ref, head_ref):
+    taps = range_ref.shape[0]
+    head_ch = proj_ref.shape[0]
+    range_ref[...] = sum_ref[pl.ds(0, taps), :].astype(F32)
+    proj_ref[...] = sum_ref[pl.ds(taps, head_ch), :].astype(F32)
+    for a in range(3):
+        for b in range(3):
+            block, half = (b, a) if a < 2 else ((3, b) if b < 2 else (4, 1))
+            start = taps + head_ch * (block + 1)
+            part = sum_ref[pl.ds(start, head_ch), :].astype(F32)
+            head_ref[2 - a, 2 - b] = part[:, half * head_ch : (half + 1) * head_ch]
+
+
+def unpack(total, taps, head_ch):
+    vmem = pl.BlockSpec(memory_space=pltpu.VMEM)
+    return pl.pallas_call(
+        unpack_kernel,
+        out_shape=(
+            jax.ShapeDtypeStruct((taps, total.shape[1]), F32),
+            jax.ShapeDtypeStruct((head_ch, total.shape[1]), F32),
+            jax.ShapeDtypeStruct((3, 3, head_ch, head_ch), F32),
+        ),
+        in_specs=[vmem],
+        out_specs=(vmem, vmem, vmem),
+        compiler_params=pltpu.CompilerParams(vmem_limit_bytes=4 << 20),
+        name="unpack",
+    )(total)
 
 
 def place_kernel(tile_ref, rows_ref, out_ref, acc):
@@ -475,6 +532,7 @@
         base, count, image, from_left, from_right, w_range.reshape(-1, channels), wp_t, targets
     )
 
+    targets_in, send = lax.optimization_barrier((targets_in, send))
     band_pitch = sweeps * grid_cols + 2 * EDGE
     cell_in = targets_in % CELLS
     pick_base = (
@@ -498,14 +556,11 @@
     tile_rows = lists[:, head_ch + 1, :: slots // per_list].astype(jnp.int32).reshape(-1)
     ground = place(tile_rows - (sweep * owned - 1), lists, owned + 2, head_ch)
     local = backward(count, mixed, slope, rows, patch, window, wp_t)
-    total = summed(local, ("sweep", "sector")).astype(F32)
+    total = summed(local, ("sweep", "sector"))
     taps = w_range.shape[0] * w_range.shape[1] * channels
-    grad_range = total[:taps].reshape(w_range.shape)
-    grad_proj = total[taps : taps + head_ch].T
-    head_total = total[taps + head_ch :].reshape(5, head_ch, 2, head_ch)
-    last = jnp.stack([head_total[3, :, 0], head_total[3, :, 1], head_total[4, :, 1]])
-    by_a = jnp.stack([head_total[:3, :, 0], head_total[:3, :, 1], last])
-    grad_head = by_a[::-1, ::-1]
+    grad_range, grad_proj, grad_head = unpack(total, taps, head_ch)
+    grad_range = grad_range.reshape(w_range.shape)
+    grad_proj = grad_proj.T
 
     ground = (
         ground.reshape(owned + 2, head_ch, TILE, TILE)

time: 113 us -> 109 us (0.965)
  the two profiles are of different devices: /device:TPU:0 before, /device:TPU:28 now
where the time goes in v3:
time: 109 us; the launch traced here: 108 us
  starting transfers between devices  29.3 us (27%)
  Pallas kernels  29.1 us (27%)
  blocking collectives  21.7 us (20%)
  waiting for transfers between devices  17 us (16%)
  other arithmetic  3.47 us (3%)
  local copies, waits for them, and re-layouts  3.39 us (3%)
  matrix products  2.99 us (3%)
    all_to_all x1, blocking collectives, shards(): lax.all_to_all(send, 'sector', split_axis=0, concat_axis=0, tiled=True)  21.7 us
    all_to_all x1, waiting for transfers between devices, summed(): lax.all_to_all(pieces, axes, split_axis=0, concat_axis=0, tiled=True)  10.5 us
    pallas_call x1, Pallas kernels, forward(): pl.pallas_call(forward_kernel, out_shape=(jax.ShapeDtypeStruct((total, ta...  10.1 us
    pallas_call x1, Pallas kernels, pick(): pl.pallas_call(pick_kernel, out_shape=(jax.ShapeDtypeStruct((total, 12 *...  6.39 us
    pallas_call x1, Pallas kernels, backward(): pl.pallas_call(backward_kernel, out_shape=jax.ShapeDtypeStruct((out_rows,...  6.1 us
    all_to_all x1, starting transfers between devices, shards(): lax.all_to_all(targets, 'sector', split_axis=0, concat_axis=0, tiled=True)  6.03 us
    all_to_all x1, starting transfers between devices, summed(): lax.all_to_all(pieces, axes, split_axis=0, concat_axis=0, tiled=True)  5.75 us
    all_to_all x1, starting transfers between devices, summed(): lax.all_to_all(spread, axes, split_axis=0, concat_axis=0, tiled=True)  5.25 us
  transfers between devices with their start and end apart: 12, of which 4 were waited for; matrix products, arithmetic and copies ran while one was open for 7% of the time, Pallas kernels for 20%

profile of v3, /device:TPU:28, one launch (start us, length us, event | category | flops | bytes accessed | tf_op | source)
XLA Modules:
  0.0 108.0 jit_solution(3611458169190692166)
XLA Ops:
  0.6 0.7 multiply_bitcast_fusion
  1.5 1.3 %reshape_add_fusion.target_ref = s32[8,1,256]{2,1,0:T(1,128)} fusion(s32[8,1,256]{2,1,0:T(1,128)S(1)} %bitcast.135, s32[1,1,8,256]{3,2,1,0:T(8,128)} %param.11), kind=kLoop, calls=%fused_computation.94 | loop fusion | flops 2048 | bytes 24576 | tf_op jit(solution)/shard_map/add | solution.py:522
  2.8 6.0 %all-to-all-start = ((s32[8,1,256]{2,1,0:T(1,128)}), s32[8,1,256]{2,1,0:T(1,128)S(1)}, u32[]{:S(2)}, u32[]{:S(2)}) async-start(s32[8,1,256]{2,1,0:T(1,128)} %reshape_add_fusion.target_ref), calls=%async_computation | async-start | bytes 16384 | tf_op jit(solution)/shard_map/all_to_all | solution.py:523
  8.8 1.3 %edges.1 = (bf16[128,128]{1,0:T(8,128)(2,1)S(1)}, bf16[128,128]{1,0:T(8,128)(2,1)S(1)}, bf16[16,64,128]{2,1,0:T(8,128)(2,1)S(1)}) custom-call(bf16[64,256,128]{2,1,0:T(8,128)(2,1)} %bitcast.114, bf16[64,16,128]{2,1,0:T(8,128)(2,1)} %cot_ref.1), custom_call_target="tpu_custom_call" | custom-call | tf_op jit(solution)/shard_map/edges/pallas_call | solution.py:95
  10.1 1.5 %collective-permute-start = (bf16[128,128]{1,0:T(8,128)(2,1)S(1)}, bf16[128,128]{1,0:T(8,128)(2,1)S(1)}, u32[]{:S(2)}, u32[]{:S(2)}) collective-permute-start(bf16[128,128]{1,0:T(8,128)(2,1)S(1)} %get-tuple-element.18), channel_id=1, source_target_pairs={{0,1},{1,2},{2,3},{3,4},{4,5},{5,6},{6,7},{7,0},{8,9},{9,10},{10,1... | collective-permute-start | bytes 98312 | tf_op jit(solution)/shard_map/ppermute | solution.py:520
  11.6 1.5 %collective-permute-start.1 = (bf16[128,128]{1,0:T(8,128)(2,1)S(1)}, bf16[128,128]{1,0:T(8,128)(2,1)S(1)}, u32[]{:S(2)}, u32[]{:S(2)}) collective-permute-start(bf16[128,128]{1,0:T(8,128)(2,1)S(1)} %get-tuple-element.19), channel_id=1, source_target_pairs={{1,0},{2,1},{3,2},{4,3},{5,4},{6,5},{7,6},{0,7},{9,8},{10,9},{11,1... | collective-permute-start | bytes 98312 | tf_op jit(solution)/shard_map/ppermute | solution.py:521
  13.3 1.6 %collective-permute-done.left_ref = bf16[128,128]{1,0:T(8,128)(2,1)S(1)} collective-permute-done((bf16[128,128]{1,0:T(8,128)(2,1)S(1)}, bf16[128,128]{1,0:T(8,128)(2,1)S(1)}, u32[]{:S(2)}, u32[]{:S(2)}) %collective-permute-start) | collective-permute-done | bytes 32800 | tf_op jit(solution)/shard_map/ppermute | solution.py:520
  16.2 1.7 %collective-permute-start.4 = (bf16[18,64,128]{2,1,0:T(8,128)(2,1)S(1)}, bf16[18,64,128]{2,1,0:T(8,128)(2,1)S(1)}, u32[]{:S(2)}, u32[]{:S(2)}) collective-permute-start(bf16[18,64,128]{2,1,0:T(8,128)(2,1)S(1)} %get-tuple-element.51), channel_id=1, source_target_pairs={{0,24},{8,0},{16,8},{24,16},{1,25},{9,1},{17,9},{25,17},{2,26},{10... | collective-permute-start | bytes 884744 | tf_op jit(solution)/shard_map/ppermute | solution.py:485
  18.2 10.1 %forward.1 = (bf16[2048,1152]{1,0:T(8,128)(2,1)S(1)}, f32[2048,128]{1,0:T(8,128)S(1)}, bf16[2048,128]{1,0:T(8,128)(2,1)S(1)}, bf16[8,2,72,256]{3,2,1,0:T(8,128)(2,1)S(1)}) custom-call(s32[2048]{0:T(1024)S(1)} %fusion.31.base_ref, s32[8]{0:T(128)S(1)} %bitcast.112, bf16[64,256,128]{2,1,0:T(8,128)(2,1)} %bitcast.115, ...), custom_call_target="tpu_custom_call" | custom-call | flops 603979776 | bytes 25165824 | tf_op jit(solution)/shard_map/forward/pallas_call | solution.py:190
  28.5 6.4 %pick.1 = (bf16[2048,768]{1,0:T(8,128)(2,1)S(1)}, bf16[8,2,72,256]{3,2,1,0:T(8,128)(2,1)S(1)}) custom-call(s32[2048]{0:T(1024)S(1)} %bitcast.111, s32[4]{0:T(128)S(1)} %and_select_fusion.order_ref, bf16[4,18,64,128]{3,2,1,0:T(8,128)(2,1)S(1)} %pad_maximum_fusion.cot_ref, bf16[64,768]{1,0:T(8,128)(2,1)S(1)} %reshape.104.wg_ref, ...), custom_call_target="tpu_custom_call", output_to_operand_aliasing={{1}: (4, {})} | custom-call | flops 201326592 | bytes 12582912 | tf_op jit(solution)/shard_map/pick/pallas_call | solution.py:279
  34.9 21.7 %all_to_all.24.back_ref.sent_ref = bf16[8,2,72,256]{3,2,1,0:T(8,128)(2,1)S(1)} all-to-all(bf16[8,2,72,256]{3,2,1,0:T(8,128)(2,1)S(1)} %get-tuple-element.24), channel_id=1, replica_groups=mesh['sweep'=4,'sector'=8] {'sector'}, dimensions={0} | all-to-all | bytes 1179648 | tf_op jit(solution)/shard_map/all_to_all | solution.py:550
  56.7 0.8 collective-permute-start.5
  57.4 6.1 %backward.1 = bf16[1536,128]{1,0:T(8,128)(2,1)} custom-call(s32[8]{0:T(128)S(1)} %bitcast.113, bf16[8,2,72,256]{3,2,1,0:T(8,128)(2,1)S(1)} %all_to_all.24.back_ref.sent_ref, bf16[8,2,72,256]{3,2,1,0:T(8,128)(2,1)S(1)} %all_to_all.24.back_ref.sent_ref, f32[2048,128]{1,0:T(8,128)S(1)} %get-tuple-element.25.slope_ref, ...), custom_call_target="tpu_custom_call" | custom-call | flops 603979776 | bytes 10485760 | tf_op jit(solution)/shard_map/backward/pallas_call | solution.py:362
  63.5 5.8 %all-to-all-start.2 = ((bf16[32,48,128]{2,1,0:T(8,128)(2,1)}), bf16[32,48,128]{2,1,0:T(8,128)(2,1)S(1)}, u32[]{:S(2)}, u32[]{:S(2)}) async-start(bf16[32,48,128]{2,1,0:T(8,128)(2,1)} %bitcast.47), calls=%async_computation.2 | async-start | bytes 786432 | tf_op jit(solution)/shard_map/all_to_all | solution.py:496
  69.6 10.5 %all-to-all-done.2 = bf16[32,48,128]{2,1,0:T(8,128)(2,1)S(1)} async-done(((bf16[32,48,128]{2,1,0:T(8,128)(2,1)}), bf16[32,48,128]{2,1,0:T(8,128)(2,1)S(1)}, u32[]{:S(2)}, u32[]{:S(2)}) %all-to-all-start.2) | async-done | bytes 393248 | tf_op jit(solution)/shard_map/all_to_all | solution.py:496
  80.1 0.8 broadcast_in_dim.20
  80.9 5.2 %all-to-all-start.3 = ((bf16[32,48,128]{2,1,0:T(8,128)(2,1)}), bf16[32,48,128]{2,1,0:T(8,128)(2,1)S(1)}, u32[]{:S(2)}, u32[]{:S(2)}) async-start(bf16[32,48,128]{2,1,0:T(8,128)(2,1)} %broadcast_in_dim.20), calls=%async_computation.3 | async-start | bytes 786432 | tf_op jit(solution)/shard_map/all_to_all | solution.py:499
  86.9 4.2 %place.1 = bf16[10,64,256]{2,1,0:T(8,128)(2,1)S(1)} custom-call(s32[64]{0:T(128)S(1)} %sub.53.tile_ref, bf16[32,72,256]{2,1,0:T(8,128)(2,1)S(1)} %bitcast.106), custom_call_target="tpu_custom_call" | custom-call | flops 268435456 | bytes 2097152 | tf_op jit(solution)/shard_map/place/pallas_call | solution.py:450
  91.9 4.2 %collective-permute-start.8 = (bf16[64,1,130]{0,2,1:T(8,128)(2,1)S(1)}, bf16[64,1,130]{0,2,1:T(8,128)(2,1)S(1)}, u32[]{:S(2)}, u32[]{:S(2)}) collective-permute-start(bf16[64,1,130]{0,2,1:T(8,128)(2,1)S(1)} %get-tuple-element.32), channel_id=1, source_target_pairs={{1,0},{2,1},{3,2},{4,3},{5,4},{6,5},{7,6},{9,8},{10,9},{11,10},{12... | collective-permute-start | bytes 49928 | tf_op jit(solution)/shard_map/ppermute | solution.py:571
  96.1 1.9 %collective-permute-start.7 = (bf16[64,1,130]{0,2,1:T(8,128)(2,1)S(1)}, bf16[64,1,130]{0,2,1:T(8,128)(2,1)S(1)}, u32[]{:S(2)}, u32[]{:S(2)}) collective-permute-start(bf16[64,1,130]{0,2,1:T(8,128)(2,1)S(1)} %get-tuple-element.33), channel_id=1, source_target_pairs={{0,1},{1,2},{2,3},{3,4},{4,5},{5,6},{6,7},{8,9},{9,10},{10,11},{11... | collective-permute-start | bytes 49928 | tf_op jit(solution)/shard_map/ppermute | solution.py:570
  98.5 4.3 %collective-permute-done.7 = bf16[64,1,130]{0,2,1:T(8,128)(2,1)S(1)} collective-permute-done((bf16[64,1,130]{0,2,1:T(8,128)(2,1)S(1)}, bf16[64,1,130]{0,2,1:T(8,128)(2,1)S(1)}, u32[]{:S(2)}, u32[]{:S(2)}) %collective-permute-start.7) | collective-permute-done | bytes 16672 | tf_op jit(solution)/shard_map/ppermute | solution.py:570
  102.8 0.8 pad_maximum_fusion.3
  106.3 0.7 copy.24
  107.1 1.0 unpack.1
  (62 shorter events, 6.9 us)
Async XLA Ops:
  2.8 15.3 %all-to-all-start = ((s32[8,1,256]{2,1,0:T(1,128)}), s32[8,1,256]{2,1,0:T(1,128)S(1)}, u32[]{:S(2)}, u32[]{:S(2)}) async-start(s32[8,1,256]{2,1,0:T(1,128)} %reshape_add_fusion.target_ref), calls=%async_computation | async-start | bytes 16384 | tf_op jit(solution)/shard_map/all_to_all | solution.py:523
  8.8 4.3 %copy-start.4 = (s32[1,1,8,256]{3,2,1,0:T(8,128)S(1)}, s32[1,1,8,256]{3,2,1,0:T(8,128)}, u32[]{:S(2)}) copy-start(s32[1,1,8,256]{3,2,1,0:T(8,128)} %param.10) | copy-start | bytes 24580
  8.8 4.3 %copy-start.3 = (bf16[3,3,64,64]{3,2,1,0:T(8,128)(2,1)S(1)}, bf16[3,3,64,64]{3,2,1,0:T(8,128)(2,1)}, u32[]{:S(2)}) copy-start(bf16[3,3,64,64]{3,2,1,0:T(8,128)(2,1)} %param.16) | copy-start | bytes 221188
  10.1 4.9 %collective-permute-start = (bf16[128,128]{1,0:T(8,128)(2,1)S(1)}, bf16[128,128]{1,0:T(8,128)(2,1)S(1)}, u32[]{:S(2)}, u32[]{:S(2)}) collective-permute-start(bf16[128,128]{1,0:T(8,128)(2,1)S(1)} %get-tuple-element.18), channel_id=1, source_target_pairs={{0,1},{1,2},{2,3},{3,4},{4,5},{5,6},{6,7},{7,0},{8,9},{9,10},{10,1... | collective-permute-start | bytes 98312 | tf_op jit(solution)/shard_map/ppermute | solution.py:520
  11.6 3.9 %collective-permute-start.1 = (bf16[128,128]{1,0:T(8,128)(2,1)S(1)}, bf16[128,128]{1,0:T(8,128)(2,1)S(1)}, u32[]{:S(2)}, u32[]{:S(2)}) collective-permute-start(bf16[128,128]{1,0:T(8,128)(2,1)S(1)} %get-tuple-element.19), channel_id=1, source_target_pairs={{1,0},{2,1},{3,2},{4,3},{5,4},{6,5},{7,6},{0,7},{9,8},{10,9},{11,1... | collective-permute-start | bytes 98312 | tf_op jit(solution)/shard_map/ppermute | solution.py:521
  13.1 5.0 %copy-start = (bf16[3,3,128,128]{3,2,1,0:T(8,128)(2,1)S(1)}, bf16[3,3,128,128]{3,2,1,0:T(8,128)(2,1)}, u32[]{:S(2)}) copy-start(bf16[3,3,128,128]{3,2,1,0:T(8,128)(2,1)} %param.14) | copy-start | bytes 884740
  13.2 5.0 %copy-start.1 = (bf16[128,64]{0,1:T(8,128)(2,1)S(1)}, bf16[128,64]{0,1:T(8,128)(2,1)}, u32[]{:S(2)}) copy-start(bf16[128,64]{0,1:T(8,128)(2,1)} %param.15) | copy-start | bytes 49156
  13.2 5.0 %copy-start.2 = (s32[1,1,8]{2,1,0:T(1,128)S(1)}, s32[1,1,8]{2,1,0:T(1,128)}, u32[]{:S(2)}) copy-start(s32[1,1,8]{2,1,0:T(1,128)} %param.13) | copy-start | bytes 100
  15.6 12.7 %collective-permute-start.3 = (bf16[18,64,128]{2,1,0:T(8,128)(2,1)S(1)}, bf16[18,64,128]{2,1,0:T(8,128)(2,1)S(1)}, u32[]{:S(2)}, u32[]{:S(2)}) collective-permute-start(bf16[18,64,128]{2,1,0:T(8,128)(2,1)S(1)} %get-tuple-element.51), channel_id=1, source_target_pairs={{0,16},{8,24},{16,0},{24,8},{1,17},{9,25},{17,1},{25,9},{2,18},{10... | collective-permute-start | bytes 884744 | tf_op jit(solution)/shard_map/ppermute | solution.py:485
  16.2 12.2 %collective-permute-start.2 = (bf16[18,64,128]{2,1,0:T(8,128)(2,1)S(1)}, bf16[18,64,128]{2,1,0:T(8,128)(2,1)S(1)}, u32[]{:S(2)}, u32[]{:S(2)}) collective-permute-start(bf16[18,64,128]{2,1,0:T(8,128)(2,1)S(1)} %get-tuple-element.51), channel_id=1, source_target_pairs={{0,8},{8,16},{16,24},{24,0},{1,9},{9,17},{17,25},{25,1},{2,10},{10... | collective-permute-start | bytes 884744 | tf_op jit(solution)/shard_map/ppermute | solution.py:485
  16.2 12.2 %collective-permute-start.4 = (bf16[18,64,128]{2,1,0:T(8,128)(2,1)S(1)}, bf16[18,64,128]{2,1,0:T(8,128)(2,1)S(1)}, u32[]{:S(2)}, u32[]{:S(2)}) collective-permute-start(bf16[18,64,128]{2,1,0:T(8,128)(2,1)S(1)} %get-tuple-element.51), channel_id=1, source_target_pairs={{0,24},{8,0},{16,8},{24,16},{1,25},{9,1},{17,9},{25,17},{2,26},{10... | collective-permute-start | bytes 884744 | tf_op jit(solution)/shard_map/ppermute | solution.py:485
  56.7 12.6 %collective-permute-start.5 = (bf16[1,8,72,256]{3,2,1,0:T(8,128)(2,1)S(1)}, bf16[1,8,72,256]{3,2,1,0:T(8,128)(2,1)S(1)}, u32[]{:S(2)}, u32[]{:S(2)}) collective-permute-start(bf16[1,8,72,256]{3,2,1,0:T(8,128)(2,1)S(1)} %get-tuple-element.46), channel_id=1, source_target_pairs={{0,16},{8,24},{16,0},{24,8},{1,17},{9,25},{17,1},{25,9},{2,18},{10... | collective-permute-start | bytes 884744 | tf_op jit(solution)/shard_map/ppermute | solution.py:475
  63.5 16.5 %all-to-all-start.2 = ((bf16[32,48,128]{2,1,0:T(8,128)(2,1)}), bf16[32,48,128]{2,1,0:T(8,128)(2,1)S(1)}, u32[]{:S(2)}, u32[]{:S(2)}) async-start(bf16[32,48,128]{2,1,0:T(8,128)(2,1)} %bitcast.47), calls=%async_computation.2 | async-start | bytes 786432 | tf_op jit(solution)/shard_map/all_to_all | solution.py:496
  69.4 16.8 %collective-permute-start.6 = (bf16[2,8,72,256]{3,2,1,0:T(8,128)(2,1)S(1)}, bf16[2,8,72,256]{3,2,1,0:T(8,128)(2,1)S(1)}, u32[]{:S(2)}, u32[]{:S(2)}) collective-permute-start(bf16[2,8,72,256]{3,2,1,0:T(8,128)(2,1)S(1)} %get-tuple-element.44), channel_id=1, source_target_pairs={{0,8},{8,0},{16,24},{24,16},{1,9},{9,1},{17,25},{25,17},{2,10},{10... | collective-permute-start | bytes 1769480 | tf_op jit(solution)/shard_map/ppermute | solution.py:475
  80.9 26.1 %all-to-all-start.3 = ((bf16[32,48,128]{2,1,0:T(8,128)(2,1)}), bf16[32,48,128]{2,1,0:T(8,128)(2,1)S(1)}, u32[]{:S(2)}, u32[]{:S(2)}) async-start(bf16[32,48,128]{2,1,0:T(8,128)(2,1)} %broadcast_in_dim.20), calls=%async_computation.3 | async-start | bytes 786432 | tf_op jit(solution)/shard_map/all_to_all | solution.py:499
  91.9 6.6 %collective-permute-start.8 = (bf16[64,1,130]{0,2,1:T(8,128)(2,1)S(1)}, bf16[64,1,130]{0,2,1:T(8,128)(2,1)S(1)}, u32[]{:S(2)}, u32[]{:S(2)}) collective-permute-start(bf16[64,1,130]{0,2,1:T(8,128)(2,1)S(1)} %get-tuple-element.32), channel_id=1, source_target_pairs={{1,0},{2,1},{3,2},{4,3},{5,4},{6,5},{7,6},{9,8},{10,9},{11,10},{12... | collective-permute-start | bytes 49928 | tf_op jit(solution)/shard_map/ppermute | solution.py:571
  96.1 6.7 %collective-permute-start.7 = (bf16[64,1,130]{0,2,1:T(8,128)(2,1)S(1)}, bf16[64,1,130]{0,2,1:T(8,128)(2,1)S(1)}, u32[]{:S(2)}, u32[]{:S(2)}) collective-permute-start(bf16[64,1,130]{0,2,1:T(8,128)(2,1)S(1)} %get-tuple-element.33), channel_id=1, source_target_pairs={{0,1},{1,2},{2,3},{3,4},{4,5},{5,6},{6,7},{8,9},{9,10},{10,11},{11... | collective-permute-start | bytes 49928 | tf_op jit(solution)/shard_map/ppermute | solution.py:570

commit v4 on v3

--- a/solution.py
+++ b/solution.py
@@ -13,6 +13,8 @@
 EDGE = 8
 WIDE = 4
 IDX_ROWS = 8
+SWEEP = ("pair", "core")
+GROUP = 4
 BF16 = jnp.bfloat16
 F32 = jnp.float32
 NT = (((1,), (1,)), ((), ()))
@@ -109,7 +111,7 @@
 
 
 def forward_kernel(
-    base_ref, count_ref, image_ref, left_ref, right_ref, w_ref, wp_ref, target_ref,
+    base_ref, count_ref, image_ref, left_ref, right_ref, w_ref, wp_ref,
     patch_ref, slope_ref, rows_ref, send_ref, raw, table, ends, even, odd, sem,
 ):
     step = pl.program_id(0)
@@ -165,25 +167,19 @@
         live = lax.broadcasted_iota(jnp.int32, preact.shape, 0) < count_ref[band]
         rows = jnp.where(live, plane(picked, slots, 1, 1) + preact * sigmoid, 0.0).astype(BF16)
         rows_ref[...] = rows
-        sent = dot(wp_ref[...], rows, NT)
-        target = jnp.broadcast_to(target_ref[0], (IDX_ROWS, slots))
-        row = lax.broadcasted_iota(jnp.int32, target.shape, 0)
-        tile = lax.div(target, CELLS)
-        whole = jnp.where(row == 0, target - tile * CELLS, jnp.where(row == 1, tile, 0))
-        send_ref[0, 0] = jnp.concatenate([sent, whole.astype(F32)], axis=0).astype(BF16)
+        send_ref[0, 0] = dot(wp_ref[...], rows, NT).astype(BF16)
 
     lists = pl.num_programs(0) - 1
     in_turn(step, lists, slots, base_ref, table, (even, odd), 3, pitch, compute)
 
 
-def forward(base, count, image, left, right, w_flat, wp_t, targets):
+def forward(base, count, image, left, right, w_flat, wp_t):
     beams, columns, channels = image.shape
     bands, slots = base.shape
     head_ch = wp_t.shape[0]
     pitch = columns + 2 * EDGE
     taps = w_flat.shape[0]
     late = lambda i, *_: (jnp.maximum(i - 1, 0), 0)
-    late3 = lambda i, *_: (jnp.maximum(i - 1, 0), 0, 0)
     late4 = lambda i, *_: (jnp.maximum(i - 1, 0), 0, 0, 0)
     whole = lambda i, *_: (0, 0)
     total = bands * slots
@@ -193,7 +189,7 @@
             jax.ShapeDtypeStruct((total, taps), BF16),
             jax.ShapeDtypeStruct((total, channels), F32),
             jax.ShapeDtypeStruct((total, channels), BF16),
-            jax.ShapeDtypeStruct((bands, 2, head_ch + IDX_ROWS, slots), BF16),
+            jax.ShapeDtypeStruct((bands, 2, head_ch, slots), BF16),
         ),
         grid_spec=pltpu.PrefetchScalarGridSpec(
             num_scalar_prefetch=2,
@@ -204,13 +200,12 @@
                 pl.BlockSpec(right.shape, whole),
                 pl.BlockSpec(w_flat.shape, whole),
                 pl.BlockSpec(wp_t.shape, whole),
-                pl.BlockSpec((1, 1, slots), late3),
             ],
             out_specs=[
                 pl.BlockSpec((slots, taps), late),
                 pl.BlockSpec((slots, channels), late),
                 pl.BlockSpec((slots, channels), late),
-                pl.BlockSpec((1, 1, head_ch + IDX_ROWS, slots), late4),
+                pl.BlockSpec((1, 1, head_ch, slots), late4),
             ],
             scratch_shapes=[
                 pltpu.VMEM((beams, columns, channels), BF16),
@@ -228,7 +223,7 @@
             flops=2 * total * taps * channels, bytes_accessed=24 << 20, transcendentals=0
         ),
         name="forward",
-    )(base.reshape(-1), count, image, left, right, w_flat, wp_t, targets[:, None])
+    )(base.reshape(-1), count, image, left, right, w_flat, wp_t)
 
 
 def pick_kernel(
@@ -261,9 +256,7 @@
         parts = [plane(picked, slots, line, tap) for line in range(2) for tap in range(3)]
         window = jnp.concatenate([p.astype(BF16) for p in parts], axis=1)
         window_ref[...] = window
-        grad = dot(wg_ref[...], window, NT)
-        spare = jnp.zeros((IDX_ROWS, slots), F32)
-        grad_ref[0, 0] = jnp.concatenate([grad, spare], axis=0).astype(BF16)
+        grad_ref[0, 0] = dot(wg_ref[...], window, NT).astype(BF16)
 
     lists = pl.num_programs(0) - 1
     in_turn(step, lists, slots, base_ref, table, (even, odd), 2, pitch, compute)
@@ -318,6 +311,7 @@
     step = pl.program_id(0)
     head_ch = wp_ref.shape[0]
     channels = rows_ref.shape[1]
+    group = back_ref.shape[0]
 
     @pl.when(step == 0)
     def _():
@@ -325,14 +319,18 @@
         proj_acc[...] = jnp.zeros_like(proj_acc)
         head_acc[...] = jnp.zeros_like(head_acc)
 
-    grads = back_ref[0, 0, :head_ch, :]
-    live = lax.broadcasted_iota(jnp.int32, grads.shape, 1) < count_ref[step]
-    grads = jnp.where(live, grads.astype(F32), 0.0).astype(BF16)
+    lists = []
+    for k in range(group):
+        grads = back_ref[k, 0]
+        live = lax.broadcasted_iota(jnp.int32, grads.shape, 1) < count_ref[step * group + k]
+        lists.append(jnp.where(live, grads.astype(F32), 0.0).astype(BF16))
+    grads = jnp.concatenate(lists, axis=1)
+    sent = jnp.concatenate([sent_ref[k, 0] for k in range(group)], axis=1)
     hidden_grad = dot(grads, wp_ref[...], TN)
     preact_grad = (hidden_grad * slope_ref[...]).T.astype(BF16)
     range_acc[...] += dot(preact_grad, patch_ref[...])
     proj_acc[...] += dot(grads, rows_ref[...])
-    head_acc[...] += dot(sent_ref[0, 0, :head_ch, :], window_ref[...])
+    head_acc[...] += dot(sent, window_ref[...])
 
     @pl.when(step == pl.num_programs(0) - 1)
     def _():
@@ -359,19 +357,20 @@
     out_rows = taps + 6 * head_ch
     each = lambda i, *_: (i, 0)
     total = bands * slots
+    group = GROUP if bands % GROUP == 0 else 1
     return pl.pallas_call(
         backward_kernel,
         out_shape=jax.ShapeDtypeStruct((out_rows, channels), BF16),
         grid_spec=pltpu.PrefetchScalarGridSpec(
             num_scalar_prefetch=1,
-            grid=(bands,),
+            grid=(bands // group,),
             in_specs=[
-                pl.BlockSpec((1, 1, depth, slots), lambda i, *_: (i, 1, 0, 0)),
-                pl.BlockSpec((1, 1, depth, slots), lambda i, *_: (i, 0, 0, 0)),
-                pl.BlockSpec((slots, channels), each),
-                pl.BlockSpec((slots, channels), each),
-                pl.BlockSpec((slots, taps), each),
-                pl.BlockSpec((slots, window.shape[1]), each),
+                pl.BlockSpec((group, 1, depth, slots), lambda i, *_: (i, 1, 0, 0)),
+                pl.BlockSpec((group, 1, depth, slots), lambda i, *_: (i, 0, 0, 0)),
+                pl.BlockSpec((group * slots, channels), each),
+                pl.BlockSpec((group * slots, channels), each),
+                pl.BlockSpec((group * slots, taps), each),
+                pl.BlockSpec((group * slots, window.shape[1]), each),
                 pl.BlockSpec(wp_t.shape, lambda i, *_: (0, 0)),
             ],
             out_specs=pl.BlockSpec((out_rows, channels), lambda i, *_: (0, 0)),
@@ -382,7 +381,7 @@
             ],
         ),
         compiler_params=pltpu.CompilerParams(
-            dimension_semantics=("arbitrary",), vmem_limit_bytes=8 << 20
+            dimension_semantics=("arbitrary",), vmem_limit_bytes=20 << 20
         ),
         cost_estimate=pl.CostEstimate(
             flops=2 * total * taps * channels, bytes_accessed=10 << 20, transcendentals=0
@@ -391,33 +390,50 @@
     )(count, mixed, mixed, slope, rows, patch, window, wp_t)
 
 
-def unpack_kernel(sum_ref, range_ref, proj_ref, head_ref):
+def unpack_kernel(sectors, *refs):
+    *held, range_ref, proj_ref, head_ref, sums = refs
+    cores = len(held)
+    pieces, height, _ = held[0].shape
     taps = range_ref.shape[0]
     head_ch = proj_ref.shape[0]
-    range_ref[...] = sum_ref[pl.ds(0, taps), :].astype(F32)
-    proj_ref[...] = sum_ref[pl.ds(taps, head_ch), :].astype(F32)
+    me = lax.axis_index("core")
+    for core in range(cores):
+
+        @pl.when(me == core)
+        def _():
+            for k in range(cores):
+                whose = (core - k) % cores
+                for piece in range(pieces):
+                    pair, sector = divmod(piece, sectors)
+                    start = ((pair * cores + whose) * sectors + sector) * height
+                    sums[pl.ds(start, height), :] = held[k][piece].astype(F32)
+
+    range_ref[...] = sums[pl.ds(0, taps), :]
+    proj_ref[...] = sums[pl.ds(taps, head_ch), :]
     for a in range(3):
         for b in range(3):
             block, half = (b, a) if a < 2 else ((3, b) if b < 2 else (4, 1))
             start = taps + head_ch * (block + 1)
-            part = sum_ref[pl.ds(start, head_ch), :].astype(F32)
+            part = sums[pl.ds(start, head_ch), :]
             head_ref[2 - a, 2 - b] = part[:, half * head_ch : (half + 1) * head_ch]
 
 
-def unpack(total, taps, head_ch):
+def unpack(held, taps, head_ch):
     vmem = pl.BlockSpec(memory_space=pltpu.VMEM)
+    pieces, height, channels = held[0].shape
     return pl.pallas_call(
-        unpack_kernel,
+        functools.partial(unpack_kernel, lax.axis_size("sector")),
         out_shape=(
-            jax.ShapeDtypeStruct((taps, total.shape[1]), F32),
-            jax.ShapeDtypeStruct((head_ch, total.shape[1]), F32),
+            jax.ShapeDtypeStruct((taps, channels), F32),
+            jax.ShapeDtypeStruct((head_ch, channels), F32),
             jax.ShapeDtypeStruct((3, 3, head_ch, head_ch), F32),
         ),
-        in_specs=[vmem],
+        in_specs=[vmem] * len(held),
         out_specs=(vmem, vmem, vmem),
-        compiler_params=pltpu.CompilerParams(vmem_limit_bytes=4 << 20),
+        scratch_shapes=[pltpu.VMEM((len(held) * pieces * height, channels), F32)],
+        compiler_params=pltpu.CompilerParams(vmem_limit_bytes=6 << 20),
         name="unpack",
-    )(total)
+    )(*held)
 
 
 def place_kernel(tile_ref, rows_ref, out_ref, acc):
@@ -481,23 +497,29 @@
 def exchanged(block, axis):
     count = lax.axis_size(axis)
     places = jnp.arange(count, dtype=jnp.int32)
-    steps = [
-        lax.ppermute(block, axis, [(i, (i + k) % count) for i in range(count)])
-        for k in range(1, count)
-    ]
+    steps = []
+    for k in range(1, count):
+        ring = [(i, (i + k) % count) for i in range(count)]
+        steps.append(lax.ppermute(block, axis, ring))
     return jnp.stack([block] + steps), (lax.axis_index(axis) - places) % count
 
 
-def summed(rows, axes):
-    count = 1
-    for axis in axes:
-        count *= lax.axis_size(axis)
+def summed(rows):
+    axes = SWEEP + ("sector",)
+    count = lax.axis_size(axes)
     pieces = rows.reshape(count, rows.shape[0] // count, rows.shape[1])
     parts = lax.all_to_all(pieces, axes, split_axis=0, concat_axis=0, tiled=True)
     total = parts.astype(F32).sum(axis=0).astype(BF16)
-    spread = jnp.broadcast_to(total[None], pieces.shape)
-    spread = lax.all_to_all(spread, axes, split_axis=0, concat_axis=0, tiled=True)
-    return spread.reshape(rows.shape)
+    cores = lax.axis_size("core")
+    spread = jnp.broadcast_to(total[None], (count // cores,) + total.shape)
+    spread = lax.all_to_all(
+        spread, ("pair", "sector"), split_axis=0, concat_axis=0, tiled=True
+    )
+    held = [spread]
+    for k in range(1, cores):
+        ring = [(i, (i + k) % cores) for i in range(cores)]
+        held.append(lax.ppermute(spread, "core", ring))
+    return held
 
 
 def shards(
@@ -511,8 +533,8 @@
     _, slots = pixels.shape
     per_list = tiles.shape[1]
     sectors = lax.axis_size("sector")
-    sweeps = lax.axis_size("sweep")
-    sweep = lax.axis_index("sweep")
+    sweeps = lax.axis_size(SWEEP)
+    sweep = lax.axis_index(SWEEP)
     slot_tiles = jnp.repeat(tiles, slots // per_list, axis=1)
 
     ahead, behind, cot_lines = edges(image, pltpu.with_memory_space_constraint(cotangent, pltpu.HBM))
@@ -527,38 +549,37 @@
     lines = jnp.concatenate(
         [from_left[beams:][None], cot_lines, from_right[beams:][None]], axis=0
     )
-    band_cot, order = exchanged(lines, "sweep")
+    band_cot, order = exchanged(lines, SWEEP)
     patch, slope, rows, send = forward(
-        base, count, image, from_left, from_right, w_range.reshape(-1, channels), wp_t, targets
+        base, count, image, from_left, from_right, w_range.reshape(-1, channels), wp_t
     )
 
     targets_in, send = lax.optimization_barrier((targets_in, send))
     band_pitch = sweeps * grid_cols + 2 * EDGE
     cell_in = targets_in % CELLS
-    pick_base = (
-        (cell_in // TILE) * band_pitch
-        + (targets_in // CELLS) * TILE
-        + cell_in % TILE
-        + EDGE
-        - 1
-    )
+    column_in = (targets_in // CELLS) * TILE + cell_in % TILE
+    pick_base = (cell_in // TILE) * band_pitch + column_in + EDGE - 1
     flipped = w_head[::-1, ::-1].transpose(2, 0, 1, 3)
     pair_low = jnp.concatenate([flipped[:, 0], flipped[:, 1]], axis=-1)
     pair_high = jnp.concatenate([jnp.zeros_like(flipped[:, 2]), flipped[:, 2]], axis=-1)
     wg = jnp.stack([pair_low, pair_high], axis=1).reshape(head_ch, -1)
     window, send = pick(pick_base, order, band_cot, wg, send)
+    targets_in, send = lax.optimization_barrier((targets_in, send))
+    index_rows = jnp.stack([targets_in % CELLS, targets_in // CELLS], axis=1).astype(BF16)
+    index_rows = jnp.pad(index_rows, ((0, 0), (0, IDX_ROWS - 2), (0, 0)))
+    index_rows, send, window = lax.optimization_barrier((index_rows, send, window))
     mixed = lax.all_to_all(send, "sector", split_axis=0, concat_axis=0, tiled=True)
-    sent_in = mixed[:, 0]
-
-    lists, _ = gathered(sent_in, "sweep")
+    sent_in = jnp.concatenate([mixed[:, 0], index_rows], axis=1)
+
+    lists, _ = gathered(sent_in, SWEEP)
     lists = lists.reshape((-1,) + sent_in.shape[1:])
     owned = grid_cols // TILE
     tile_rows = lists[:, head_ch + 1, :: slots // per_list].astype(jnp.int32).reshape(-1)
     ground = place(tile_rows - (sweep * owned - 1), lists, owned + 2, head_ch)
     local = backward(count, mixed, slope, rows, patch, window, wp_t)
-    total = summed(local, ("sweep", "sector"))
+    held = summed(local)
     taps = w_range.shape[0] * w_range.shape[1] * channels
-    grad_range, grad_proj, grad_head = unpack(total, taps, head_ch)
+    grad_range, grad_proj, grad_head = unpack(held, taps, head_ch)
     grad_range = grad_range.reshape(w_range.shape)
     grad_proj = grad_proj.T
 
@@ -582,20 +603,24 @@
 
 
 def solution(mesh):
+    sweeps, sectors = mesh.devices.shape
+    cores = 2 if sweeps % 2 == 0 else 1
+    devices = mesh.devices.reshape(sweeps // cores, cores, sectors)
+    split = jax.sharding.Mesh(devices, SWEEP + ("sector",))
     return jax.shard_map(
         shards,
-        mesh=mesh,
+        mesh=split,
         in_specs=(
-            P("sweep", None, "sector", None),
-            P("sweep", "sector", None, None),
-            P("sweep", "sector", None, None),
-            P("sweep", "sector", None, None),
-            P("sweep", "sector", None),
+            P(SWEEP, None, "sector", None),
+            P(SWEEP, "sector", None, None),
+            P(SWEEP, "sector", None, None),
+            P(SWEEP, "sector", None, None),
+            P(SWEEP, "sector", None),
             P(),
             P(),
             P(),
-            P(None, "sector", "sweep"),
-        ),
-        out_specs=(P(None, "sector", "sweep"), P(), P(), P()),
+            P(None, "sector", SWEEP),
+        ),
+        out_specs=(P(None, "sector", SWEEP), P(), P(), P()),
         check_vma=False,
     )

time: 109 us -> 106 us (0.972)
  the two profiles are of different devices: /device:TPU:28 before, /device:TPU:29 now
where the time goes in v4:
time: 106 us; the launch traced here: 105 us
  starting transfers between devices  33.9 us (32%)
  Pallas kernels  25.6 us (24%)
  blocking collectives  19.2 us (18%)
  waiting for transfers between devices  16 us (15%)
  other arithmetic  3.35 us (3%)
  local copies, waits for them, and re-layouts  3.29 us (3%)
  matrix products  2.99 us (3%)
  between operations  1.07 us (1%)
    all_to_all x1, blocking collectives, shards(): lax.all_to_all(send, 'sector', split_axis=0, concat_axis=0, tiled=True)  19.2 us
    all_to_all x1, waiting for transfers between devices, summed(): lax.all_to_all(pieces, axes, split_axis=0, concat_axis=0, tiled=True)  10.2 us
    pallas_call x1, Pallas kernels, forward(): pl.pallas_call(forward_kernel, out_shape=(jax.ShapeDtypeStruct((total, ta...  9.37 us
    all_to_all x1, starting transfers between devices, summed(): lax.all_to_all(pieces, axes, split_axis=0, concat_axis=0, tiled=True)  6.9 us
    pallas_call x1, Pallas kernels, pick(): pl.pallas_call(pick_kernel, out_shape=(jax.ShapeDtypeStruct((total, 12 *...  6.39 us
    all_to_all x1, starting transfers between devices, summed(): lax.all_to_all(spread, ('pair', 'sector'), split_axis=0, concat_axis=0, t...  5.55 us
    all_to_all x1, starting transfers between devices, shards(): lax.all_to_all(targets, 'sector', split_axis=0, concat_axis=0, tiled=True)  5.47 us
    ppermute x3, starting transfers between devices, exchanged(): steps.append(lax.ppermute(block, axis, ring))  4.3 us
  transfers between devices with their start and end apart: 13, of which 5 were waited for; matrix products, arithmetic and copies ran while one was open for 7% of the time, Pallas kernels for 17%

profile of v4, /device:TPU:29, one launch (start us, length us, event | category | flops | bytes accessed | tf_op | source)
XLA Modules:
  0.0 105.4 jit_solution(17530701949191573206)
XLA Ops:
  0.6 0.7 multiply_bitcast_fusion
  1.5 1.3 %reshape_add_fusion = s32[8,1,256]{2,1,0:T(1,128)} fusion(s32[8,1,256]{2,1,0:T(1,128)S(1)} %bitcast.141, s32[1,1,8,256]{3,2,1,0:T(8,128)} %param.11), kind=kLoop, calls=%fused_computation.108 | loop fusion | flops 2048 | bytes 24576 | tf_op jit(solution)/shard_map/add | solution.py:544
  2.8 5.5 %all-to-all-start = ((s32[8,1,256]{2,1,0:T(1,128)}), s32[8,1,256]{2,1,0:T(1,128)S(1)}, u32[]{:S(2)}, u32[]{:S(2)}) async-start(s32[8,1,256]{2,1,0:T(1,128)} %reshape_add_fusion), calls=%async_computation | async-start | bytes 16384 | tf_op jit(solution)/shard_map/all_to_all | solution.py:545
  8.3 1.3 %edges.1 = (bf16[128,128]{1,0:T(8,128)(2,1)S(1)}, bf16[128,128]{1,0:T(8,128)(2,1)S(1)}, bf16[16,64,128]{2,1,0:T(8,128)(2,1)S(1)}) custom-call(bf16[64,256,128]{2,1,0:T(8,128)(2,1)} %bitcast.118, bf16[64,16,128]{2,1,0:T(8,128)(2,1)} %cot_ref.1), custom_call_target="tpu_custom_call" | custom-call | tf_op jit(solution)/shard_map/edges/pallas_call | solution.py:97
  9.6 1.2 %collective-permute-start = (bf16[128,128]{1,0:T(8,128)(2,1)S(1)}, bf16[128,128]{1,0:T(8,128)(2,1)S(1)}, u32[]{:S(2)}, u32[]{:S(2)}) collective-permute-start(bf16[128,128]{1,0:T(8,128)(2,1)S(1)} %get-tuple-element.23), channel_id=1, source_target_pairs={{0,1},{1,2},{2,3},{3,4},{4,5},{5,6},{6,7},{7,0},{8,9},{9,10},{10,1... | collective-permute-start | bytes 98312 | tf_op jit(solution)/shard_map/ppermute | solution.py:542
  10.8 1.2 %collective-permute-start.1 = (bf16[128,128]{1,0:T(8,128)(2,1)S(1)}, bf16[128,128]{1,0:T(8,128)(2,1)S(1)}, u32[]{:S(2)}, u32[]{:S(2)}) collective-permute-start(bf16[128,128]{1,0:T(8,128)(2,1)S(1)} %get-tuple-element.24), channel_id=1, source_target_pairs={{1,0},{2,1},{3,2},{4,3},{5,4},{6,5},{7,6},{0,7},{9,8},{10,9},{11,1... | collective-permute-start | bytes 98312 | tf_op jit(solution)/shard_map/ppermute | solution.py:543
  12.2 1.1 %collective-permute-done.left_ref = bf16[128,128]{1,0:T(8,128)(2,1)S(1)} collective-permute-done((bf16[128,128]{1,0:T(8,128)(2,1)S(1)}, bf16[128,128]{1,0:T(8,128)(2,1)S(1)}, u32[]{:S(2)}, u32[]{:S(2)}) %collective-permute-start) | collective-permute-done | bytes 32800 | tf_op jit(solution)/shard_map/ppermute | solution.py:542
  14.0 4.0 %collective-permute-start.2 = (bf16[18,64,128]{2,1,0:T(8,128)(2,1)S(1)}, bf16[18,64,128]{2,1,0:T(8,128)(2,1)S(1)}, u32[]{:S(2)}, u32[]{:S(2)}) collective-permute-start(bf16[18,64,128]{2,1,0:T(8,128)(2,1)S(1)} %get-tuple-element.61), channel_id=1, source_target_pairs={{0,8},{8,16},{16,24},{24,0},{1,9},{9,17},{17,25},{25,1},{2,10},{10... | collective-permute-start | bytes 884744 | tf_op jit(solution)/shard_map/ppermute | solution.py:503
  18.2 9.4 %forward.1 = (bf16[2048,1152]{1,0:T(8,128)(2,1)S(1)}, f32[2048,128]{1,0:T(8,128)S(1)}, bf16[2048,128]{1,0:T(8,128)(2,1)S(1)}, bf16[8,2,64,256]{3,2,1,0:T(8,128)(2,1)S(1)}) custom-call(s32[2048]{0:T(1024)S(1)} %fusion.36.base_ref, s32[8]{0:T(128)S(1)} %bitcast.116, bf16[64,256,128]{2,1,0:T(8,128)(2,1)} %bitcast.119, ...), custom_call_target="tpu_custom_call" | custom-call | flops 603979776 | bytes 25165824 | tf_op jit(solution)/shard_map/forward/pallas_call | solution.py:186
  27.7 1.1 %collective-permute-done.4 = bf16[18,64,128]{2,1,0:T(8,128)(2,1)S(1)} collective-permute-done((bf16[18,64,128]{2,1,0:T(8,128)(2,1)S(1)}, bf16[18,64,128]{2,1,0:T(8,128)(2,1)S(1)}, u32[]{:S(2)}, u32[]{:S(2)}) %collective-permute-start.4) | collective-permute-done | bytes 294944 | tf_op jit(solution)/shard_map/ppermute | solution.py:503
  29.0 6.4 %pick.1 = (bf16[2048,768]{1,0:T(8,128)(2,1)S(1)}, bf16[8,2,64,256]{3,2,1,0:T(8,128)(2,1)S(1)}) custom-call(s32[2048]{0:T(1024)S(1)} %bitcast.115, s32[4]{0:T(128)S(1)} %and_select_fusion.order_ref, bf16[4,18,64,128]{3,2,1,0:T(8,128)(2,1)S(1)} %pad_maximum_fusion.cot_ref, bf16[64,768]{1,0:T(8,128)(2,1)S(1)} %reshape.99.wg_ref, ...), custom_call_target="tpu_custom_call", output_to_operand_aliasing={{1}: (4, {})} | custom-call | flops 201326592 | bytes 12582912 | tf_op jit(solution)/shard_map/pick/pallas_call | solution.py:272
  35.4 19.2 %all_to_all.24.back_ref.sent_ref = bf16[8,2,64,256]{3,2,1,0:T(8,128)(2,1)S(1)} all-to-all(bf16[8,2,64,256]{3,2,1,0:T(8,128)(2,1)S(1)} %get-tuple-element.33), channel_id=1, replica_groups=mesh['pair'=2,'core'=2,'sector'=8] {'sector'}, dimensions={0} | all-to-all | bytes 1048576 | tf_op jit(solution)/shard_map/all_to_all | solution.py:571
  54.8 3.8 %backward.1 = bf16[1536,128]{1,0:T(8,128)(2,1)} custom-call(s32[8]{0:T(128)S(1)} %bitcast.117, bf16[8,2,64,256]{3,2,1,0:T(8,128)(2,1)S(1)} %all_to_all.24.back_ref.sent_ref, bf16[8,2,64,256]{3,2,1,0:T(8,128)(2,1)S(1)} %all_to_all.24.back_ref.sent_ref, f32[2048,128]{1,0:T(8,128)S(1)} %get-tuple-element.35.slope_ref, ...), custom_call_target="tpu_custom_call" | custom-call | flops 603979776 | bytes 10485760 | tf_op jit(solution)/shard_map/backward/pallas_call | solution.py:361
  58.6 6.9 %all-to-all-start.2 = ((bf16[32,48,128]{2,1,0:T(8,128)(2,1)}), bf16[32,48,128]{2,1,0:T(8,128)(2,1)S(1)}, u32[]{:S(2)}, u32[]{:S(2)}) async-start(bf16[32,48,128]{2,1,0:T(8,128)(2,1)} %bitcast.50), calls=%async_computation.2 | async-start | bytes 786432 | tf_op jit(solution)/shard_map/all_to_all | solution.py:511
  66.0 10.2 %all-to-all-done.2 = bf16[32,48,128]{2,1,0:T(8,128)(2,1)S(1)} async-done(((bf16[32,48,128]{2,1,0:T(8,128)(2,1)}), bf16[32,48,128]{2,1,0:T(8,128)(2,1)S(1)}, u32[]{:S(2)}, u32[]{:S(2)}) %all-to-all-start.2) | async-done | bytes 393248 | tf_op jit(solution)/shard_map/all_to_all | solution.py:511
  76.4 0.7 broadcast_in_dim.23
  77.1 5.5 %all-to-all-start.3 = ((bf16[16,48,128]{2,1,0:T(8,128)(2,1)}), bf16[16,48,128]{2,1,0:T(8,128)(2,1)S(1)}, u32[]{:S(2)}, u32[]{:S(2)}) async-start(bf16[16,48,128]{2,1,0:T(8,128)(2,1)} %broadcast_in_dim.23), calls=%async_computation.3 | async-start | bytes 393216 | tf_op jit(solution)/shard_map/all_to_all | solution.py:515
  83.2 3.8 %place.1 = bf16[10,64,256]{2,1,0:T(8,128)(2,1)S(1)} custom-call(s32[64]{0:T(128)S(1)} %sub.58.tile_ref, bf16[32,72,256]{2,1,0:T(8,128)(2,1)S(1)} %bitcast.111), custom_call_target="tpu_custom_call" | custom-call | flops 268435456 | bytes 2097152 | tf_op jit(solution)/shard_map/place/pallas_call | solution.py:466
  87.9 3.8 %collective-permute-start.8 = (bf16[64,1,130]{0,2,1:T(8,128)(2,1)S(1)}, bf16[64,1,130]{0,2,1:T(8,128)(2,1)S(1)}, u32[]{:S(2)}, u32[]{:S(2)}) collective-permute-start(bf16[64,1,130]{0,2,1:T(8,128)(2,1)S(1)} %get-tuple-element.42), channel_id=1, source_target_pairs={{1,0},{2,1},{3,2},{4,3},{5,4},{6,5},{7,6},{9,8},{10,9},{11,10},{12... | collective-permute-start | bytes 49928 | tf_op jit(solution)/shard_map/ppermute | solution.py:592
  91.8 1.9 %collective-permute-start.7 = (bf16[64,1,130]{0,2,1:T(8,128)(2,1)S(1)}, bf16[64,1,130]{0,2,1:T(8,128)(2,1)S(1)}, u32[]{:S(2)}, u32[]{:S(2)}) collective-permute-start(bf16[64,1,130]{0,2,1:T(8,128)(2,1)S(1)} %get-tuple-element.43), channel_id=1, source_target_pairs={{0,1},{1,2},{2,3},{3,4},{4,5},{5,6},{6,7},{8,9},{9,10},{10,11},{11... | collective-permute-start | bytes 49928 | tf_op jit(solution)/shard_map/ppermute | solution.py:591
  94.2 3.1 %collective-permute-done.7 = bf16[64,1,130]{0,2,1:T(8,128)(2,1)S(1)} collective-permute-done((bf16[64,1,130]{0,2,1:T(8,128)(2,1)S(1)}, bf16[64,1,130]{0,2,1:T(8,128)(2,1)S(1)}, u32[]{:S(2)}, u32[]{:S(2)}) %collective-permute-start.7) | collective-permute-done | bytes 16672 | tf_op jit(solution)/shard_map/ppermute | solution.py:591
  100.0 3.0 %collective-permute-start.9 = (bf16[16,48,128]{2,1,0:T(8,128)(2,1)S(1)}, bf16[16,48,128]{2,1,0:T(8,128)(2,1)S(1)}, u32[]{:S(2)}, u32[]{:S(2)}) collective-permute-start(bf16[16,48,128]{2,1,0:T(8,128)(2,1)S(1)} %all-to-all-done.3.refs_0_), channel_id=1, source_target_pairs={{0,8},{8,0},{1,9},{9,1},{2,10},{10,2},{3,11},{11,3},{4,12},{12,4},... | collective-permute-start | bytes 589832 | tf_op jit(solution)/shard_map/ppermute | solution.py:521
  103.7 0.7 copy.37
  104.4 1.0 unpack.1
  (69 shorter events, 7.4 us)
Async XLA Ops:
  2.8 15.4 %all-to-all-start = ((s32[8,1,256]{2,1,0:T(1,128)}), s32[8,1,256]{2,1,0:T(1,128)S(1)}, u32[]{:S(2)}, u32[]{:S(2)}) async-start(s32[8,1,256]{2,1,0:T(1,128)} %reshape_add_fusion), calls=%async_computation | async-start | bytes 16384 | tf_op jit(solution)/shard_map/all_to_all | solution.py:545
  8.2 3.7 %copy-start.4 = (s32[1,1,8,256]{3,2,1,0:T(8,128)S(1)}, s32[1,1,8,256]{3,2,1,0:T(8,128)}, u32[]{:S(2)}) copy-start(s32[1,1,8,256]{3,2,1,0:T(8,128)} %param.10) | copy-start | bytes 24580
  8.2 3.8 %copy-start.3 = (bf16[3,3,64,64]{3,2,1,0:T(8,128)(2,1)S(1)}, bf16[3,3,64,64]{3,2,1,0:T(8,128)(2,1)}, u32[]{:S(2)}) copy-start(bf16[3,3,64,64]{3,2,1,0:T(8,128)(2,1)} %param.16) | copy-start | bytes 221188
  9.6 3.7 %collective-permute-start = (bf16[128,128]{1,0:T(8,128)(2,1)S(1)}, bf16[128,128]{1,0:T(8,128)(2,1)S(1)}, u32[]{:S(2)}, u32[]{:S(2)}) collective-permute-start(bf16[128,128]{1,0:T(8,128)(2,1)S(1)} %get-tuple-element.23), channel_id=1, source_target_pairs={{0,1},{1,2},{2,3},{3,4},{4,5},{5,6},{6,7},{7,0},{8,9},{9,10},{10,1... | collective-permute-start | bytes 98312 | tf_op jit(solution)/shard_map/ppermute | solution.py:542
  10.8 2.8 %collective-permute-start.1 = (bf16[128,128]{1,0:T(8,128)(2,1)S(1)}, bf16[128,128]{1,0:T(8,128)(2,1)S(1)}, u32[]{:S(2)}, u32[]{:S(2)}) collective-permute-start(bf16[128,128]{1,0:T(8,128)(2,1)S(1)} %get-tuple-element.24), channel_id=1, source_target_pairs={{1,0},{2,1},{3,2},{4,3},{5,4},{6,5},{7,6},{0,7},{9,8},{10,9},{11,1... | collective-permute-start | bytes 98312 | tf_op jit(solution)/shard_map/ppermute | solution.py:543
  12.0 6.2 %copy-start = (bf16[3,3,128,128]{3,2,1,0:T(8,128)(2,1)S(1)}, bf16[3,3,128,128]{3,2,1,0:T(8,128)(2,1)}, u32[]{:S(2)}) copy-start(bf16[3,3,128,128]{3,2,1,0:T(8,128)(2,1)} %param.14) | copy-start | bytes 884740
  12.0 6.2 %copy-start.1 = (bf16[128,64]{0,1:T(8,128)(2,1)S(1)}, bf16[128,64]{0,1:T(8,128)(2,1)}, u32[]{:S(2)}) copy-start(bf16[128,64]{0,1:T(8,128)(2,1)} %param.15) | copy-start | bytes 49156
  12.0 6.2 %copy-start.2 = (s32[1,1,8]{2,1,0:T(1,128)S(1)}, s32[1,1,8]{2,1,0:T(1,128)}, u32[]{:S(2)}) copy-start(s32[1,1,8]{2,1,0:T(1,128)} %param.13) | copy-start | bytes 100
  13.7 14.0 %collective-permute-start.3 = (bf16[18,64,128]{2,1,0:T(8,128)(2,1)S(1)}, bf16[18,64,128]{2,1,0:T(8,128)(2,1)S(1)}, u32[]{:S(2)}, u32[]{:S(2)}) collective-permute-start(bf16[18,64,128]{2,1,0:T(8,128)(2,1)S(1)} %get-tuple-element.61), channel_id=1, source_target_pairs={{0,16},{8,24},{16,0},{24,8},{1,17},{9,25},{17,1},{25,9},{2,18},{10... | collective-permute-start | bytes 884744 | tf_op jit(solution)/shard_map/ppermute | solution.py:503
  14.0 13.7 %collective-permute-start.2 = (bf16[18,64,128]{2,1,0:T(8,128)(2,1)S(1)}, bf16[18,64,128]{2,1,0:T(8,128)(2,1)S(1)}, u32[]{:S(2)}, u32[]{:S(2)}) collective-permute-start(bf16[18,64,128]{2,1,0:T(8,128)(2,1)S(1)} %get-tuple-element.61), channel_id=1, source_target_pairs={{0,8},{8,16},{16,24},{24,0},{1,9},{9,17},{17,25},{25,1},{2,10},{10... | collective-permute-start | bytes 884744 | tf_op jit(solution)/shard_map/ppermute | solution.py:503
  18.0 10.8 %collective-permute-start.4 = (bf16[18,64,128]{2,1,0:T(8,128)(2,1)S(1)}, bf16[18,64,128]{2,1,0:T(8,128)(2,1)S(1)}, u32[]{:S(2)}, u32[]{:S(2)}) collective-permute-start(bf16[18,64,128]{2,1,0:T(8,128)(2,1)S(1)} %get-tuple-element.61), channel_id=1, source_target_pairs={{0,24},{8,0},{16,8},{24,16},{1,25},{9,1},{17,9},{25,17},{2,26},{10... | collective-permute-start | bytes 884744 | tf_op jit(solution)/shard_map/ppermute | solution.py:503
  54.7 10.8 %collective-permute-start.5 = (bf16[1,8,72,256]{3,2,1,0:T(8,128)(2,1)S(1)}, bf16[1,8,72,256]{3,2,1,0:T(8,128)(2,1)S(1)}, u32[]{:S(2)}, u32[]{:S(2)}) collective-permute-start(bf16[1,8,72,256]{3,2,1,0:T(8,128)(2,1)S(1)} %get-tuple-element.59), channel_id=1, source_target_pairs={{0,16},{8,24},{16,0},{24,8},{1,17},{9,25},{17,1},{25,9},{2,18},{10... | collective-permute-start | bytes 884744 | tf_op jit(solution)/shard_map/ppermute | solution.py:491
  58.6 17.7 %all-to-all-start.2 = ((bf16[32,48,128]{2,1,0:T(8,128)(2,1)}), bf16[32,48,128]{2,1,0:T(8,128)(2,1)S(1)}, u32[]{:S(2)}, u32[]{:S(2)}) async-start(bf16[32,48,128]{2,1,0:T(8,128)(2,1)} %bitcast.50), calls=%async_computation.2 | async-start | bytes 786432 | tf_op jit(solution)/shard_map/all_to_all | solution.py:511
  65.6 17.0 %collective-permute-start.6 = (bf16[2,8,72,256]{3,2,1,0:T(8,128)(2,1)S(1)}, bf16[2,8,72,256]{3,2,1,0:T(8,128)(2,1)S(1)}, u32[]{:S(2)}, u32[]{:S(2)}) collective-permute-start(bf16[2,8,72,256]{3,2,1,0:T(8,128)(2,1)S(1)} %get-tuple-element.54), channel_id=1, source_target_pairs={{0,8},{8,0},{16,24},{24,16},{1,9},{9,1},{17,25},{25,17},{2,10},{10... | collective-permute-start | bytes 1769480 | tf_op jit(solution)/shard_map/ppermute | solution.py:491
  77.1 22.9 %all-to-all-start.3 = ((bf16[16,48,128]{2,1,0:T(8,128)(2,1)}), bf16[16,48,128]{2,1,0:T(8,128)(2,1)S(1)}, u32[]{:S(2)}, u32[]{:S(2)}) async-start(bf16[16,48,128]{2,1,0:T(8,128)(2,1)} %broadcast_in_dim.23), calls=%async_computation.3 | async-start | bytes 393216 | tf_op jit(solution)/shard_map/all_to_all | solution.py:515
  87.9 6.3 %collective-permute-start.8 = (bf16[64,1,130]{0,2,1:T(8,128)(2,1)S(1)}, bf16[64,1,130]{0,2,1:T(8,128)(2,1)S(1)}, u32[]{:S(2)}, u32[]{:S(2)}) collective-permute-start(bf16[64,1,130]{0,2,1:T(8,128)(2,1)S(1)} %get-tuple-element.42), channel_id=1, source_target_pairs={{1,0},{2,1},{3,2},{4,3},{5,4},{6,5},{7,6},{9,8},{10,9},{11,10},{12... | collective-permute-start | bytes 49928 | tf_op jit(solution)/shard_map/ppermute | solution.py:592
  91.8 5.6 %collective-permute-start.7 = (bf16[64,1,130]{0,2,1:T(8,128)(2,1)S(1)}, bf16[64,1,130]{0,2,1:T(8,128)(2,1)S(1)}, u32[]{:S(2)}, u32[]{:S(2)}) collective-permute-start(bf16[64,1,130]{0,2,1:T(8,128)(2,1)S(1)} %get-tuple-element.43), channel_id=1, source_target_pairs={{0,1},{1,2},{2,3},{3,4},{4,5},{5,6},{6,7},{8,9},{9,10},{10,11},{11... | collective-permute-start | bytes 49928 | tf_op jit(solution)/shard_map/ppermute | solution.py:591
  100.0 4.4 %collective-permute-start.9 = (bf16[16,48,128]{2,1,0:T(8,128)(2,1)S(1)}, bf16[16,48,128]{2,1,0:T(8,128)(2,1)S(1)}, u32[]{:S(2)}, u32[]{:S(2)}) collective-permute-start(bf16[16,48,128]{2,1,0:T(8,128)(2,1)S(1)} %all-to-all-done.3.refs_0_), channel_id=1, source_target_pairs={{0,8},{8,0},{1,9},{9,1},{2,10},{10,2},{3,11},{11,3},{4,12},{12,4},... | collective-permute-start | bytes 589832 | tf_op jit(solution)/shard_map/ppermute | solution.py:521

commit v5 on v4

--- a/solution.py
+++ b/solution.py
@@ -102,7 +102,7 @@
         scratch_shapes=[
             pltpu.VMEM((2, beams, TILE, channels), BF16),
             pltpu.VMEM(cot.shape, BF16),
-            pltpu.VMEM((max(beams * TILE, head_ch * rows), channels), F32),
+            pltpu.VMEM((max(beams * TILE, head_ch * rows) + EDGE, channels), F32),
             pltpu.SemaphoreType.DMA((3,)),
         ],
         compiler_params=pltpu.CompilerParams(vmem_limit_bytes=4 << 20),
@@ -131,8 +131,8 @@
         blank = jnp.zeros((pitch, channels), F32)
         table[pl.ds(0, pitch), :] = blank
         table[pl.ds((beams + 1) * pitch, pitch), :] = blank
-        ends[0] = left_ref[pl.ds(0, beams), :].astype(F32)
-        ends[1] = right_ref[pl.ds(0, beams), :].astype(F32)
+        ends[0, pl.ds(0, beams), :] = left_ref[pl.ds(0, beams), :].astype(F32)
+        ends[1, pl.ds(0, beams), :] = right_ref[pl.ds(0, beams), :].astype(F32)
 
         def sides(beam, _):
             line = (beam + 1) * pitch
@@ -209,10 +209,10 @@
             ],
             scratch_shapes=[
                 pltpu.VMEM((beams, columns, channels), BF16),
-                pltpu.VMEM(((beams + 2) * pitch, channels), F32),
-                pltpu.VMEM((2, beams, channels), F32),
-                pltpu.VMEM((3 * slots * WIDE, channels), F32),
-                pltpu.VMEM((3 * slots * WIDE, channels), F32),
+                pltpu.VMEM(((beams + 2) * pitch + EDGE, channels), F32),
+                pltpu.VMEM((2, beams + EDGE, channels), F32),
+                pltpu.VMEM((3 * slots * WIDE + EDGE, channels), F32),
+                pltpu.VMEM((3 * slots * WIDE + EDGE, channels), F32),
                 pltpu.SemaphoreType.DMA((beams // 8,)),
             ],
         ),
@@ -288,9 +288,9 @@
                 pl.BlockSpec((1, 1) + send.shape[2:], late4),
             ],
             scratch_shapes=[
-                pltpu.VMEM(((lines - 1) * pitch, 2 * head_ch), F32),
-                pltpu.VMEM((2 * slots * WIDE, 2 * head_ch), F32),
-                pltpu.VMEM((2 * slots * WIDE, 2 * head_ch), F32),
+                pltpu.VMEM(((lines - 1) * pitch + EDGE, 2 * head_ch), F32),
+                pltpu.VMEM((2 * slots * WIDE + EDGE, 2 * head_ch), F32),
+                pltpu.VMEM((2 * slots * WIDE + EDGE, 2 * head_ch), F32),
             ],
         ),
         input_output_aliases={4: 1},
@@ -590,14 +590,16 @@
     )
     over = lax.ppermute(ground[:, -1:], "sector", ring[:-1])
     under = lax.ppermute(ground[:, :1], "sector", [(j, i) for i, j in ring[:-1]])
-    ground_pad = jnp.concatenate([over, ground, under], axis=1)
     head_sum = jnp.zeros((head_ch, grid_rows * grid_cols), F32)
-    for row_off in range(3):
+    for row_off in (1, 0, 2):
+        block = ground
+        if row_off == 0:
+            block = jnp.concatenate([over, ground[:, :-1]], axis=1)
+        elif row_off == 2:
+            block = jnp.concatenate([ground[:, 1:], under], axis=1)
         for col_off in range(3):
-            view = ground_pad[:, row_off : row_off + grid_rows, col_off : col_off + grid_cols]
-            head_sum = head_sum + dot(
-                w_head[row_off, col_off].T, view.reshape(head_ch, -1)
-            )
+            view = block[:, :, col_off : col_off + grid_cols].reshape(head_ch, -1)
+            head_sum = head_sum + dot(w_head[row_off, col_off].T, view)
     head_out = head_sum.astype(BF16).reshape(head_ch, grid_rows, grid_cols)
     return head_out, grad_range, grad_proj, grad_head
 

time: 106 us -> 104 us (0.981)
  the two profiles are of different devices: /device:TPU:29 before, /device:TPU:0 now
where the time goes in v5:
time: 104 us; the launch traced here: 103 us
  starting transfers between devices  28 us (27%)
  Pallas kernels  26.4 us (25%)
  blocking collectives  20.7 us (20%)
  waiting for transfers between devices  17.1 us (16%)
  other arithmetic  3.54 us (3%)
  local copies, waits for them, and re-layouts  3.3 us (3%)
  matrix products  2.99 us (3%)
  between operations  1.11 us (1%)
    all_to_all x1, blocking collectives, shards(): lax.all_to_all(send, 'sector', split_axis=0, concat_axis=0, tiled=True)  20.7 us
    all_to_all x1, waiting for transfers between devices, summed(): lax.all_to_all(pieces, axes, split_axis=0, concat_axis=0, tiled=True)  12.5 us
    pallas_call x1, Pallas kernels, forward(): pl.pallas_call(forward_kernel, out_shape=(jax.ShapeDtypeStruct((total, ta...  9.37 us
    all_to_all x1, starting transfers between devices, shards(): lax.all_to_all(targets, 'sector', split_axis=0, concat_axis=0, tiled=True)  7.28 us
    pallas_call x1, Pallas kernels, pick(): pl.pallas_call(pick_kernel, out_shape=(jax.ShapeDtypeStruct((total, 12 *...  6.39 us
    pallas_call x1, Pallas kernels, place(): pl.pallas_call(place_kernel, out_shape=jax.ShapeDtypeStruct((count, head_...  4.52 us
    pallas_call x1, Pallas kernels, backward(): pl.pallas_call(backward_kernel, out_shape=jax.ShapeDtypeStruct((out_rows,...  3.76 us
    all_to_all x1, starting transfers between devices, summed(): lax.all_to_all(spread, ('pair', 'sector'), split_axis=0, concat_axis=0, t...  3.52 us
  transfers between devices with their start and end apart: 13, of which 4 were waited for; matrix products, arithmetic and copies ran while one was open for 7% of the time, Pallas kernels for 18%

profile of v5, /device:TPU:0, one launch (start us, length us, event | category | flops | bytes accessed | tf_op | source)
XLA Modules:
  0.0 103.1 jit_solution(6508461660555872638)
XLA Ops:
  1.5 1.3 %reshape_add_fusion = s32[8,1,256]{2,1,0:T(1,128)} fusion(s32[8,1,256]{2,1,0:T(1,128)S(1)} %bitcast.141, s32[1,1,8,256]{3,2,1,0:T(8,128)} %param.11), kind=kLoop, calls=%fused_computation.104 | loop fusion | flops 2048 | bytes 24576 | tf_op jit(solution)/shard_map/add | solution.py:544
  2.8 7.3 %all-to-all-start = ((s32[8,1,256]{2,1,0:T(1,128)}), s32[8,1,256]{2,1,0:T(1,128)S(1)}, u32[]{:S(2)}, u32[]{:S(2)}) async-start(s32[8,1,256]{2,1,0:T(1,128)} %reshape_add_fusion), calls=%async_computation | async-start | bytes 16384 | tf_op jit(solution)/shard_map/all_to_all | solution.py:545
  10.1 1.3 %edges.1 = (bf16[128,128]{1,0:T(8,128)(2,1)S(1)}, bf16[128,128]{1,0:T(8,128)(2,1)S(1)}, bf16[16,64,128]{2,1,0:T(8,128)(2,1)S(1)}) custom-call(bf16[64,256,128]{2,1,0:T(8,128)(2,1)} %bitcast.121, bf16[64,16,128]{2,1,0:T(8,128)(2,1)} %cot_ref.1), custom_call_target="tpu_custom_call" | custom-call | tf_op jit(solution)/shard_map/edges/pallas_call | solution.py:97
  11.4 2.1 %collective-permute-start = (bf16[128,128]{1,0:T(8,128)(2,1)S(1)}, bf16[128,128]{1,0:T(8,128)(2,1)S(1)}, u32[]{:S(2)}, u32[]{:S(2)}) collective-permute-start(bf16[128,128]{1,0:T(8,128)(2,1)S(1)} %get-tuple-element.23), channel_id=1, source_target_pairs={{0,1},{1,2},{2,3},{3,4},{4,5},{5,6},{6,7},{7,0},{8,9},{9,10},{10,1... | collective-permute-start | bytes 98312 | tf_op jit(solution)/shard_map/ppermute | solution.py:542
  13.5 2.8 %collective-permute-start.1 = (bf16[128,128]{1,0:T(8,128)(2,1)S(1)}, bf16[128,128]{1,0:T(8,128)(2,1)S(1)}, u32[]{:S(2)}, u32[]{:S(2)}) collective-permute-start(bf16[128,128]{1,0:T(8,128)(2,1)S(1)} %get-tuple-element.24), channel_id=1, source_target_pairs={{1,0},{2,1},{3,2},{4,3},{5,4},{6,5},{7,6},{0,7},{9,8},{10,9},{11,1... | collective-permute-start | bytes 98312 | tf_op jit(solution)/shard_map/ppermute | solution.py:543
  16.5 1.6 %collective-permute-done.left_ref = bf16[128,128]{1,0:T(8,128)(2,1)S(1)} collective-permute-done((bf16[128,128]{1,0:T(8,128)(2,1)S(1)}, bf16[128,128]{1,0:T(8,128)(2,1)S(1)}, u32[]{:S(2)}, u32[]{:S(2)}) %collective-permute-start) | collective-permute-done | bytes 32800 | tf_op jit(solution)/shard_map/ppermute | solution.py:542
  18.1 1.6 %collective-permute-start.3 = (bf16[18,64,128]{2,1,0:T(8,128)(2,1)S(1)}, bf16[18,64,128]{2,1,0:T(8,128)(2,1)S(1)}, u32[]{:S(2)}, u32[]{:S(2)}) collective-permute-start(bf16[18,64,128]{2,1,0:T(8,128)(2,1)S(1)} %get-tuple-element.60), channel_id=1, source_target_pairs={{0,16},{8,24},{16,0},{24,8},{1,17},{9,25},{17,1},{25,9},{2,18},{10... | collective-permute-start | bytes 884744 | tf_op jit(solution)/shard_map/ppermute | solution.py:503
  19.7 1.7 %collective-permute-start.4 = (bf16[18,64,128]{2,1,0:T(8,128)(2,1)S(1)}, bf16[18,64,128]{2,1,0:T(8,128)(2,1)S(1)}, u32[]{:S(2)}, u32[]{:S(2)}) collective-permute-start(bf16[18,64,128]{2,1,0:T(8,128)(2,1)S(1)} %get-tuple-element.60), channel_id=1, source_target_pairs={{0,24},{8,0},{16,8},{24,16},{1,25},{9,1},{17,9},{25,17},{2,26},{10... | collective-permute-start | bytes 884744 | tf_op jit(solution)/shard_map/ppermute | solution.py:503
  21.7 9.4 %forward.1 = (bf16[2048,1152]{1,0:T(8,128)(2,1)S(1)}, f32[2048,128]{1,0:T(8,128)S(1)}, bf16[2048,128]{1,0:T(8,128)(2,1)S(1)}, bf16[8,2,64,256]{3,2,1,0:T(8,128)(2,1)S(1)}) custom-call(s32[2048]{0:T(1024)S(1)} %fusion.36.base_ref, s32[8]{0:T(128)S(1)} %bitcast.116, bf16[64,256,128]{2,1,0:T(8,128)(2,1)} %bitcast.122, ...), custom_call_target="tpu_custom_call" | custom-call | flops 603979776 | bytes 25165824 | tf_op jit(solution)/shard_map/forward/pallas_call | solution.py:186
  31.3 6.4 %pick.1 = (bf16[2048,768]{1,0:T(8,128)(2,1)S(1)}, bf16[8,2,64,256]{3,2,1,0:T(8,128)(2,1)S(1)}) custom-call(s32[2048]{0:T(1024)S(1)} %bitcast.115, s32[4]{0:T(128)S(1)} %and_select_fusion.order_ref, bf16[4,18,64,128]{3,2,1,0:T(8,128)(2,1)S(1)} %pad_maximum_fusion.cot_ref, bf16[64,768]{1,0:T(8,128)(2,1)S(1)} %reshape.99.wg_ref, ...), custom_call_target="tpu_custom_call", output_to_operand_aliasing={{1}: (4, {})} | custom-call | flops 201326592 | bytes 12582912 | tf_op jit(solution)/shard_map/pick/pallas_call | solution.py:272
  37.8 20.7 %all_to_all.24.back_ref.sent_ref = bf16[8,2,64,256]{3,2,1,0:T(8,128)(2,1)S(1)} all-to-all(bf16[8,2,64,256]{3,2,1,0:T(8,128)(2,1)S(1)} %get-tuple-element.33), channel_id=1, replica_groups=mesh['pair'=2,'core'=2,'sector'=8] {'sector'}, dimensions={0} | all-to-all | bytes 1048576 | tf_op jit(solution)/shard_map/all_to_all | solution.py:571
  58.6 1.6 %collective-permute-start.5 = (bf16[1,8,72,256]{3,2,1,0:T(8,128)(2,1)S(1)}, bf16[1,8,72,256]{3,2,1,0:T(8,128)(2,1)S(1)}, u32[]{:S(2)}, u32[]{:S(2)}) collective-permute-start(bf16[1,8,72,256]{3,2,1,0:T(8,128)(2,1)S(1)} %get-tuple-element.58), channel_id=1, source_target_pairs={{0,16},{8,24},{16,0},{24,8},{1,17},{9,25},{17,1},{25,9},{2,18},{10... | collective-permute-start | bytes 884744 | tf_op jit(solution)/shard_map/ppermute | solution.py:491
  60.2 3.8 %backward.1 = bf16[1536,128]{1,0:T(8,128)(2,1)} custom-call(s32[8]{0:T(128)S(1)} %bitcast.117, bf16[8,2,64,256]{3,2,1,0:T(8,128)(2,1)S(1)} %all_to_all.24.back_ref.sent_ref, bf16[8,2,64,256]{3,2,1,0:T(8,128)(2,1)S(1)} %all_to_all.24.back_ref.sent_ref, f32[2048,128]{1,0:T(8,128)S(1)} %get-tuple-element.35.slope_ref, ...), custom_call_target="tpu_custom_call" | custom-call | flops 603979776 | bytes 10485760 | tf_op jit(solution)/shard_map/backward/pallas_call | solution.py:361
  64.0 2.7 %all-to-all-start.2 = ((bf16[32,48,128]{2,1,0:T(8,128)(2,1)}), bf16[32,48,128]{2,1,0:T(8,128)(2,1)S(1)}, u32[]{:S(2)}, u32[]{:S(2)}) async-start(bf16[32,48,128]{2,1,0:T(8,128)(2,1)} %bitcast.50), calls=%async_computation.2 | async-start | bytes 786432 | tf_op jit(solution)/shard_map/all_to_all | solution.py:511
  66.7 0.8 collective-permute-done.5
  67.6 12.5 %all-to-all-done.2 = bf16[32,48,128]{2,1,0:T(8,128)(2,1)S(1)} async-done(((bf16[32,48,128]{2,1,0:T(8,128)(2,1)}), bf16[32,48,128]{2,1,0:T(8,128)(2,1)S(1)}, u32[]{:S(2)}, u32[]{:S(2)}) %all-to-all-start.2) | async-done | bytes 393248 | tf_op jit(solution)/shard_map/all_to_all | solution.py:511
  80.2 0.7 broadcast_in_dim.23
  80.9 3.5 %all-to-all-start.3 = ((bf16[16,48,128]{2,1,0:T(8,128)(2,1)}), bf16[16,48,128]{2,1,0:T(8,128)(2,1)S(1)}, u32[]{:S(2)}, u32[]{:S(2)}) async-start(bf16[16,48,128]{2,1,0:T(8,128)(2,1)} %broadcast_in_dim.23), calls=%async_computation.3 | async-start | bytes 393216 | tf_op jit(solution)/shard_map/all_to_all | solution.py:515
  85.1 4.5 %place.1 = bf16[10,64,256]{2,1,0:T(8,128)(2,1)S(1)} custom-call(s32[64]{0:T(128)S(1)} %sub.58.tile_ref, bf16[32,72,256]{2,1,0:T(8,128)(2,1)S(1)} %bitcast.111), custom_call_target="tpu_custom_call" | custom-call | flops 268435456 | bytes 2097152 | tf_op jit(solution)/shard_map/place/pallas_call | solution.py:466
  90.4 3.3 %collective-permute-start.7 = (bf16[64,1,130]{0,2,1:T(8,128)(2,1)S(1)}, bf16[64,1,130]{0,2,1:T(8,128)(2,1)S(1)}, u32[]{:S(2)}, u32[]{:S(2)}) collective-permute-start(bf16[64,1,130]{0,2,1:T(8,128)(2,1)S(1)} %get-tuple-element.44), channel_id=1, source_target_pairs={{0,1},{1,2},{2,3},{3,4},{4,5},{5,6},{6,7},{8,9},{9,10},{10,11},{11... | collective-permute-start | bytes 49928 | tf_op jit(solution)/shard_map/ppermute | solution.py:591
  93.7 1.3 %collective-permute-start.8 = (bf16[64,1,130]{0,2,1:T(8,128)(2,1)S(1)}, bf16[64,1,130]{0,2,1:T(8,128)(2,1)S(1)}, u32[]{:S(2)}, u32[]{:S(2)}) collective-permute-start(bf16[64,1,130]{0,2,1:T(8,128)(2,1)S(1)} %get-tuple-element.45), channel_id=1, source_target_pairs={{1,0},{2,1},{3,2},{4,3},{5,4},{6,5},{7,6},{9,8},{10,9},{11,10},{12... | collective-permute-start | bytes 49928 | tf_op jit(solution)/shard_map/ppermute | solution.py:592
  97.3 2.2 %collective-permute-done.8 = bf16[64,1,130]{0,2,1:T(8,128)(2,1)S(1)} collective-permute-done((bf16[64,1,130]{0,2,1:T(8,128)(2,1)S(1)}, bf16[64,1,130]{0,2,1:T(8,128)(2,1)S(1)}, u32[]{:S(2)}, u32[]{:S(2)}) %collective-permute-start.8) | collective-permute-done | bytes 16672 | tf_op jit(solution)/shard_map/ppermute | solution.py:592
  101.3 0.7 copy.37
  102.1 1.0 unpack.1
  (70 shorter events, 7.2 us)
Async XLA Ops:
  2.8 18.9 %all-to-all-start = ((s32[8,1,256]{2,1,0:T(1,128)}), s32[8,1,256]{2,1,0:T(1,128)S(1)}, u32[]{:S(2)}, u32[]{:S(2)}) async-start(s32[8,1,256]{2,1,0:T(1,128)} %reshape_add_fusion), calls=%async_computation | async-start | bytes 16384 | tf_op jit(solution)/shard_map/all_to_all | solution.py:545
  10.1 6.2 %copy-start.4 = (s32[1,1,8,256]{3,2,1,0:T(8,128)S(1)}, s32[1,1,8,256]{3,2,1,0:T(8,128)}, u32[]{:S(2)}) copy-start(s32[1,1,8,256]{3,2,1,0:T(8,128)} %param.10) | copy-start | bytes 24580
  10.1 6.2 %copy-start.3 = (bf16[3,3,64,64]{3,2,1,0:T(8,128)(2,1)S(1)}, bf16[3,3,64,64]{3,2,1,0:T(8,128)(2,1)}, u32[]{:S(2)}) copy-start(bf16[3,3,64,64]{3,2,1,0:T(8,128)(2,1)} %param.16) | copy-start | bytes 221188
  11.4 6.7 %collective-permute-start = (bf16[128,128]{1,0:T(8,128)(2,1)S(1)}, bf16[128,128]{1,0:T(8,128)(2,1)S(1)}, u32[]{:S(2)}, u32[]{:S(2)}) collective-permute-start(bf16[128,128]{1,0:T(8,128)(2,1)S(1)} %get-tuple-element.23), channel_id=1, source_target_pairs={{0,1},{1,2},{2,3},{3,4},{4,5},{5,6},{6,7},{7,0},{8,9},{9,10},{10,1... | collective-permute-start | bytes 98312 | tf_op jit(solution)/shard_map/ppermute | solution.py:542
  13.5 4.6 %collective-permute-start.1 = (bf16[128,128]{1,0:T(8,128)(2,1)S(1)}, bf16[128,128]{1,0:T(8,128)(2,1)S(1)}, u32[]{:S(2)}, u32[]{:S(2)}) collective-permute-start(bf16[128,128]{1,0:T(8,128)(2,1)S(1)} %get-tuple-element.24), channel_id=1, source_target_pairs={{1,0},{2,1},{3,2},{4,3},{5,4},{6,5},{7,6},{0,7},{9,8},{10,9},{11,1... | collective-permute-start | bytes 98312 | tf_op jit(solution)/shard_map/ppermute | solution.py:543
  16.3 5.4 %copy-start = (bf16[3,3,128,128]{3,2,1,0:T(8,128)(2,1)S(1)}, bf16[3,3,128,128]{3,2,1,0:T(8,128)(2,1)}, u32[]{:S(2)}) copy-start(bf16[3,3,128,128]{3,2,1,0:T(8,128)(2,1)} %param.14) | copy-start | bytes 884740
  16.3 5.4 %copy-start.1 = (bf16[128,64]{0,1:T(8,128)(2,1)S(1)}, bf16[128,64]{0,1:T(8,128)(2,1)}, u32[]{:S(2)}) copy-start(bf16[128,64]{0,1:T(8,128)(2,1)} %param.15) | copy-start | bytes 49156
  16.3 5.4 %copy-start.2 = (s32[1,1,8]{2,1,0:T(1,128)S(1)}, s32[1,1,8]{2,1,0:T(1,128)}, u32[]{:S(2)}) copy-start(s32[1,1,8]{2,1,0:T(1,128)} %param.13) | copy-start | bytes 100
  18.1 13.0 %collective-permute-start.3 = (bf16[18,64,128]{2,1,0:T(8,128)(2,1)S(1)}, bf16[18,64,128]{2,1,0:T(8,128)(2,1)S(1)}, u32[]{:S(2)}, u32[]{:S(2)}) collective-permute-start(bf16[18,64,128]{2,1,0:T(8,128)(2,1)S(1)} %get-tuple-element.60), channel_id=1, source_target_pairs={{0,16},{8,24},{16,0},{24,8},{1,17},{9,25},{17,1},{25,9},{2,18},{10... | collective-permute-start | bytes 884744 | tf_op jit(solution)/shard_map/ppermute | solution.py:503
  19.7 11.4 %collective-permute-start.2 = (bf16[18,64,128]{2,1,0:T(8,128)(2,1)S(1)}, bf16[18,64,128]{2,1,0:T(8,128)(2,1)S(1)}, u32[]{:S(2)}, u32[]{:S(2)}) collective-permute-start(bf16[18,64,128]{2,1,0:T(8,128)(2,1)S(1)} %get-tuple-element.60), channel_id=1, source_target_pairs={{0,8},{8,16},{16,24},{24,0},{1,9},{9,17},{17,25},{25,1},{2,10},{10... | collective-permute-start | bytes 884744 | tf_op jit(solution)/shard_map/ppermute | solution.py:503
  19.7 11.4 %collective-permute-start.4 = (bf16[18,64,128]{2,1,0:T(8,128)(2,1)S(1)}, bf16[18,64,128]{2,1,0:T(8,128)(2,1)S(1)}, u32[]{:S(2)}, u32[]{:S(2)}) collective-permute-start(bf16[18,64,128]{2,1,0:T(8,128)(2,1)S(1)} %get-tuple-element.60), channel_id=1, source_target_pairs={{0,24},{8,0},{16,8},{24,16},{1,25},{9,1},{17,9},{25,17},{2,26},{10... | collective-permute-start | bytes 884744 | tf_op jit(solution)/shard_map/ppermute | solution.py:503
  58.6 8.9 %collective-permute-start.5 = (bf16[1,8,72,256]{3,2,1,0:T(8,128)(2,1)S(1)}, bf16[1,8,72,256]{3,2,1,0:T(8,128)(2,1)S(1)}, u32[]{:S(2)}, u32[]{:S(2)}) collective-permute-start(bf16[1,8,72,256]{3,2,1,0:T(8,128)(2,1)S(1)} %get-tuple-element.58), channel_id=1, source_target_pairs={{0,16},{8,24},{16,0},{24,8},{1,17},{9,25},{17,1},{25,9},{2,18},{10... | collective-permute-start | bytes 884744 | tf_op jit(solution)/shard_map/ppermute | solution.py:491
  64.0 16.1 %all-to-all-start.2 = ((bf16[32,48,128]{2,1,0:T(8,128)(2,1)}), bf16[32,48,128]{2,1,0:T(8,128)(2,1)S(1)}, u32[]{:S(2)}, u32[]{:S(2)}) async-start(bf16[32,48,128]{2,1,0:T(8,128)(2,1)} %bitcast.50), calls=%async_computation.2 | async-start | bytes 786432 | tf_op jit(solution)/shard_map/all_to_all | solution.py:511
  67.5 16.9 %collective-permute-start.6 = (bf16[2,8,72,256]{3,2,1,0:T(8,128)(2,1)S(1)}, bf16[2,8,72,256]{3,2,1,0:T(8,128)(2,1)S(1)}, u32[]{:S(2)}, u32[]{:S(2)}) collective-permute-start(bf16[2,8,72,256]{3,2,1,0:T(8,128)(2,1)S(1)} %get-tuple-element.50), channel_id=1, source_target_pairs={{0,8},{8,0},{16,24},{24,16},{1,9},{9,1},{17,25},{25,17},{2,10},{10... | collective-permute-start | bytes 1769480 | tf_op jit(solution)/shard_map/ppermute | solution.py:491
  80.9 19.7 %all-to-all-start.3 = ((bf16[16,48,128]{2,1,0:T(8,128)(2,1)}), bf16[16,48,128]{2,1,0:T(8,128)(2,1)S(1)}, u32[]{:S(2)}, u32[]{:S(2)}) async-start(bf16[16,48,128]{2,1,0:T(8,128)(2,1)} %broadcast_in_dim.23), calls=%async_computation.3 | async-start | bytes 393216 | tf_op jit(solution)/shard_map/all_to_all | solution.py:515
  90.4 5.7 %collective-permute-start.7 = (bf16[64,1,130]{0,2,1:T(8,128)(2,1)S(1)}, bf16[64,1,130]{0,2,1:T(8,128)(2,1)S(1)}, u32[]{:S(2)}, u32[]{:S(2)}) collective-permute-start(bf16[64,1,130]{0,2,1:T(8,128)(2,1)S(1)} %get-tuple-element.44), channel_id=1, source_target_pairs={{0,1},{1,2},{2,3},{3,4},{4,5},{5,6},{6,7},{8,9},{9,10},{10,11},{11... | collective-permute-start | bytes 49928 | tf_op jit(solution)/shard_map/ppermute | solution.py:591
  93.7 5.8 %collective-permute-start.8 = (bf16[64,1,130]{0,2,1:T(8,128)(2,1)S(1)}, bf16[64,1,130]{0,2,1:T(8,128)(2,1)S(1)}, u32[]{:S(2)}, u32[]{:S(2)}) collective-permute-start(bf16[64,1,130]{0,2,1:T(8,128)(2,1)S(1)} %get-tuple-element.45), channel_id=1, source_target_pairs={{1,0},{2,1},{3,2},{4,3},{5,4},{6,5},{7,6},{9,8},{10,9},{11,10},{12... | collective-permute-start | bytes 49928 | tf_op jit(solution)/shard_map/ppermute | solution.py:592
  100.6 1.5 %collective-permute-start.9 = (bf16[16,48,128]{2,1,0:T(8,128)(2,1)S(1)}, bf16[16,48,128]{2,1,0:T(8,128)(2,1)S(1)}, u32[]{:S(2)}, u32[]{:S(2)}) collective-permute-start(bf16[16,48,128]{2,1,0:T(8,128)(2,1)S(1)} %all-to-all-done.3.refs_0_), channel_id=1, source_target_pairs={{0,8},{8,0},{1,9},{9,1},{2,10},{10,2},{3,11},{11,3},{4,12},{12,4},... | collective-permute-start | bytes 589832 | tf_op jit(solution)/shard_map/ppermute | solution.py:521

commit v6 on v5

--- a/solution.py
+++ b/solution.py
@@ -14,7 +14,7 @@
 WIDE = 4
 IDX_ROWS = 8
 SWEEP = ("pair", "core")
-GROUP = 4
+GROUP = 8
 BF16 = jnp.bfloat16
 F32 = jnp.float32
 NT = (((1,), (1,)), ((), ()))
@@ -381,7 +381,7 @@
             ],
         ),
         compiler_params=pltpu.CompilerParams(
-            dimension_semantics=("arbitrary",), vmem_limit_bytes=20 << 20
+            dimension_semantics=("arbitrary",), vmem_limit_bytes=28 << 20
         ),
         cost_estimate=pl.CostEstimate(
             flops=2 * total * taps * channels, bytes_accessed=10 << 20, transcendentals=0
@@ -590,13 +590,12 @@
     )
     over = lax.ppermute(ground[:, -1:], "sector", ring[:-1])
     under = lax.ppermute(ground[:, :1], "sector", [(j, i) for i, j in ring[:-1]])
+    ground_pad = jnp.concatenate([over, ground, under], axis=1)
     head_sum = jnp.zeros((head_ch, grid_rows * grid_cols), F32)
     for row_off in (1, 0, 2):
         block = ground
-        if row_off == 0:
-            block = jnp.concatenate([over, ground[:, :-1]], axis=1)
-        elif row_off == 2:
-            block = jnp.concatenate([ground[:, 1:], under], axis=1)
+        if row_off != 1:
+            block = ground_pad[:, row_off : row_off + grid_rows]
         for col_off in range(3):
             view = block[:, :, col_off : col_off + grid_cols].reshape(head_ch, -1)
             head_sum = head_sum + dot(w_head[row_off, col_off].T, view)

time: 104 us -> 104 us (level)
  waiting for transfers between devices: 17.1 us -> 18.2 us
    ppermute x1, waiting for transfers between devices: 2.23 us -> 3.34 us  [shards(): lax.ppermute(ground[:, :1], 'sector', [(j, i) for i, j in ring[:-1]])]
where the time goes in v6:
time: 104 us; the launch traced here: 103 us
  starting transfers between devices  28 us (27%)
  Pallas kernels  25.9 us (25%)
  blocking collectives  20.7 us (20%)
  waiting for transfers between devices  18.2 us (18%)
  local copies, waits for them, and re-layouts  3.3 us (3%)
  other arithmetic  3.27 us (3%)
  matrix products  2.98 us (3%)
  between operations  1.11 us (1%)
    all_to_all x1, blocking collectives, shards(): lax.all_to_all(send, 'sector', split_axis=0, concat_axis=0, tiled=True)  20.7 us
    all_to_all x1, waiting for transfers between devices, summed(): lax.all_to_all(pieces, axes, split_axis=0, concat_axis=0, tiled=True)  12 us
    pallas_call x1, Pallas kernels, forward(): pl.pallas_call(forward_kernel, out_shape=(jax.ShapeDtypeStruct((total, ta...  9.37 us
    all_to_all x1, starting transfers between devices, shards(): lax.all_to_all(targets, 'sector', split_axis=0, concat_axis=0, tiled=True)  7.28 us
    pallas_call x1, Pallas kernels, pick(): pl.pallas_call(pick_kernel, out_shape=(jax.ShapeDtypeStruct((total, 12 *...  6.39 us
    pallas_call x1, Pallas kernels, place(): pl.pallas_call(place_kernel, out_shape=jax.ShapeDtypeStruct((count, head_...  4.52 us
    all_to_all x1, starting transfers between devices, summed(): lax.all_to_all(spread, ('pair', 'sector'), split_axis=0, concat_axis=0, t...  3.52 us
    ppermute x1, waiting for transfers between devices, shards(): lax.ppermute(ground[:, :1], 'sector', [(j, i) for i, j in ring[:-1]])  3.34 us
  transfers between devices with their start and end apart: 13, of which 4 were waited for; matrix products, arithmetic and copies ran while one was open for 7% of the time, Pallas kernels for 18%

profile of v6, /device:TPU:0, one launch (start us, length us, event | category | flops | bytes accessed | tf_op | source)
XLA Modules:
  0.0 103.4 jit_solution(14216133396428740751)
XLA Ops:
  1.5 1.3 %reshape_add_fusion = s32[8,1,256]{2,1,0:T(1,128)} fusion(s32[8,1,256]{2,1,0:T(1,128)S(1)} %bitcast.141, s32[1,1,8,256]{3,2,1,0:T(8,128)} %param.11), kind=kLoop, calls=%fused_computation.108 | loop fusion | flops 2048 | bytes 24576 | tf_op jit(solution)/shard_map/add | solution.py:544
  2.8 7.3 %all-to-all-start = ((s32[8,1,256]{2,1,0:T(1,128)}), s32[8,1,256]{2,1,0:T(1,128)S(1)}, u32[]{:S(2)}, u32[]{:S(2)}) async-start(s32[8,1,256]{2,1,0:T(1,128)} %reshape_add_fusion), calls=%async_computation | async-start | bytes 16384 | tf_op jit(solution)/shard_map/all_to_all | solution.py:545
  10.1 1.3 %edges.1 = (bf16[128,128]{1,0:T(8,128)(2,1)S(1)}, bf16[128,128]{1,0:T(8,128)(2,1)S(1)}, bf16[16,64,128]{2,1,0:T(8,128)(2,1)S(1)}) custom-call(bf16[64,256,128]{2,1,0:T(8,128)(2,1)} %bitcast.118, bf16[64,16,128]{2,1,0:T(8,128)(2,1)} %cot_ref.1), custom_call_target="tpu_custom_call" | custom-call | tf_op jit(solution)/shard_map/edges/pallas_call | solution.py:97
  11.4 2.1 %collective-permute-start = (bf16[128,128]{1,0:T(8,128)(2,1)S(1)}, bf16[128,128]{1,0:T(8,128)(2,1)S(1)}, u32[]{:S(2)}, u32[]{:S(2)}) collective-permute-start(bf16[128,128]{1,0:T(8,128)(2,1)S(1)} %get-tuple-element.23), channel_id=1, source_target_pairs={{0,1},{1,2},{2,3},{3,4},{4,5},{5,6},{6,7},{7,0},{8,9},{9,10},{10,1... | collective-permute-start | bytes 98312 | tf_op jit(solution)/shard_map/ppermute | solution.py:542
  13.5 2.8 %collective-permute-start.1 = (bf16[128,128]{1,0:T(8,128)(2,1)S(1)}, bf16[128,128]{1,0:T(8,128)(2,1)S(1)}, u32[]{:S(2)}, u32[]{:S(2)}) collective-permute-start(bf16[128,128]{1,0:T(8,128)(2,1)S(1)} %get-tuple-element.24), channel_id=1, source_target_pairs={{1,0},{2,1},{3,2},{4,3},{5,4},{6,5},{7,6},{0,7},{9,8},{10,9},{11,1... | collective-permute-start | bytes 98312 | tf_op jit(solution)/shard_map/ppermute | solution.py:543
  16.5 1.6 %collective-permute-done.left_ref = bf16[128,128]{1,0:T(8,128)(2,1)S(1)} collective-permute-done((bf16[128,128]{1,0:T(8,128)(2,1)S(1)}, bf16[128,128]{1,0:T(8,128)(2,1)S(1)}, u32[]{:S(2)}, u32[]{:S(2)}) %collective-permute-start) | collective-permute-done | bytes 32800 | tf_op jit(solution)/shard_map/ppermute | solution.py:542
  18.1 1.6 %collective-permute-start.3 = (bf16[18,64,128]{2,1,0:T(8,128)(2,1)S(1)}, bf16[18,64,128]{2,1,0:T(8,128)(2,1)S(1)}, u32[]{:S(2)}, u32[]{:S(2)}) collective-permute-start(bf16[18,64,128]{2,1,0:T(8,128)(2,1)S(1)} %get-tuple-element.61), channel_id=1, source_target_pairs={{0,16},{8,24},{16,0},{24,8},{1,17},{9,25},{17,1},{25,9},{2,18},{10... | collective-permute-start | bytes 884744 | tf_op jit(solution)/shard_map/ppermute | solution.py:503
  19.7 1.7 %collective-permute-start.4 = (bf16[18,64,128]{2,1,0:T(8,128)(2,1)S(1)}, bf16[18,64,128]{2,1,0:T(8,128)(2,1)S(1)}, u32[]{:S(2)}, u32[]{:S(2)}) collective-permute-start(bf16[18,64,128]{2,1,0:T(8,128)(2,1)S(1)} %get-tuple-element.61), channel_id=1, source_target_pairs={{0,24},{8,0},{16,8},{24,16},{1,25},{9,1},{17,9},{25,17},{2,26},{10... | collective-permute-start | bytes 884744 | tf_op jit(solution)/shard_map/ppermute | solution.py:503
  21.7 9.4 %forward.1 = (bf16[2048,1152]{1,0:T(8,128)(2,1)S(1)}, f32[2048,128]{1,0:T(8,128)S(1)}, bf16[2048,128]{1,0:T(8,128)(2,1)S(1)}, bf16[8,2,64,256]{3,2,1,0:T(8,128)(2,1)S(1)}) custom-call(s32[2048]{0:T(1024)S(1)} %fusion.36.base_ref, s32[8]{0:T(128)S(1)} %bitcast.116, bf16[64,256,128]{2,1,0:T(8,128)(2,1)} %bitcast.119, ...), custom_call_target="tpu_custom_call" | custom-call | flops 603979776 | bytes 25165824 | tf_op jit(solution)/shard_map/forward/pallas_call | solution.py:186
  31.3 6.4 %pick.1 = (bf16[2048,768]{1,0:T(8,128)(2,1)S(1)}, bf16[8,2,64,256]{3,2,1,0:T(8,128)(2,1)S(1)}) custom-call(s32[2048]{0:T(1024)S(1)} %bitcast.115, s32[4]{0:T(128)S(1)} %and_select_fusion.order_ref, bf16[4,18,64,128]{3,2,1,0:T(8,128)(2,1)S(1)} %pad_maximum_fusion.cot_ref, bf16[64,768]{1,0:T(8,128)(2,1)S(1)} %reshape.99.wg_ref, ...), custom_call_target="tpu_custom_call", output_to_operand_aliasing={{1}: (4, {})} | custom-call | flops 201326592 | bytes 12582912 | tf_op jit(solution)/shard_map/pick/pallas_call | solution.py:272
  37.8 20.7 %all_to_all.24.back_ref.sent_ref = bf16[8,2,64,256]{3,2,1,0:T(8,128)(2,1)S(1)} all-to-all(bf16[8,2,64,256]{3,2,1,0:T(8,128)(2,1)S(1)} %get-tuple-element.33), channel_id=1, replica_groups=mesh['pair'=2,'core'=2,'sector'=8] {'sector'}, dimensions={0} | all-to-all | bytes 1048576 | tf_op jit(solution)/shard_map/all_to_all | solution.py:571
  58.6 1.6 %collective-permute-start.5 = (bf16[1,8,72,256]{3,2,1,0:T(8,128)(2,1)S(1)}, bf16[1,8,72,256]{3,2,1,0:T(8,128)(2,1)S(1)}, u32[]{:S(2)}, u32[]{:S(2)}) collective-permute-start(bf16[1,8,72,256]{3,2,1,0:T(8,128)(2,1)S(1)} %get-tuple-element.59), channel_id=1, source_target_pairs={{0,16},{8,24},{16,0},{24,8},{1,17},{9,25},{17,1},{25,9},{2,18},{10... | collective-permute-start | bytes 884744 | tf_op jit(solution)/shard_map/ppermute | solution.py:491
  60.2 3.3 %backward.1 = bf16[1536,128]{1,0:T(8,128)(2,1)} custom-call(s32[8]{0:T(128)S(1)} %bitcast.117, bf16[8,2,64,256]{3,2,1,0:T(8,128)(2,1)S(1)} %all_to_all.24.back_ref.sent_ref, bf16[8,2,64,256]{3,2,1,0:T(8,128)(2,1)S(1)} %all_to_all.24.back_ref.sent_ref, f32[2048,128]{1,0:T(8,128)S(1)} %get-tuple-element.35.slope_ref, ...), custom_call_target="tpu_custom_call" | custom-call | flops 603979776 | bytes 10485760 | tf_op jit(solution)/shard_map/backward/pallas_call | solution.py:361
  63.5 2.7 %all-to-all-start.2 = ((bf16[32,48,128]{2,1,0:T(8,128)(2,1)}), bf16[32,48,128]{2,1,0:T(8,128)(2,1)S(1)}, u32[]{:S(2)}, u32[]{:S(2)}) async-start(bf16[32,48,128]{2,1,0:T(8,128)(2,1)} %bitcast.50), calls=%async_computation.2 | async-start | bytes 786432 | tf_op jit(solution)/shard_map/all_to_all | solution.py:511
  66.2 1.3 %collective-permute-done.5 = bf16[1,8,72,256]{3,2,1,0:T(8,128)(2,1)S(1)} collective-permute-done((bf16[1,8,72,256]{3,2,1,0:T(8,128)(2,1)S(1)}, bf16[1,8,72,256]{3,2,1,0:T(8,128)(2,1)S(1)}, u32[]{:S(2)}, u32[]{:S(2)}) %collective-permute-start.5) | collective-permute-done | bytes 294944 | tf_op jit(solution)/shard_map/ppermute | solution.py:491
  67.6 12.0 %all-to-all-done.2 = bf16[32,48,128]{2,1,0:T(8,128)(2,1)S(1)} async-done(((bf16[32,48,128]{2,1,0:T(8,128)(2,1)}), bf16[32,48,128]{2,1,0:T(8,128)(2,1)S(1)}, u32[]{:S(2)}, u32[]{:S(2)}) %all-to-all-start.2) | async-done | bytes 393248 | tf_op jit(solution)/shard_map/all_to_all | solution.py:511
  79.7 0.7 broadcast_in_dim.23
  80.4 3.5 %all-to-all-start.3 = ((bf16[16,48,128]{2,1,0:T(8,128)(2,1)}), bf16[16,48,128]{2,1,0:T(8,128)(2,1)S(1)}, u32[]{:S(2)}, u32[]{:S(2)}) async-start(bf16[16,48,128]{2,1,0:T(8,128)(2,1)} %broadcast_in_dim.23), calls=%async_computation.3 | async-start | bytes 393216 | tf_op jit(solution)/shard_map/all_to_all | solution.py:515
  84.5 4.5 %place.1 = bf16[10,64,256]{2,1,0:T(8,128)(2,1)S(1)} custom-call(s32[64]{0:T(128)S(1)} %sub.58.tile_ref, bf16[32,72,256]{2,1,0:T(8,128)(2,1)S(1)} %bitcast.111), custom_call_target="tpu_custom_call" | custom-call | flops 268435456 | bytes 2097152 | tf_op jit(solution)/shard_map/place/pallas_call | solution.py:466
  89.9 3.3 %collective-permute-start.7 = (bf16[64,1,130]{0,2,1:T(8,128)(2,1)S(1)}, bf16[64,1,130]{0,2,1:T(8,128)(2,1)S(1)}, u32[]{:S(2)}, u32[]{:S(2)}) collective-permute-start(bf16[64,1,130]{0,2,1:T(8,128)(2,1)S(1)} %get-tuple-element.42), channel_id=1, source_target_pairs={{0,1},{1,2},{2,3},{3,4},{4,5},{5,6},{6,7},{8,9},{9,10},{10,11},{11... | collective-permute-start | bytes 49928 | tf_op jit(solution)/shard_map/ppermute | solution.py:591
  93.2 1.3 %collective-permute-start.8 = (bf16[64,1,130]{0,2,1:T(8,128)(2,1)S(1)}, bf16[64,1,130]{0,2,1:T(8,128)(2,1)S(1)}, u32[]{:S(2)}, u32[]{:S(2)}) collective-permute-start(bf16[64,1,130]{0,2,1:T(8,128)(2,1)S(1)} %get-tuple-element.43), channel_id=1, source_target_pairs={{1,0},{2,1},{3,2},{4,3},{5,4},{6,5},{7,6},{9,8},{10,9},{11,10},{12... | collective-permute-start | bytes 49928 | tf_op jit(solution)/shard_map/ppermute | solution.py:592
  95.7 3.3 %collective-permute-done.8 = bf16[64,1,130]{0,2,1:T(8,128)(2,1)S(1)} collective-permute-done((bf16[64,1,130]{0,2,1:T(8,128)(2,1)S(1)}, bf16[64,1,130]{0,2,1:T(8,128)(2,1)S(1)}, u32[]{:S(2)}, u32[]{:S(2)}) %collective-permute-start.8) | collective-permute-done | bytes 16672 | tf_op jit(solution)/shard_map/ppermute | solution.py:592
  101.7 0.7 copy.37
  102.4 1.0 unpack.1
  (69 shorter events, 7.0 us)
Async XLA Ops:
  2.8 18.9 %all-to-all-start = ((s32[8,1,256]{2,1,0:T(1,128)}), s32[8,1,256]{2,1,0:T(1,128)S(1)}, u32[]{:S(2)}, u32[]{:S(2)}) async-start(s32[8,1,256]{2,1,0:T(1,128)} %reshape_add_fusion), calls=%async_computation | async-start | bytes 16384 | tf_op jit(solution)/shard_map/all_to_all | solution.py:545
  10.1 6.2 %copy-start.4 = (s32[1,1,8,256]{3,2,1,0:T(8,128)S(1)}, s32[1,1,8,256]{3,2,1,0:T(8,128)}, u32[]{:S(2)}) copy-start(s32[1,1,8,256]{3,2,1,0:T(8,128)} %param.10) | copy-start | bytes 24580
  10.1 6.2 %copy-start.3 = (bf16[3,3,64,64]{3,2,1,0:T(8,128)(2,1)S(1)}, bf16[3,3,64,64]{3,2,1,0:T(8,128)(2,1)}, u32[]{:S(2)}) copy-start(bf16[3,3,64,64]{3,2,1,0:T(8,128)(2,1)} %param.16) | copy-start | bytes 221188
  11.4 6.7 %collective-permute-start = (bf16[128,128]{1,0:T(8,128)(2,1)S(1)}, bf16[128,128]{1,0:T(8,128)(2,1)S(1)}, u32[]{:S(2)}, u32[]{:S(2)}) collective-permute-start(bf16[128,128]{1,0:T(8,128)(2,1)S(1)} %get-tuple-element.23), channel_id=1, source_target_pairs={{0,1},{1,2},{2,3},{3,4},{4,5},{5,6},{6,7},{7,0},{8,9},{9,10},{10,1... | collective-permute-start | bytes 98312 | tf_op jit(solution)/shard_map/ppermute | solution.py:542
  13.5 4.6 %collective-permute-start.1 = (bf16[128,128]{1,0:T(8,128)(2,1)S(1)}, bf16[128,128]{1,0:T(8,128)(2,1)S(1)}, u32[]{:S(2)}, u32[]{:S(2)}) collective-permute-start(bf16[128,128]{1,0:T(8,128)(2,1)S(1)} %get-tuple-element.24), channel_id=1, source_target_pairs={{1,0},{2,1},{3,2},{4,3},{5,4},{6,5},{7,6},{0,7},{9,8},{10,9},{11,1... | collective-permute-start | bytes 98312 | tf_op jit(solution)/shard_map/ppermute | solution.py:543
  16.3 5.4 %copy-start = (bf16[3,3,128,128]{3,2,1,0:T(8,128)(2,1)S(1)}, bf16[3,3,128,128]{3,2,1,0:T(8,128)(2,1)}, u32[]{:S(2)}) copy-start(bf16[3,3,128,128]{3,2,1,0:T(8,128)(2,1)} %param.14) | copy-start | bytes 884740
  16.3 5.4 %copy-start.1 = (bf16[128,64]{0,1:T(8,128)(2,1)S(1)}, bf16[128,64]{0,1:T(8,128)(2,1)}, u32[]{:S(2)}) copy-start(bf16[128,64]{0,1:T(8,128)(2,1)} %param.15) | copy-start | bytes 49156
  16.3 5.4 %copy-start.2 = (s32[1,1,8]{2,1,0:T(1,128)S(1)}, s32[1,1,8]{2,1,0:T(1,128)}, u32[]{:S(2)}) copy-start(s32[1,1,8]{2,1,0:T(1,128)} %param.13) | copy-start | bytes 100
  18.1 13.0 %collective-permute-start.3 = (bf16[18,64,128]{2,1,0:T(8,128)(2,1)S(1)}, bf16[18,64,128]{2,1,0:T(8,128)(2,1)S(1)}, u32[]{:S(2)}, u32[]{:S(2)}) collective-permute-start(bf16[18,64,128]{2,1,0:T(8,128)(2,1)S(1)} %get-tuple-element.61), channel_id=1, source_target_pairs={{0,16},{8,24},{16,0},{24,8},{1,17},{9,25},{17,1},{25,9},{2,18},{10... | collective-permute-start | bytes 884744 | tf_op jit(solution)/shard_map/ppermute | solution.py:503
  19.7 11.4 %collective-permute-start.2 = (bf16[18,64,128]{2,1,0:T(8,128)(2,1)S(1)}, bf16[18,64,128]{2,1,0:T(8,128)(2,1)S(1)}, u32[]{:S(2)}, u32[]{:S(2)}) collective-permute-start(bf16[18,64,128]{2,1,0:T(8,128)(2,1)S(1)} %get-tuple-element.61), channel_id=1, source_target_pairs={{0,8},{8,16},{16,24},{24,0},{1,9},{9,17},{17,25},{25,1},{2,10},{10... | collective-permute-start | bytes 884744 | tf_op jit(solution)/shard_map/ppermute | solution.py:503
  19.7 11.4 %collective-permute-start.4 = (bf16[18,64,128]{2,1,0:T(8,128)(2,1)S(1)}, bf16[18,64,128]{2,1,0:T(8,128)(2,1)S(1)}, u32[]{:S(2)}, u32[]{:S(2)}) collective-permute-start(bf16[18,64,128]{2,1,0:T(8,128)(2,1)S(1)} %get-tuple-element.61), channel_id=1, source_target_pairs={{0,24},{8,0},{16,8},{24,16},{1,25},{9,1},{17,9},{25,17},{2,26},{10... | collective-permute-start | bytes 884744 | tf_op jit(solution)/shard_map/ppermute | solution.py:503
  58.6 8.9 %collective-permute-start.5 = (bf16[1,8,72,256]{3,2,1,0:T(8,128)(2,1)S(1)}, bf16[1,8,72,256]{3,2,1,0:T(8,128)(2,1)S(1)}, u32[]{:S(2)}, u32[]{:S(2)}) collective-permute-start(bf16[1,8,72,256]{3,2,1,0:T(8,128)(2,1)S(1)} %get-tuple-element.59), channel_id=1, source_target_pairs={{0,16},{8,24},{16,0},{24,8},{1,17},{9,25},{17,1},{25,9},{2,18},{10... | collective-permute-start | bytes 884744 | tf_op jit(solution)/shard_map/ppermute | solution.py:491
  63.5 16.1 %all-to-all-start.2 = ((bf16[32,48,128]{2,1,0:T(8,128)(2,1)}), bf16[32,48,128]{2,1,0:T(8,128)(2,1)S(1)}, u32[]{:S(2)}, u32[]{:S(2)}) async-start(bf16[32,48,128]{2,1,0:T(8,128)(2,1)} %bitcast.50), calls=%async_computation.2 | async-start | bytes 786432 | tf_op jit(solution)/shard_map/all_to_all | solution.py:511
  67.5 16.4 %collective-permute-start.6 = (bf16[2,8,72,256]{3,2,1,0:T(8,128)(2,1)S(1)}, bf16[2,8,72,256]{3,2,1,0:T(8,128)(2,1)S(1)}, u32[]{:S(2)}, u32[]{:S(2)}) collective-permute-start(bf16[2,8,72,256]{3,2,1,0:T(8,128)(2,1)S(1)} %get-tuple-element.54), channel_id=1, source_target_pairs={{0,8},{8,0},{16,24},{24,16},{1,9},{9,1},{17,25},{25,17},{2,10},{10... | collective-permute-start | bytes 1769480 | tf_op jit(solution)/shard_map/ppermute | solution.py:491
  80.4 20.5 %all-to-all-start.3 = ((bf16[16,48,128]{2,1,0:T(8,128)(2,1)}), bf16[16,48,128]{2,1,0:T(8,128)(2,1)S(1)}, u32[]{:S(2)}, u32[]{:S(2)}) async-start(bf16[16,48,128]{2,1,0:T(8,128)(2,1)} %broadcast_in_dim.23), calls=%async_computation.3 | async-start | bytes 393216 | tf_op jit(solution)/shard_map/all_to_all | solution.py:515
  89.9 5.7 %collective-permute-start.7 = (bf16[64,1,130]{0,2,1:T(8,128)(2,1)S(1)}, bf16[64,1,130]{0,2,1:T(8,128)(2,1)S(1)}, u32[]{:S(2)}, u32[]{:S(2)}) collective-permute-start(bf16[64,1,130]{0,2,1:T(8,128)(2,1)S(1)} %get-tuple-element.42), channel_id=1, source_target_pairs={{0,1},{1,2},{2,3},{3,4},{4,5},{5,6},{6,7},{8,9},{9,10},{10,11},{11... | collective-permute-start | bytes 49928 | tf_op jit(solution)/shard_map/ppermute | solution.py:591
  93.2 5.8 %collective-permute-start.8 = (bf16[64,1,130]{0,2,1:T(8,128)(2,1)S(1)}, bf16[64,1,130]{0,2,1:T(8,128)(2,1)S(1)}, u32[]{:S(2)}, u32[]{:S(2)}) collective-permute-start(bf16[64,1,130]{0,2,1:T(8,128)(2,1)S(1)} %get-tuple-element.43), channel_id=1, source_target_pairs={{1,0},{2,1},{3,2},{4,3},{5,4},{6,5},{7,6},{9,8},{10,9},{11,10},{12... | collective-permute-start | bytes 49928 | tf_op jit(solution)/shard_map/ppermute | solution.py:592
  100.9 1.5 %collective-permute-start.9 = (bf16[16,48,128]{2,1,0:T(8,128)(2,1)S(1)}, bf16[16,48,128]{2,1,0:T(8,128)(2,1)S(1)}, u32[]{:S(2)}, u32[]{:S(2)}) collective-permute-start(bf16[16,48,128]{2,1,0:T(8,128)(2,1)S(1)} %all-to-all-done.3.refs_0_), channel_id=1, source_target_pairs={{0,8},{8,0},{1,9},{9,1},{2,10},{10,2},{3,11},{11,3},{4,12},{12,4},... | collective-permute-start | bytes 589832 | tf_op jit(solution)/shard_map/ppermute | solution.py:521
